TPU v7x, 256 devices: a whole 4x4x8 slice. The times are simulated.
256 devices in a mesh: tile: 64 (over x, z_hi, y, core), lev: 4 (over z_lo).
Axes of the slice: x: 4, y: 4, z: 8 (z_hi: 2, z_lo: 4; z = z_hi * 4 + z_lo), core: 2. Of those that a mesh axis runs over, the one named last changes fastest.
Arguments:
- control: float32 [80, 32, 16384], P(None, 'lev', 'tile'), may hold values from -6 to 6
- ensemble: bfloat16 [80, 32, 16384], P(None, 'lev', 'tile'), may hold values from -6 to 6
- loc_blocks: bfloat16 [128, 9, 128, 128], P('tile'), may hold values from -0.1875 to 0.1875
- neighbours: int32 [128, 9], P('tile'), may hold values from 0 to 127, as said below
- vert_band: float32 [32, 9], replicated, may hold values from 0.1 to 0.6
- channel_weights: float32 [16, 32], P(None, 'lev'), may hold values from -1 to 1
- innovation: float32 [16, 16384], P(None, 'tile'), may hold values from -6 to 6
- inv_error: float32 [16, 16384], P(None, 'tile'), may hold values from 0.25 to 4
Outputs:
- grad_first: float32 [80, 32, 16384], P(None, 'lev', 'tile')
- grad_second: float32 [80, 32, 16384], P(None, 'lev', 'tile')
- costs: float32 [2], replicated
Inputs may be any that keep to these rules, and one draw needn't show every extreme that they name: neighbours[b,0] = b; neighbours[b,1] lies in tile b // 2 - 1 and neighbours[b,2] in tile b // 2 + 1, tiles counted cyclically modulo 64; every other entry lies in one of these three tiles; block n belongs to tile n // 2.
All inputs are finite; a program needn't handle non-finite values.
Results may differ from a plain program's by a relative error of at most 0.005.
Values may be sent and summed in bfloat16 or wider, within the bound.
No kernel may reach another device: no remote copies, remote signals or barrier semaphores. Data moves between devices by JAX's collectives and lax.ppermute only.
A program may use at most 64 MiB of HBM per device.

v0:
```python
import math

import jax
import jax.numpy as jnp
from jax import lax
from jax.sharding import PartitionSpec as P

HV = 4


step_length = 0.5


def with_halo(value, sides, width, wrap):
    for axis, dim in sides:
        peers, length = (lax.axis_size(axis), value.shape[dim])
        up = [(i, (i + 1) % peers) for i in range(peers if wrap else peers - 1)]
        down = [(j, i) for i, j in up]
        last = lax.slice_in_dim(value, length - width, length, axis=dim)
        first = lax.slice_in_dim(value, 0, width, axis=dim)
        before = lax.ppermute(last, axis, up)
        after = lax.ppermute(first, axis, down)
        value = jnp.concatenate([before, value, after], axis=dim)
    return value


def passed_along(value, axis, by):
    peers = lax.axis_size(axis)
    return lax.ppermute(value, axis, [(i, (i + by) % peers) for i in range(peers)])


def per_device(
    control, ensemble, loc_blocks, neighbours, vert_band, channel_weights, innovation, inv_error
):
    members, ldev, pdev = control.shape
    bpd = loc_blocks.shape[0]
    nbrs = loc_blocks.shape[1]
    ntile = lax.axis_size("tile")
    nlev = lax.axis_size("lev")
    tile_pos = lax.axis_index("tile")
    lev_pos = lax.axis_index("lev")
    norm_factor = 1.0 / math.sqrt(members - 1)
    offsets = jnp.mod(neighbours // bpd - tile_pos + 1, ntile)
    slots = (offsets * bpd + neighbours % bpd).reshape(-1)
    band_padded = jnp.pad(vert_band, ((HV, HV), (0, 0)))
    band_ext = lax.dynamic_slice_in_dim(band_padded, lev_pos * ldev, ldev + 2 * HV, 0)
    band_own = band_ext[HV : HV + ldev]
    ens_float = ensemble.astype(jnp.float32)

    def evaluate(field):
        extended = with_halo(field, (("lev", 1),), HV, False)
        smooth = jnp.zeros_like(field)
        for s in range(2 * HV + 1):
            smooth = smooth + band_own[:, s][None, :, None] * extended[:, s : s + ldev, :]
        smooth_half = smooth.astype(jnp.bfloat16)
        widened = with_halo(smooth_half, (("tile", 2),), pdev, True)
        picked = jnp.take(widened.reshape(members, ldev, 3 * bpd, 128), slots, axis=2)
        picked = picked.reshape(members, ldev, bpd, nbrs, 128)
        local_u = jnp.einsum(
            "mlbjc,bjic->mlbi", picked, loc_blocks, preferred_element_type=jnp.float32
        )
        local_u = local_u.reshape(members, ldev, pdev)
        incr = jnp.sum(ens_float * local_u, axis=0) * norm_factor
        partial_obs = jnp.einsum(
            "kl,lp->kp", channel_weights, incr, precision=lax.Precision.HIGHEST
        )
        evolved = lax.psum(partial_obs, "lev")
        misfit = evolved - innovation
        weighted = inv_error * misfit
        obs_term = jnp.where(lev_pos == 0, 0.5 * jnp.sum(weighted * misfit), 0.0)
        back_term = 0.5 * jnp.sum(field * field)
        incr_adj = jnp.einsum(
            "kl,kp->lp", channel_weights, weighted, precision=lax.Precision.HIGHEST
        )
        cotangent = (ens_float * incr_adj[None] * norm_factor).astype(jnp.bfloat16)
        terms = jnp.einsum(
            "mlbi,bjic->mlbjc",
            cotangent.reshape(members, ldev, bpd, 128),
            loc_blocks,
            preferred_element_type=jnp.float32,
        )
        spread = (
            jnp.zeros((members, ldev, 3 * bpd, 128), jnp.float32)
            .at[:, :, slots, :]
            .add(terms.reshape(members, ldev, bpd * nbrs, 128))
        )
        spread = spread.reshape(members, ldev, 3, pdev)
        adjoint = spread[:, :, 1] + passed_along(spread[:, :, 0], "tile", -1)
        adjoint = adjoint + passed_along(spread[:, :, 2], "tile", 1)
        adj_ext = with_halo(adjoint, (("lev", 1),), HV, False)
        gradient = field
        for s in range(2 * HV + 1):
            lower = 2 * HV - s
            gradient = (
                gradient
                + band_ext[lower : lower + ldev, s][None, :, None]
                * adj_ext[:, lower : lower + ldev, :]
            )
        return (gradient, back_term, obs_term)

    count = float(members * ldev * pdev * nlev * ntile)
    grad_first, back_first, obs_first = evaluate(control)
    back_first, obs_first, squares = lax.psum(
        (back_first, obs_first, jnp.sum(grad_first * grad_first)), ("tile", "lev")
    )
    tau = step_length / jnp.sqrt(squares / count + 1e-06)
    grad_second, back_second, obs_second = evaluate(control - tau * grad_first)
    back_second, obs_second = lax.psum((back_second, obs_second), ("tile", "lev"))
    costs = jnp.stack([back_first + obs_first, back_second + obs_second]) / count
    return (grad_first, grad_second, costs)


def solution(mesh):
    placed = (
        P(None, "lev", "tile"),
        P(None, "lev", "tile"),
        P("tile", None, None, None),
        P("tile", None),
        P(),
        P(None, "lev"),
        P(None, "tile"),
        P(None, "tile"),
    )
    return jax.shard_map(
        per_device,
        mesh=mesh,
        in_specs=placed,
        out_specs=(P(None, "lev", "tile"), P(None, "lev", "tile"), P()),
        check_vma=False,
    )
```

profile of v0, /device:TPU:2, one launch (start us, length us, event | category | flops | bytes accessed | tf_op | source)
XLA Modules:
  0.0 408.0 jit_solution(17185516404099371895)
XLA Ops:
  3.5 4.6 %collective-permute-start = (f32[80,4,256]{2,1,0:T(4,128)S(1)}, f32[80,4,256]{2,1,0:T(4,128)S(1)}, u32[]{:S(2)}, u32[]{:S(2)}) collective-permute-start(f32[80,4,256]{2,1,0:T(4,128)S(1)} %get-tuple-element.27), channel_id=1, source_target_pairs={{0,1},{1,2},{2,3},{4,5},{5,6},{6,7},{8,9},{9,10},{10,11},{12,13},{... | collective-permute-start | bytes 983048 | tf_op jit(solution)/shard_map/ppermute | solution.py:21
  15.9 8.6 %collective-permute-start.3 = (bf16[80,8,256]{2,1,0:T(8,128)(2,1)S(1)}, bf16[80,8,256]{2,1,0:T(8,128)(2,1)S(1)}, u32[]{:S(2)}, u32[]{:S(2)}) collective-permute-start(bf16[80,8,256]{2,1,0:T(8,128)(2,1)S(1)} %fusion.78), channel_id=1, source_target_pairs={{4,0},{8,4},{12,8},{16,12},{20,16},{24,20},{28,24},{32,28},{36,32}... | collective-permute-start | bytes 983048 | tf_op jit(solution)/shard_map/ppermute | solution.py:22
  25.1 4.3 %collective-permute-done.2 = bf16[80,8,256]{2,1,0:T(8,128)(2,1)S(1)} collective-permute-done((bf16[80,8,256]{2,1,0:T(8,128)(2,1)S(1)}, bf16[80,8,256]{2,1,0:T(8,128)(2,1)S(1)}, u32[]{:S(2)}, u32[]{:S(2)}) %collective-permute-start.2) | collective-permute-done | bytes 327712 | tf_op jit(solution)/shard_map/ppermute | solution.py:21
  36.1 23.8 %psum.49 = f32[16,256]{1,0:T(8,128)S(1)} all-reduce(f32[16,256]{1,0:T(8,128)S(1)} %convolution_bitcast_fusion.5), channel_id=1, replica_groups=mesh['tile'=64,'lev'=4] {'lev'}, use_global_device_ids=true, to_apply=%region_1.3 | all-reduce | flops 4096 | bytes 32768 | tf_op jit(solution)/shard_map/psum | solution.py:67
  64.8 10.7 %scatter_fusion = f32[80,8,6,128]{3,1,2,0:T(8,128)S(1)} fusion(f32[80,8,6,128]{3,1,2,0:T(8,128)S(1)} %broadcast.72.clone, s32[18]{0:T(128)} %fusion.114, f32[18,80,8,128]{3,2,1,0:T(8,128)} %copy.35), kind=kCustom, calls=%fused_computation.2 | custom fusion | flops 1474560 | bytes 17694792 | tf_op jit(solution)/shard_map/scatter-add | solution.py:85
  77.5 4.4 %reshape.107 = f32[80,8,3,256]{3,2,1,0:T(4,128)} reshape(f32[80,8,6,128]{3,2,1,0:T(8,128)} %copy.36) | data formatting | bytes 3932160 | tf_op jit(solution)/shard_map/reshape | solution.py:87
  81.9 5.5 %fusion.119 = (f32[80,8,1,256]{3,2,1,0:T(1,128)S(1)}, f32[80,8,1,256]{3,2,1,0:T(1,128)S(1)}, f32[80,8,1,256]{3,2,1,0:T(1,128)S(1)}) fusion(f32[80,8,3,256]{3,2,1,0:T(4,128)} %reshape.107), kind=kLoop, calls=%fused_computation.235 | loop fusion | bytes 3932160 | tf_op jit(solution)/shard_map/slice | solution.py:88
  87.5 5.0 %collective-permute-start.4 = (f32[80,8,256]{2,1,0:T(8,128)S(1)}, f32[80,8,256]{2,1,0:T(8,128)S(1)}, u32[]{:S(2)}, u32[]{:S(2)}) collective-permute-start(f32[80,8,256]{2,1,0:T(8,128)S(1)} %bitcast.144), channel_id=1, source_target_pairs={{0,252},{4,0},{8,4},{12,8},{16,12},{20,16},{24,20},{28,24},{32,28}... | collective-permute-start | bytes 1966088 | tf_op jit(solution)/shard_map/ppermute | solution.py:29
  92.6 17.9 %collective-permute-done.4 = f32[80,8,256]{2,1,0:T(8,128)S(1)} collective-permute-done((f32[80,8,256]{2,1,0:T(8,128)S(1)}, f32[80,8,256]{2,1,0:T(8,128)S(1)}, u32[]{:S(2)}, u32[]{:S(2)}) %collective-permute-start.4) | collective-permute-done | bytes 655392 | tf_op jit(solution)/shard_map/ppermute | solution.py:29
  110.5 8.7 %collective-permute-done.5 = f32[80,8,256]{2,1,0:T(8,128)S(1)} collective-permute-done((f32[80,8,256]{2,1,0:T(8,128)S(1)}, f32[80,8,256]{2,1,0:T(8,128)S(1)}, u32[]{:S(2)}, u32[]{:S(2)}) %collective-permute-start.5) | collective-permute-done | bytes 655392 | tf_op jit(solution)/shard_map/ppermute | solution.py:29
  120.7 4.6 %collective-permute-start.7 = (f32[80,4,256]{2,1,0:T(4,128)S(1)}, f32[80,4,256]{2,1,0:T(4,128)S(1)}, u32[]{:S(2)}, u32[]{:S(2)}) collective-permute-start(f32[80,4,256]{2,1,0:T(4,128)S(1)} %get-tuple-element.25), channel_id=1, source_target_pairs={{0,1},{1,2},{2,3},{4,5},{5,6},{6,7},{8,9},{9,10},{10,11},{12,13},{... | collective-permute-start | bytes 983048 | tf_op jit(solution)/shard_map/ppermute | solution.py:21
  132.5 74.9 %psum.50 = f32[]{:T(128)} all-reduce(f32[]{:T(128)} %get-tuple-element.10), channel_id=1, replica_groups=mesh['tile'=64,'lev'=4] {'tile','lev'}, use_global_device_ids=true, to_apply=%region_4.6 | all-reduce | flops 1 | bytes 8 | tf_op jit(solution)/shard_map/psum | solution.py:103
  213.2 5.4 %collective-permute-done.8 = f32[80,4,256]{2,1,0:T(4,128)S(1)} collective-permute-done((f32[80,4,256]{2,1,0:T(4,128)S(1)}, f32[80,4,256]{2,1,0:T(4,128)S(1)}, u32[]{:S(2)}, u32[]{:S(2)}) %collective-permute-start.8) | collective-permute-done | bytes 327712 | tf_op jit(solution)/shard_map/ppermute | solution.py:21
  224.2 8.6 %collective-permute-start.11 = (bf16[80,8,256]{2,1,0:T(8,128)(2,1)S(1)}, bf16[80,8,256]{2,1,0:T(8,128)(2,1)S(1)}, u32[]{:S(2)}, u32[]{:S(2)}) collective-permute-start(bf16[80,8,256]{2,1,0:T(8,128)(2,1)S(1)} %fusion.31), channel_id=1, source_target_pairs={{4,0},{8,4},{12,8},{16,12},{20,16},{24,20},{28,24},{32,28},{36,32}... | collective-permute-start | bytes 983048 | tf_op jit(solution)/shard_map/ppermute | solution.py:22
  232.8 8.2 %collective-permute-done.10 = bf16[80,8,256]{2,1,0:T(8,128)(2,1)S(1)} collective-permute-done((bf16[80,8,256]{2,1,0:T(8,128)(2,1)S(1)}, bf16[80,8,256]{2,1,0:T(8,128)(2,1)S(1)}, u32[]{:S(2)}, u32[]{:S(2)}) %collective-permute-start.10) | collective-permute-done | bytes 327712 | tf_op jit(solution)/shard_map/ppermute | solution.py:21
  247.8 15.5 %psum.51 = f32[16,256]{1,0:T(8,128)S(1)} all-reduce(f32[16,256]{1,0:T(8,128)S(1)} %convolution_bitcast_fusion.4), channel_id=1, replica_groups=mesh['tile'=64,'lev'=4] {'lev'}, use_global_device_ids=true, to_apply=%region_6.8 | all-reduce | flops 4096 | bytes 32768 | tf_op jit(solution)/shard_map/psum | solution.py:67
  268.2 10.5 %scatter_fusion.1 = f32[80,8,6,128]{3,1,2,0:T(8,128)S(1)} fusion(f32[80,8,6,128]{3,1,2,0:T(8,128)S(1)} %broadcast.72, s32[18]{0:T(128)S(1)} %copy-done.45, f32[18,80,8,128]{3,2,1,0:T(8,128)} %copy.44), kind=kCustom, calls=%fused_computation.3 | custom fusion | flops 1474560 | bytes 17694792 | tf_op jit(solution)/shard_map/scatter-add | solution.py:85
  280.7 4.4 %reshape.113 = f32[80,8,3,256]{3,2,1,0:T(4,128)} reshape(f32[80,8,6,128]{3,2,1,0:T(8,128)} %copy.45) | data formatting | bytes 3932160 | tf_op jit(solution)/shard_map/reshape | solution.py:87
  285.1 5.5 %fusion.118 = (f32[80,8,1,256]{3,2,1,0:T(1,128)S(1)}, f32[80,8,1,256]{3,2,1,0:T(1,128)S(1)}, f32[80,8,1,256]{3,2,1,0:T(1,128)S(1)}) fusion(f32[80,8,3,256]{3,2,1,0:T(4,128)} %reshape.113), kind=kLoop, calls=%fused_computation.234 | loop fusion | bytes 3932160 | tf_op jit(solution)/shard_map/slice | solution.py:88
  290.7 5.5 %collective-permute-start.12 = (f32[80,8,256]{2,1,0:T(8,128)S(1)}, f32[80,8,256]{2,1,0:T(8,128)S(1)}, u32[]{:S(2)}, u32[]{:S(2)}) collective-permute-start(f32[80,8,256]{2,1,0:T(8,128)S(1)} %bitcast.145), channel_id=1, source_target_pairs={{0,252},{4,0},{8,4},{12,8},{16,12},{20,16},{24,20},{28,24},{32,28}... | collective-permute-start | bytes 1966088 | tf_op jit(solution)/shard_map/ppermute | solution.py:29
  296.5 15.4 %collective-permute-done.12 = f32[80,8,256]{2,1,0:T(8,128)S(1)} collective-permute-done((f32[80,8,256]{2,1,0:T(8,128)S(1)}, f32[80,8,256]{2,1,0:T(8,128)S(1)}, u32[]{:S(2)}, u32[]{:S(2)}) %collective-permute-start.12) | collective-permute-done | bytes 655392 | tf_op jit(solution)/shard_map/ppermute | solution.py:29
  311.9 9.9 %collective-permute-done.13 = f32[80,8,256]{2,1,0:T(8,128)S(1)} collective-permute-done((f32[80,8,256]{2,1,0:T(8,128)S(1)}, f32[80,8,256]{2,1,0:T(8,128)S(1)}, u32[]{:S(2)}, u32[]{:S(2)}) %collective-permute-start.13) | collective-permute-done | bytes 655392 | tf_op jit(solution)/shard_map/ppermute | solution.py:29
  323.4 4.6 %collective-permute-start.15 = (f32[80,4,256]{2,1,0:T(4,128)S(1)}, f32[80,4,256]{2,1,0:T(4,128)S(1)}, u32[]{:S(2)}, u32[]{:S(2)}) collective-permute-start(f32[80,4,256]{2,1,0:T(4,128)S(1)} %get-tuple-element.21), channel_id=1, source_target_pairs={{0,1},{1,2},{2,3},{4,5},{5,6},{6,7},{8,9},{9,10},{10,11},{12,13},{... | collective-permute-start | bytes 983048 | tf_op jit(solution)/shard_map/ppermute | solution.py:21
  331.1 72.8 %all-reduce.1 = (f32[]{:T(128)}, f32[]{:T(128)}) all-reduce(f32[]{:T(128)S(6)} %add.223, f32[]{:T(128)S(6)} %add.222), channel_id=1, replica_groups=mesh['tile'=64,'lev'=4] {'tile','lev'}, use_global_device_ids=true, to_apply=%region_13.15 | all-reduce | flops 2 | bytes 16 | tf_op jit(solution)/shard_map/psum | solution.py:108
  (169 shorter events, 63.8 us)
Async XLA Ops:
  2.2 11.6 %collective-permute-start.1 = (f32[80,4,256]{2,1,0:T(4,128)S(1)}, f32[80,4,256]{2,1,0:T(4,128)}, u32[]{:S(2)}, u32[]{:S(2)}) collective-permute-start(f32[80,4,256]{2,1,0:T(4,128)S(1)} %get-tuple-element.26), channel_id=1, source_target_pairs={{1,0},{2,1},{3,2},{5,4},{6,5},{7,6},{9,8},{10,9},{11,10},{13,12},{... | collective-permute-start | bytes 983048 | tf_op jit(solution)/shard_map/ppermute | solution.py:22
  3.5 11.4 %collective-permute-start = (f32[80,4,256]{2,1,0:T(4,128)S(1)}, f32[80,4,256]{2,1,0:T(4,128)S(1)}, u32[]{:S(2)}, u32[]{:S(2)}) collective-permute-start(f32[80,4,256]{2,1,0:T(4,128)S(1)} %get-tuple-element.27), channel_id=1, source_target_pairs={{0,1},{1,2},{2,3},{4,5},{5,6},{6,7},{8,9},{9,10},{10,11},{12,13},{... | collective-permute-start | bytes 983048 | tf_op jit(solution)/shard_map/ppermute | solution.py:21
  15.8 13.6 %collective-permute-start.2 = (bf16[80,8,256]{2,1,0:T(8,128)(2,1)S(1)}, bf16[80,8,256]{2,1,0:T(8,128)(2,1)S(1)}, u32[]{:S(2)}, u32[]{:S(2)}) collective-permute-start(bf16[80,8,256]{2,1,0:T(8,128)(2,1)S(1)} %fusion.78), channel_id=1, source_target_pairs={{0,4},{4,8},{8,12},{12,16},{16,20},{20,24},{24,28},{28,32},{32,36}... | collective-permute-start | bytes 983048 | tf_op jit(solution)/shard_map/ppermute | solution.py:21
  15.9 13.5 %collective-permute-start.3 = (bf16[80,8,256]{2,1,0:T(8,128)(2,1)S(1)}, bf16[80,8,256]{2,1,0:T(8,128)(2,1)S(1)}, u32[]{:S(2)}, u32[]{:S(2)}) collective-permute-start(bf16[80,8,256]{2,1,0:T(8,128)(2,1)S(1)} %fusion.78), channel_id=1, source_target_pairs={{4,0},{8,4},{12,8},{16,12},{20,16},{24,20},{28,24},{32,28},{36,32}... | collective-permute-start | bytes 983048 | tf_op jit(solution)/shard_map/ppermute | solution.py:22
  87.5 23.0 %collective-permute-start.4 = (f32[80,8,256]{2,1,0:T(8,128)S(1)}, f32[80,8,256]{2,1,0:T(8,128)S(1)}, u32[]{:S(2)}, u32[]{:S(2)}) collective-permute-start(f32[80,8,256]{2,1,0:T(8,128)S(1)} %bitcast.144), channel_id=1, source_target_pairs={{0,252},{4,0},{8,4},{12,8},{16,12},{20,16},{24,20},{28,24},{32,28}... | collective-permute-start | bytes 1966088 | tf_op jit(solution)/shard_map/ppermute | solution.py:29
  92.5 26.7 %collective-permute-start.5 = (f32[80,8,256]{2,1,0:T(8,128)S(1)}, f32[80,8,256]{2,1,0:T(8,128)S(1)}, u32[]{:S(2)}, u32[]{:S(2)}) collective-permute-start(f32[80,8,256]{2,1,0:T(8,128)S(1)} %bitcast.146), channel_id=1, source_target_pairs={{0,4},{4,8},{8,12},{12,16},{16,20},{20,24},{24,28},{28,32},{32,36}... | collective-permute-start | bytes 1966088 | tf_op jit(solution)/shard_map/ppermute | solution.py:29
  119.4 9.0 %collective-permute-start.6 = (f32[80,4,256]{2,1,0:T(4,128)S(1)}, f32[80,4,256]{2,1,0:T(4,128)S(1)}, u32[]{:S(2)}, u32[]{:S(2)}) collective-permute-start(f32[80,4,256]{2,1,0:T(4,128)S(1)} %get-tuple-element.24), channel_id=1, source_target_pairs={{1,0},{2,1},{3,2},{5,4},{6,5},{7,6},{9,8},{10,9},{11,10},{13,12},{... | collective-permute-start | bytes 983048 | tf_op jit(solution)/shard_map/ppermute | solution.py:22
  120.7 9.1 %collective-permute-start.7 = (f32[80,4,256]{2,1,0:T(4,128)S(1)}, f32[80,4,256]{2,1,0:T(4,128)S(1)}, u32[]{:S(2)}, u32[]{:S(2)}) collective-permute-start(f32[80,4,256]{2,1,0:T(4,128)S(1)} %get-tuple-element.25), channel_id=1, source_target_pairs={{0,1},{1,2},{2,3},{4,5},{5,6},{6,7},{8,9},{9,10},{10,11},{12,13},{... | collective-permute-start | bytes 983048 | tf_op jit(solution)/shard_map/ppermute | solution.py:21
  209.0 9.6 %collective-permute-start.8 = (f32[80,4,256]{2,1,0:T(4,128)S(1)}, f32[80,4,256]{2,1,0:T(4,128)S(1)}, u32[]{:S(2)}, u32[]{:S(2)}) collective-permute-start(f32[80,4,256]{2,1,0:T(4,128)S(1)} %get-tuple-element.22), channel_id=1, source_target_pairs={{0,1},{1,2},{2,3},{4,5},{5,6},{6,7},{8,9},{9,10},{10,11},{12,13},{... | collective-permute-start | bytes 983048 | tf_op jit(solution)/shard_map/ppermute | solution.py:21
  211.7 11.1 %collective-permute-start.9 = (f32[80,4,256]{2,1,0:T(4,128)S(1)}, f32[80,4,256]{2,1,0:T(4,128)S(1)}, u32[]{:S(2)}, u32[]{:S(2)}) collective-permute-start(f32[80,4,256]{2,1,0:T(4,128)S(1)} %get-tuple-element.23), channel_id=1, source_target_pairs={{1,0},{2,1},{3,2},{5,4},{6,5},{7,6},{9,8},{10,9},{11,10},{13,12},{... | collective-permute-start | bytes 983048 | tf_op jit(solution)/shard_map/ppermute | solution.py:22
  224.1 16.9 %collective-permute-start.10 = (bf16[80,8,256]{2,1,0:T(8,128)(2,1)S(1)}, bf16[80,8,256]{2,1,0:T(8,128)(2,1)S(1)}, u32[]{:S(2)}, u32[]{:S(2)}) collective-permute-start(bf16[80,8,256]{2,1,0:T(8,128)(2,1)S(1)} %fusion.31), channel_id=1, source_target_pairs={{0,4},{4,8},{8,12},{12,16},{16,20},{20,24},{24,28},{28,32},{32,36}... | collective-permute-start | bytes 983048 | tf_op jit(solution)/shard_map/ppermute | solution.py:21
  224.2 16.8 %collective-permute-start.11 = (bf16[80,8,256]{2,1,0:T(8,128)(2,1)S(1)}, bf16[80,8,256]{2,1,0:T(8,128)(2,1)S(1)}, u32[]{:S(2)}, u32[]{:S(2)}) collective-permute-start(bf16[80,8,256]{2,1,0:T(8,128)(2,1)S(1)} %fusion.31), channel_id=1, source_target_pairs={{4,0},{8,4},{12,8},{16,12},{20,16},{24,20},{28,24},{32,28},{36,32}... | collective-permute-start | bytes 983048 | tf_op jit(solution)/shard_map/ppermute | solution.py:22
  290.7 21.2 %collective-permute-start.12 = (f32[80,8,256]{2,1,0:T(8,128)S(1)}, f32[80,8,256]{2,1,0:T(8,128)S(1)}, u32[]{:S(2)}, u32[]{:S(2)}) collective-permute-start(f32[80,8,256]{2,1,0:T(8,128)S(1)} %bitcast.145), channel_id=1, source_target_pairs={{0,252},{4,0},{8,4},{12,8},{16,12},{20,16},{24,20},{28,24},{32,28}... | collective-permute-start | bytes 1966088 | tf_op jit(solution)/shard_map/ppermute | solution.py:29
  296.3 109.6 %copy-start.35 = (f32[8]{0:T(128)S(1)}, f32[8]{0:T(128)}, u32[]{:S(2)}) copy-start(f32[8]{0:T(128)} %get-tuple-element.28) | copy-start | bytes 100
  296.3 109.6 %copy-start.36 = (f32[8]{0:T(128)S(1)}, f32[8]{0:T(128)}, u32[]{:S(2)}) copy-start(f32[8]{0:T(128)} %get-tuple-element.37) | copy-start | bytes 100
  296.3 109.6 %copy-start.37 = (f32[8]{0:T(128)S(1)}, f32[8]{0:T(128)}, u32[]{:S(2)}) copy-start(f32[8]{0:T(128)} %get-tuple-element.39) | copy-start | bytes 100
  296.3 109.6 %copy-start.38 = (f32[8]{0:T(128)S(1)}, f32[8]{0:T(128)}, u32[]{:S(2)}) copy-start(f32[8]{0:T(128)} %get-tuple-element.40) | copy-start | bytes 100
  296.3 109.6 %copy-start.39 = (f32[8]{0:T(128)S(1)}, f32[8]{0:T(128)}, u32[]{:S(2)}) copy-start(f32[8]{0:T(128)} %get-tuple-element.41) | copy-start | bytes 100
  296.3 109.6 %copy-start.40 = (f32[8]{0:T(128)S(1)}, f32[8]{0:T(128)}, u32[]{:S(2)}) copy-start(f32[8]{0:T(128)} %get-tuple-element.42) | copy-start | bytes 100
  296.3 109.6 %copy-start.42 = (f32[8]{0:T(128)S(1)}, f32[8]{0:T(128)}, u32[]{:S(2)}) copy-start(f32[8]{0:T(128)} %copy-done.41) | copy-start | bytes 100
  296.3 109.6 %copy-start.44 = (f32[8]{0:T(128)S(1)}, f32[8]{0:T(128)}, u32[]{:S(2)}) copy-start(f32[8]{0:T(128)} %copy-done.43) | copy-start | bytes 100
  296.4 25.5 %collective-permute-start.13 = (f32[80,8,256]{2,1,0:T(8,128)S(1)}, f32[80,8,256]{2,1,0:T(8,128)S(1)}, u32[]{:S(2)}, u32[]{:S(2)}) collective-permute-start(f32[80,8,256]{2,1,0:T(8,128)S(1)} %bitcast.147), channel_id=1, source_target_pairs={{0,4},{4,8},{8,12},{12,16},{16,20},{20,24},{24,28},{28,32},{32,36}... | collective-permute-start | bytes 1966088 | tf_op jit(solution)/shard_map/ppermute | solution.py:29
  322.1 83.7 %collective-permute-start.14 = (f32[80,4,256]{2,1,0:T(4,128)S(1)}, f32[80,4,256]{2,1,0:T(4,128)S(1)}, u32[]{:S(2)}, u32[]{:S(2)}) collective-permute-start(f32[80,4,256]{2,1,0:T(4,128)S(1)} %get-tuple-element.20), channel_id=1, source_target_pairs={{1,0},{2,1},{3,2},{5,4},{6,5},{7,6},{9,8},{10,9},{11,10},{13,12},{... | collective-permute-start | bytes 983048 | tf_op jit(solution)/shard_map/ppermute | solution.py:22
  323.4 82.4 %collective-permute-start.15 = (f32[80,4,256]{2,1,0:T(4,128)S(1)}, f32[80,4,256]{2,1,0:T(4,128)S(1)}, u32[]{:S(2)}, u32[]{:S(2)}) collective-permute-start(f32[80,4,256]{2,1,0:T(4,128)S(1)} %get-tuple-element.21), channel_id=1, source_target_pairs={{0,1},{1,2},{2,3},{4,5},{5,6},{6,7},{8,9},{9,10},{10,11},{12,13},{... | collective-permute-start | bytes 983048 | tf_op jit(solution)/shard_map/ppermute | solution.py:21
  (41 other events, 1489.5 us)
where the time goes:
time: 410 us; the launch traced here: 408 us
  blocking collectives  187 us (46%)
  waiting for transfers between devices  78.2 us (19%)
  starting transfers between devices  49.9 us (12%)
  local copies, waits for them, and re-layouts  43.7 us (11%)
  other arithmetic  40.1 us (10%)
  between operations  4.67 us (1%)
  matrix products  4.36 us (1%)
    psum x1, blocking collectives, per_device(): lax.psum((back_first, obs_first, jnp.sum(grad_first * grad_first)), ('til...  74.9 us
    psum x1, blocking collectives, per_device(): lax.psum((back_second, obs_second), ('tile', 'lev'))  72.8 us
    ppermute x4, waiting for transfers between devices, passed_along(): lax.ppermute(value, axis, [(i, (i + by) % peers) for i in range(peers)])  51.9 us
    psum x2, blocking collectives, evaluate(): evolved = lax.psum(partial_obs, 'lev')  39.3 us
    ppermute x6, starting transfers between devices, with_halo(): after = lax.ppermute(first, axis, down)  22.7 us
    scatter-add x2, other arithmetic, evaluate(): spread = jnp.zeros((members, ldev, 3 * bpd, 128), jnp.float32).at[:, :, s...  21.2 us
    ppermute x6, waiting for transfers between devices, with_halo(): before = lax.ppermute(last, axis, up)  19.4 us
    ppermute x6, starting transfers between devices, with_halo(): before = lax.ppermute(last, axis, up)  16.5 us
  transfers between devices with their start and end apart: 16, of which 11 were waited for; matrix products, arithmetic and copies ran while one was open for 3% of the time, Pallas kernels for 0%

commit v1 on v0

v1 whole, which is shorter than its diff:
```python
import math

import jax
import jax.numpy as jnp
from jax import lax
from jax.experimental import pallas as pl
from jax.experimental.pallas import tpu as pltpu
from jax.sharding import PartitionSpec as P

HV = 4
NS = 2 * HV + 1
STEP = 0.5
F32 = jnp.float32
BF16 = jnp.bfloat16
VM = pl.BlockSpec(memory_space=pltpu.VMEM)
SM = pl.BlockSpec(memory_space=pltpu.SMEM)


def call(body, outs, args, scalars, scratch=(), flops=0):
    specs = [SM] * scalars + [VM] * (len(args) - scalars)
    moved = sum(a.size * a.dtype.itemsize for a in args)
    moved += sum(math.prod(o.shape) * jnp.dtype(o.dtype).itemsize for o in outs)
    return pl.pallas_call(
        body,
        out_shape=tuple(outs),
        in_specs=specs,
        out_specs=tuple(VM for _ in outs),
        scratch_shapes=list(scratch),
        cost_estimate=pl.CostEstimate(flops=flops, bytes_accessed=moved, transcendentals=0),
        compiler_params=pltpu.CompilerParams(vmem_limit_bytes=48 * 1024 * 1024),
    )(*args)


def sds(shape, dtype):
    return jax.ShapeDtypeStruct(shape, dtype)


def split3(x):
    hi = x.astype(BF16)
    rest = x - hi.astype(F32)
    mid = rest.astype(BF16)
    lo = (rest - mid.astype(F32)).astype(BF16)
    return hi, mid, lo


def join3(hi, mid, lo):
    return (hi.astype(F32) + mid.astype(F32)) + lo.astype(F32)


def pack_ens_kernel(scal, ens, *outs):
    share = outs[0].shape[0]
    for k in range(4):
        outs[k][...] = ens[pl.ds(share * (scal[2] ^ k), share)]


def pack_ctl_kernel(scal, ctl, wt, *outs):
    share = outs[0].shape[0] - 3
    parts = split3(wt[...])
    for k in range(4):
        outs[k][pl.ds(0, share)] = ctl[pl.ds(share * (scal[2] ^ k), share)].astype(BF16)
        for i in range(3):
            outs[k][share + i] = parts[i]
    sq = jnp.zeros(outs[4].shape, F32)

    def body(m, acc):
        v = ctl[m]
        return acc + v * v

    outs[4][...] = lax.fori_loop(0, ctl.shape[0], body, sq, unroll=4)


def densify_kernel(scal, nb, loc, inv, inn, vb, d_own, x_core, x_edge, vw, vwt, acc):
    tile = scal[0]
    core_rel = 2 - 2 * (tile & 1)
    acc[...] = jnp.zeros(acc.shape, F32)
    for b in range(2):
        for j in range(loc.shape[1]):
            n = nb[b, j]
            rel = ((n >> 1) - tile + 65) & 63
            role = jnp.where(rel == 1, 0, jnp.where(rel == core_rel, 1, 2))
            slot = b * 6 + role * 2 + (n & 1)
            acc[slot] = acc[slot] + loc[b, j].astype(F32)
    for role, out in enumerate((d_own, x_core, x_edge)):
        for b in range(2):
            for h in range(2):
                out[128 * b : 128 * b + 128, 128 * h : 128 * h + 128] = acc[
                    b * 6 + role * 2 + h
                ].astype(BF16)
    for out in (x_core, x_edge):
        for i, v in enumerate(split3(inv[...]) + split3(inn[...])):
            out[256 + 16 * i : 272 + 16 * i, :] = v
    lev = vb.shape[0]
    row = lax.broadcasted_iota(jnp.int32, (lev, 128), 0)
    for s in range(NS):
        col = jnp.broadcast_to(vb[:, s : s + 1], (lev, 128))
        src = row + (s - HV)
        vw[s] = jnp.where((src >= 0) & (src < lev), col, 0.0)
        src = row + (HV - s)
        moved = pltpu.roll(col, (s - HV) % lev, 0)
        vwt[s] = jnp.where((src >= 0) & (src < lev), moved, 0.0)


def assemble_kernel(scal, e0, e1, e2, e3, out):
    for k, e in enumerate((e0, e1, e2, e3)):
        out[:, scal[1] ^ k] = e[...]


def forward_part(src, vw, avb, umat, ens3, dmats, w, hxs, norm):
    ms = src.shape[0]
    lev = 32

    def smooth(m, _):
        block = src[m].reshape(lev, 256)
        cols = []
        for h in range(2):
            a = block[:, 128 * h : 128 * h + 128]
            tot = vw[HV] * a
            for s in range(NS):
                if s != HV:
                    tot = tot + vw[s] * pltpu.roll(a, (HV - s) % lev, 0)
            cols.append(tot)
        avb[pl.ds(pl.multiple_of(lev * m, lev), lev), :] = jnp.concatenate(cols, axis=1).astype(
            BF16
        )
        return 0

    lax.fori_loop(0, ms, smooth, 0)
    for ens, d, hx in zip(ens3, dmats, hxs):
        umat[...] = lax.dot_general(
            avb[...], d, (((1,), (1,)), ((), ())), preferred_element_type=F32
        )

        def member(m, acc):
            e = ens[m].astype(F32).reshape(lev, 256)
            return acc + e * umat[pl.ds(pl.multiple_of(lev * m, lev), lev), :]

        dx = lax.fori_loop(0, ms, member, jnp.zeros((lev, 256), F32), unroll=2)
        hx(
            jnp.dot(
                w[:, 0:lev], dx * norm, precision=lax.Precision.HIGHEST, preferred_element_type=F32
            )
        )


def adjoint_part(qs, wt, vwt, ens3, dmats, ua, umat, out, norm):
    ms = out.shape[0]
    lev = 32
    for r, (q, ens, d) in enumerate(zip(qs, ens3, dmats)):
        dxa = (
            jnp.dot(
                wt[:, 0:16], q, precision=lax.Precision.HIGHEST, preferred_element_type=F32
            )
            * norm
        )

        def member(m, _):
            e = ens[m].astype(F32).reshape(lev, 256)
            ua[pl.ds(pl.multiple_of(lev * m, lev), lev), :] = (e * dxa).astype(BF16)
            return 0

        lax.fori_loop(0, ms, member, 0, unroll=2)
        part = jnp.dot(ua[...], d, preferred_element_type=F32)
        if r == 0:
            umat[...] = part
        else:
            umat[...] = umat[...] + part

    def spread(m, _):
        block = umat[pl.ds(pl.multiple_of(lev * m, lev), lev), :]
        cols = []
        for h in range(2):
            a = block[:, 128 * h : 128 * h + 128]
            tot = vwt[HV] * a
            for s in range(NS):
                if s != HV:
                    tot = tot + vwt[s] * pltpu.roll(a, (s - HV) % lev, 0)
            cols.append(tot)
        out[m] = jnp.concatenate(cols, axis=1).reshape(4, 8, 256)
        return 0

    lax.fori_loop(0, ms, spread, 0)


def dmats_of(d_own, x_core, x_edge):
    return d_own[...], x_core[0:256, :], x_edge[0:256, :]


def obs_of(x):
    return (
        join3(x[256:272, :], x[272:288, :], x[288:304, :]),
        join3(x[304:320, :], x[320:336, :], x[336:352, :]),
    )


def first_kernel(
    norm, scal, c0, c1, c2, c3, e_own, e_core, e_edge, d_own, x_core, x_edge, vw,
    cm, hx_core, hx_oe, w, wt, src, wsq, avb, umat,
):
    share = src.shape[0]
    wsq[...] = jnp.zeros(wsq.shape, F32)
    for k, c in enumerate((c0, c1, c2, c3)):
        group = scal[1] ^ k
        val = c[pl.ds(0, share)]
        cm[:, group] = val
        src[:, group] = val.astype(F32)
        wsq[pl.ds(pl.multiple_of(8 * group, 8), 8), :] = join3(
            c[share], c[share + 1], c[share + 2]
        )[:, 0:128]
    w[...] = wsq[...].T[0:16, :]
    wt[...] = wsq[0:32, :]

    def put_own(v):
        hx_oe[0:16, :] = v

    def put_core(v):
        hx_core[...] = v

    def put_edge(v):
        hx_oe[16:32, :] = v

    forward_part(
        src, vw, avb, umat, (e_own, e_core, e_edge), dmats_of(d_own, x_core, x_edge), w,
        (put_own, put_core, put_edge), norm,
    )


def second_kernel(
    norm, scal, h_oe, h_core, inv, inn, cm, e_own, e_core, e_edge, d_own, x_core, x_edge,
    vw, vwt, w, wt, s0, a0, a1, a2, a3, hx_core, hx_oe, adj, ua, umat,
):
    share = adj.shape[0]
    ic, yc = obs_of(x_core)
    ie, ye = obs_of(x_edge)
    qs = (
        inv[...] * (h_oe[0:16, :] - inn[...]),
        ic * (h_core[...] - yc),
        ie * (h_oe[16:32, :] - ye),
    )
    ens3 = (e_own, e_core, e_edge)
    dmats = dmats_of(d_own, x_core, x_edge)
    adjoint_part(qs, wt, vwt, ens3, dmats, ua, umat, adj, norm)
    for k, a in enumerate((a0, a1, a2, a3)):
        a[...] = adj[:, scal[1] ^ k].astype(BF16)

    def total(m, carry):
        gg, cg = carry
        c = cm[m].astype(F32)
        g = c + adj[m]
        adj[m] = g
        return gg + jnp.sum(g * g, axis=0), cg + jnp.sum(c * g, axis=0)

    zero = jnp.zeros((8, 256), F32)
    gg, cg = lax.fori_loop(0, share, total, (zero, zero))

    def put_own(v):
        hx_oe[0:16, :] = v

    def put_core(v):
        hx_core[0:16, :] = v

    def put_edge(v):
        hx_oe[16:32, :] = v

    forward_part(
        adj, vw, ua, umat, ens3, dmats, w, (put_own, put_core, put_edge), norm
    )
    hx_core[16:24, :] = jnp.zeros((8, 256), F32)
    hx_core[16:17, :] = jnp.sum(s0[...], axis=0, keepdims=True)
    hx_core[17:18, :] = jnp.sum(gg, axis=0, keepdims=True)
    hx_core[18:19, :] = jnp.sum(cg, axis=0, keepdims=True)


def sums_kernel(hs, h_core, h1_oe, h1_core, inv, inn, x_core, out):
    ic, yc = obs_of(x_core)

    def rows(h1, i, y, d):
        diff = h1 - y
        q = i * diff
        return [
            jnp.sum(q * diff, axis=0, keepdims=True),
            jnp.sum(q * d, axis=0, keepdims=True),
            jnp.sum(i * d * d, axis=0, keepdims=True),
        ]

    own = rows(h1_oe[0:16, :], inv[...], inn[...], hs[0:16, :])
    core = rows(h1_core[...], ic, yc, h_core[...])
    out[...] = hs[32:40, :]
    for i in range(3):
        out[3 + i : 4 + i, :] = own[i] + core[i]


def third_kernel(
    norm, scal, h_oe, h_core, inv, e_own, e_core, e_edge, d_own, x_core, x_edge,
    vwt, wt, a0, a1, a2, a3, adj, ua, umat,
):
    ic, _ = obs_of(x_core)
    ie, _ = obs_of(x_edge)
    qs = (inv[...] * h_oe[0:16, :], ic * h_core[...], ie * h_oe[16:32, :])
    adjoint_part(
        qs, wt, vwt, (e_own, e_core, e_edge), dmats_of(d_own, x_core, x_edge), ua, umat, adj,
        norm,
    )
    for k, a in enumerate((a0, a1, a2, a3)):
        a[...] = adj[:, scal[1] ^ k].astype(BF16)


def grad_first_kernel(scal, ctl, a0, a1, a2, a3, out):
    share = a0.shape[0]
    for k, a in enumerate((a0, a1, a2, a3)):
        at = pl.ds(share * (scal[2] ^ k), share)
        out[at] = ctl[at] + a[...].astype(F32)


def grad_second_kernel(count, scal, g1, a0, a1, a2, a3, sums, out, costs):
    tot = jnp.sum(sums[...], axis=1, keepdims=True)
    cc, gg, cg = tot[0:1], tot[1:2], tot[2:3]
    dd, qd, rd = tot[3:4], tot[4:5], tot[5:6]
    tau = STEP / jnp.sqrt(gg / count + 1e-06)
    first = 0.5 * cc + 0.5 * dd
    second = 0.5 * (cc - 2.0 * tau * cg + tau * tau * gg) + 0.5 * (
        dd - 2.0 * tau * qd + tau * tau * rd
    )
    costs[0:1, :] = jnp.broadcast_to(first / count, (1, 128))
    costs[1:2, :] = jnp.broadcast_to(second / count, (1, 128))
    costs[2:8, :] = jnp.zeros((6, 128), F32)
    tb = jnp.broadcast_to(tau, (8, 256))
    share = a0.shape[0]
    for k, a in enumerate((a0, a1, a2, a3)):

        def body(m, _, a=a, k=k):
            at = share * (scal[2] ^ k) + m
            g = g1[at]
            out[at] = g - tb * (g + a[m].astype(F32))
            return 0

        lax.fori_loop(0, share, body, 0, unroll=4)


def make_pairs(tiles, levs):
    def flat(t, g):
        return t * levs + g

    def zh(t):
        return (t >> 3) & 1

    edge = []
    for t in range(tiles):
        e = (t + 1) % tiles if t & 1 else (t - 1) % tiles
        for g in range(levs):
            edge.append((flat(t, g), flat(e, g if zh(t) == zh(e) else levs - 1 - g)))
    far = [(flat(t, g), flat(t ^ 8, levs - 1 - g)) for t in range(tiles) for g in range(levs)]

    def tile_xor(k):
        return [(t, t ^ k) for t in range(tiles)]

    def lev_xor(k):
        return [(g, g ^ k) for g in range(levs)]

    return edge, far, tile_xor, lev_xor


def per_device(
    control, ensemble, loc_blocks, neighbours, vert_band, channel_weights, innovation, inv_error
):
    members, ldev, pdev = control.shape
    tiles = lax.axis_size("tile")
    levs = lax.axis_size("lev")
    lev = levs * ldev
    share = members // levs
    rows = share * lev
    norm = 1.0 / math.sqrt(members - 1)
    edge, far, tile_xor, lev_xor = make_pairs(tiles, levs)
    both = ("tile", "lev")
    tile_pos = lax.axis_index("tile").astype(jnp.int32)
    lev_pos = lax.axis_index("lev").astype(jnp.int32)
    mset = lev_pos ^ (3 * ((tile_pos >> 3) & 1))
    scal = jnp.stack([tile_pos, lev_pos, mset, mset])

    def swap_core(x):
        return lax.ppermute(x, "tile", tile_xor(1))

    def swap_edge(x):
        return lax.ppermute(x, both, edge)

    def shuffle(parts):
        return [parts[0]] + [lax.ppermute(parts[k], "lev", lev_xor(k)) for k in range(1, 4)]

    chunk = sds((share, ldev, pdev), BF16)
    eparts = call(pack_ens_kernel, [chunk] * 4, (scal, ensemble), 1)
    eparts = shuffle(eparts)
    d_own, x_core, x_edge, vw, vwt = call(
        densify_kernel,
        [
            sds((256, 256), BF16), sds((352, 256), BF16), sds((352, 256), BF16),
            sds((NS, lev, 128), F32), sds((NS, lev, 128), F32),
        ],
        (scal, neighbours, loc_blocks, inv_error, innovation, vert_band),
        2,
        [pltpu.VMEM((12, 128, 128), F32)],
    )
    wt_own = jnp.pad(channel_weights.T, ((0, 0), (0, pdev - channel_weights.shape[0])))
    packed = call(
        pack_ctl_kernel,
        [sds((share + 3, ldev, pdev), BF16)] * 4 + [sds((ldev, pdev), F32)],
        (scal, control, wt_own),
        1,
    )
    s0 = packed[4]
    x_edge = swap_edge(x_edge)
    x_core = swap_core(x_core)
    field = sds((share, levs, ldev, pdev), BF16)
    (e_own,) = call(assemble_kernel, [field], (scal, *eparts), 1)
    e_edge = swap_edge(e_own)
    e_core = swap_core(e_own)
    cparts = shuffle(packed[:4])

    umat = pltpu.VMEM((rows, pdev), F32)
    half = pltpu.VMEM((rows, pdev), BF16)
    full = pltpu.VMEM((share, levs, ldev, pdev), F32)
    obs = channel_weights.shape[0]
    mm = 2 * rows * pdev * pdev * 3

    def bind(fn, arg):
        def body(*refs):
            fn(arg, *refs)

        return body

    cm, hx_core, hx_oe, w, wt = call(
        bind(first_kernel, norm),
        [
            field, sds((obs, pdev), F32), sds((2 * obs, pdev), F32),
            sds((obs, 128), F32), sds((lev, 128), F32),
        ],
        (scal, *cparts, e_own, e_core, e_edge, d_own, x_core, x_edge, vw),
        1,
        [full, pltpu.VMEM((128, 128), F32), half, umat],
        mm,
    )

    def reduce_obs(core_msg, oe):
        got = swap_core(core_msg)
        mine = jnp.concatenate([oe[:obs] + got[:obs], oe[obs:]], axis=0)
        other = swap_edge(mine)
        tot = mine + jnp.concatenate([other[obs:], other[:obs]], axis=0)
        if core_msg.shape[0] > obs:
            tot = jnp.concatenate([tot, core_msg[obs:] + got[obs:]], axis=0)
        tot = tot + lax.ppermute(tot, "lev", lev_xor(1))
        tot = tot + lax.ppermute(tot, "lev", lev_xor(2))
        return tot, swap_core(tot[:obs])

    h1_oe, h1_core = reduce_obs(hx_core, hx_oe)
    outs = call(
        bind(second_kernel, norm),
        [chunk] * 4 + [sds((obs + 8, pdev), F32), sds((2 * obs, pdev), F32)],
        (
            scal, h1_oe, h1_core, inv_error, innovation, cm, e_own, e_core, e_edge,
            d_own, x_core, x_edge, vw, vwt, w, wt, s0,
        ),
        1,
        [full, half, umat],
        2 * mm,
    )
    hs, hd_core = reduce_obs(outs[4], outs[5])
    sums = call(
        sums_kernel,
        [sds((8, pdev), F32)],
        (hs, hd_core, h1_oe, h1_core, inv_error, innovation, x_core),
        0,
    )[0]
    aparts = shuffle(outs[:4])
    bparts = call(
        bind(third_kernel, norm),
        [chunk] * 4,
        (
            scal, hs, hd_core, inv_error, e_own, e_core, e_edge, d_own, x_core, x_edge,
            vwt, wt,
        ),
        1,
        [full, half, umat],
        mm,
    )
    bparts = shuffle(bparts)
    for k in (2, 6):
        sums = sums + lax.ppermute(sums, "tile", tile_xor(k))
    sums = sums + lax.ppermute(sums, both, far)
    for k in (16, 48):
        sums = sums + lax.ppermute(sums, "tile", tile_xor(k))
    whole = sds((members, ldev, pdev), F32)
    (grad_first,) = call(grad_first_kernel, [whole], (scal, control, *aparts), 1)
    count = float(members * lev * pdev * tiles)
    grad_second, costs = call(
        bind(grad_second_kernel, count),
        [whole, sds((8, 128), F32)],
        (scal, grad_first, *bparts, sums),
        1,
    )
    return grad_first, grad_second, costs[0:2, 0]


def solution(mesh):
    placed = (
        P(None, "lev", "tile"),
        P(None, "lev", "tile"),
        P("tile", None, None, None),
        P("tile", None),
        P(),
        P(None, "lev"),
        P(None, "tile"),
        P(None, "tile"),
    )
    return jax.shard_map(
        per_device,
        mesh=mesh,
        in_specs=placed,
        out_specs=(P(None, "lev", "tile"), P(None, "lev", "tile"), P()),
        check_vma=False,
    )
```

time: 410 us -> 128 us (0.31)
  blocking collectives: 187 us -> 0 us
  local copies, waits for them, and re-layouts: 43.7 us -> 2.89 us
  other arithmetic: 40.1 us -> 0.16 us
  Pallas kernels: 0 us -> 17.4 us
  waiting for transfers between devices: 78.2 us -> 63 us
  starting transfers between devices: 49.9 us -> 43.8 us
  matrix products: 4.36 us -> 0 us
    psum x4 -> x0, blocking collectives: 187 us -> none  [the longest x1 74.9 us: per_device(): lax.psum((back_first, obs_first, jnp.sum(grad_first * grad_first)), ('til...]
    scatter-add x2 -> x0, other arithmetic: 21.2 us -> none  [evaluate(): spread = jnp.zeros((members, ldev, 3 * bpd, 128), jnp.float32).at[:, :, s...]
    pallas_call x0 -> x10, Pallas kernels: none -> 17.4 us  [call(): pl.pallas_call(body, out_shape=tuple(outs), in_specs=specs, out_specs=tup...]
    reshape x6 -> x0, local copies, waits for them, and re-layouts: 15.8 us -> none  [the longest x2 8.81 us: evaluate(): spread = spread.reshape(members, ldev, 3, pdev)]
    ppermute x16 -> x31, waiting for transfers between devices: 78.2 us -> 63 us  [the longest x4 19.6 us: swap_edge(): return lax.ppermute(x, both, edge)]
    slice x6 -> x5, local copies, waits for them, and re-layouts: 12.9 us -> 0.64 us  [the longest x1 0.63 us: per_device(): return (grad_first, grad_second, costs[0:2, 0])]
    gather x2 -> x0, local copies, waits for them, and re-layouts: 6.22 us -> none  [evaluate(): jnp.take(widened.reshape(members, ldev, 3 * bpd, 128), slots, axis=2)]
    reduce_sum x6 -> x0, other arithmetic: 6.17 us -> none  [the longest x2 2.68 us: evaluate(): back_term = 0.5 * jnp.sum(field * field)]
  transfers between devices with their start and end apart: 16 -> 31, of which waited for: 11 -> 20; matrix products, arithmetic and copies ran while one was open for 3% -> 0% of each run, Pallas kernels for 0% -> 5%
where the time goes in v1:
time: 128 us
  waiting for transfers between devices  63 us (49%)
  starting transfers between devices  43.8 us (34%)
  Pallas kernels  17.4 us (14%)
  local copies, waits for them, and re-layouts  2.89 us (2%)
    ppermute x12, starting transfers between devices, shuffle(): lax.ppermute(parts[k], 'lev', lev_xor(k))  22.4 us
    ppermute x4, waiting for transfers between devices, swap_edge(): return lax.ppermute(x, both, edge)  19.6 us
    ppermute x12, waiting for transfers between devices, shuffle(): lax.ppermute(parts[k], 'lev', lev_xor(k))  17.9 us
    pallas_call x10, Pallas kernels, call(): pl.pallas_call(body, out_shape=tuple(outs), in_specs=specs, out_specs=tup...  17.4 us
    ppermute x4, waiting for transfers between devices, per_device(): sums = sums + lax.ppermute(sums, 'tile', tile_xor(k))  10.7 us
    ppermute x4, starting transfers between devices, per_device(): sums = sums + lax.ppermute(sums, 'tile', tile_xor(k))  6.55 us
    ppermute x4, starting transfers between devices, swap_edge(): return lax.ppermute(x, both, edge)  5.09 us
    ppermute x2, waiting for transfers between devices, reduce_obs(): tot = tot + lax.ppermute(tot, 'lev', lev_xor(2))  4.99 us
  transfers between devices with their start and end apart: 31, of which 20 were waited for; matrix products, arithmetic and copies ran while one was open for 0% of the time, Pallas kernels for 5%

profile of v1, /device:TPU:2, one launch (start us, length us, event | category | flops | bytes accessed | tf_op | source)
XLA Modules:
  0.0 128.1 jit_solution(11165585010740205422)
XLA Ops:
  4.3 3.3 %collective-permute-start.4 = (bf16[20,8,256]{2,1,0:T(8,128)(2,1)S(1)}, bf16[20,8,256]{2,1,0:T(8,128)(2,1)S(1)}, u32[]{:S(2)}, u32[]{:S(2)}) collective-permute-start(bf16[20,8,256]{2,1,0:T(8,128)(2,1)S(1)} %get-tuple-element.40), channel_id=1, source_target_pairs={{0,2},{1,3},{2,0},{3,1},{4,6},{5,7},{6,4},{7,5},{8,10},{9,11},{10,... | collective-permute-start | bytes 245768 | tf_op jit(solution)/shard_map/ppermute | solution.py:386
  7.6 6.5 %collective-permute-done.4.e2 = bf16[20,8,256]{2,1,0:T(8,128)(2,1)S(1)} collective-permute-done((bf16[20,8,256]{2,1,0:T(8,128)(2,1)S(1)}, bf16[20,8,256]{2,1,0:T(8,128)(2,1)S(1)}, u32[]{:S(2)}, u32[]{:S(2)}) %collective-permute-start.4) | collective-permute-done | bytes 81952 | tf_op jit(solution)/shard_map/ppermute | solution.py:386
  14.7 4.5 %collective-permute-start.7 = (bf16[20,4,8,256]{3,2,1,0:T(8,128)(2,1)S(1)}, bf16[20,4,8,256]{3,2,1,0:T(8,128)(2,1)S(1)}, u32[]{:S(2)}, u32[]{:S(2)}) collective-permute-start(bf16[20,4,8,256]{3,2,1,0:T(8,128)(2,1)S(1)} %shard_map.105.refs_5_.refs_6_.refs_4_), channel_id=1, source_target_pairs={{0,255},{1,254},{2,253},{3,252},{4,8},{5,9},{6,10},{7,11},{8,4},{9... | collective-permute-start | bytes 983048 | tf_op jit(solution)/shard_map/ppermute | solution.py:383
  19.9 3.3 %collective-permute-start = (bf16[23,8,256]{2,1,0:T(8,128)(2,1)S(1)}, bf16[23,8,256]{2,1,0:T(8,128)(2,1)S(1)}, u32[]{:S(2)}, u32[]{:S(2)}) collective-permute-start(bf16[23,8,256]{2,1,0:T(8,128)(2,1)S(1)} %get-tuple-element.35), channel_id=1, source_target_pairs={{0,1},{1,0},{2,3},{3,2},{4,5},{5,4},{6,7},{7,6},{8,9},{9,8},{10,11... | collective-permute-start | bytes 282632 | tf_op jit(solution)/shard_map/ppermute | solution.py:386
  25.1 6.3 %collective-permute-done.refs_2_ = bf16[23,8,256]{2,1,0:T(8,128)(2,1)S(1)} collective-permute-done((bf16[23,8,256]{2,1,0:T(8,128)(2,1)S(1)}, bf16[23,8,256]{2,1,0:T(8,128)(2,1)S(1)}, u32[]{:S(2)}, u32[]{:S(2)}) %collective-permute-start) | collective-permute-done | bytes 94240 | tf_op jit(solution)/shard_map/ppermute | solution.py:386
  31.5 2.4 %collective-permute-start.2 = (bf16[23,8,256]{2,1,0:T(8,128)(2,1)S(1)}, bf16[23,8,256]{2,1,0:T(8,128)(2,1)S(1)}, u32[]{:S(2)}, u32[]{:S(2)}) collective-permute-start(bf16[23,8,256]{2,1,0:T(8,128)(2,1)S(1)} %get-tuple-element.37), channel_id=1, source_target_pairs={{0,3},{1,2},{2,1},{3,0},{4,7},{5,6},{6,5},{7,4},{8,11},{9,10},{10,... | collective-permute-start | bytes 282632 | tf_op jit(solution)/shard_map/ppermute | solution.py:386
  33.8 4.1 %collective-permute-done.2.refs_4_ = bf16[23,8,256]{2,1,0:T(8,128)(2,1)S(1)} collective-permute-done((bf16[23,8,256]{2,1,0:T(8,128)(2,1)S(1)}, bf16[23,8,256]{2,1,0:T(8,128)(2,1)S(1)}, u32[]{:S(2)}, u32[]{:S(2)}) %collective-permute-start.2) | collective-permute-done | bytes 94240 | tf_op jit(solution)/shard_map/ppermute | solution.py:386
  38.0 4.5 %collective-permute-done.9.refs_10_.refs_11_.refs_9_ = bf16[352,256]{1,0:T(8,128)(2,1)S(1)} collective-permute-done((bf16[352,256]{1,0:T(8,128)(2,1)S(1)}, bf16[352,256]{1,0:T(8,128)(2,1)S(1)}, u32[]{:S(2)}, u32[]{:S(2)}) %collective-permute-start.9) | collective-permute-done | bytes 180256 | tf_op jit(solution)/shard_map/ppermute | solution.py:383
  42.4 3.1 %shard_map.107 = (bf16[20,4,8,256]{3,2,1,0:T(8,128)(2,1)S(1)}, f32[16,256]{1,0:T(8,128)S(1)}, f32[32,256]{1,0:T(8,128)S(1)}, f32[16,128]{1,0:T(8,128)S(1)}, f32[32,128]{1,0:T(8,128)S(1)}) custom-call(s32[4]{0:T(128)S(1)} %pad_add_fusion.scal.refs_0_, bf16[23,8,256]{2,1,0:T(8,128)(2,1)S(1)} %get-tuple-element.34.refs_1_, ...), custom_call_target="tpu_custom_call" | custom-call | flops 251658240 | bytes 2400272 | tf_op jit(solution)/shard_map/pallas_call | solution.py:23
  47.1 7.6 %collective-permute-done.11 = f32[32,256]{1,0:T(8,128)S(1)} collective-permute-done((f32[32,256]{1,0:T(8,128)S(1)}, f32[32,256]{1,0:T(8,128)S(1)}, u32[]{:S(2)}, u32[]{:S(2)}) %collective-permute-start.11) | collective-permute-done | bytes 32800 | tf_op jit(solution)/shard_map/ppermute | solution.py:383
  56.0 2.8 %collective-permute-done.12 = f32[32,256]{1,0:T(8,128)S(1)} collective-permute-done((f32[32,256]{1,0:T(8,128)S(1)}, f32[32,256]{1,0:T(8,128)S(1)}, u32[]{:S(2)}, u32[]{:S(2)}) %collective-permute-start.12) | collective-permute-done | bytes 32800 | tf_op jit(solution)/shard_map/ppermute | solution.py:448
  60.6 2.9 %collective-permute-done.13 = f32[32,256]{1,0:T(8,128)S(1)} collective-permute-done((f32[32,256]{1,0:T(8,128)S(1)}, f32[32,256]{1,0:T(8,128)S(1)}, u32[]{:S(2)}, u32[]{:S(2)}) %collective-permute-start.13) | collective-permute-done | bytes 32800 | tf_op jit(solution)/shard_map/ppermute | solution.py:449
  64.8 5.5 %shard_map.108 = (bf16[20,8,256]{2,1,0:T(8,128)(2,1)S(1)}, bf16[20,8,256]{2,1,0:T(8,128)(2,1)S(1)}, bf16[20,8,256]{2,1,0:T(8,128)(2,1)S(1)}, bf16[20,8,256]{2,1,...) custom-call(s32[4]{0:T(128)S(1)} %pad_add_fusion.scal.refs_0_, f32[32,256]{1,0:T(8,128)S(1)} %add.47.refs_1_.h1_oe, ...), custom_call_target="tpu_custom_call" | custom-call | flops 503316480 | bytes 2596880 | tf_op jit(solution)/shard_map/pallas_call | solution.py:23
  71.8 7.5 %collective-permute-done.19 = f32[32,256]{1,0:T(8,128)S(1)} collective-permute-done((f32[32,256]{1,0:T(8,128)S(1)}, f32[32,256]{1,0:T(8,128)S(1)}, u32[]{:S(2)}, u32[]{:S(2)}) %collective-permute-start.19) | collective-permute-done | bytes 32800 | tf_op jit(solution)/shard_map/ppermute | solution.py:383
  79.4 3.1 %collective-permute-start.20 = (f32[40,256]{1,0:T(8,128)S(1)}, f32[40,256]{1,0:T(8,128)S(1)}, u32[]{:S(2)}, u32[]{:S(2)}) collective-permute-start(f32[40,256]{1,0:T(8,128)S(1)} %pad_maximum_fusion), channel_id=1, source_target_pairs={{0,1},{1,0},{2,3},{3,2},{4,5},{5,4},{6,7},{7,6},{8,9},{9,8},{10,11... | collective-permute-start | bytes 122888 | tf_op jit(solution)/shard_map/ppermute | solution.py:448
  84.5 2.8 %collective-permute-start.21 = (f32[40,256]{1,0:T(8,128)S(1)}, f32[40,256]{1,0:T(8,128)S(1)}, u32[]{:S(2)}, u32[]{:S(2)}) collective-permute-start(f32[40,256]{1,0:T(8,128)S(1)} %fusion), channel_id=1, source_target_pairs={{0,2},{1,3},{2,0},{3,1},{4,6},{5,7},{6,4},{7,5},{8,10},{9,11},{10,... | collective-permute-start | bytes 122888 | tf_op jit(solution)/shard_map/ppermute | solution.py:449
  87.3 2.1 %collective-permute-done.21 = f32[40,256]{1,0:T(8,128)S(1)} collective-permute-done((f32[40,256]{1,0:T(8,128)S(1)}, f32[40,256]{1,0:T(8,128)S(1)}, u32[]{:S(2)}, u32[]{:S(2)}) %collective-permute-start.21) | collective-permute-done | bytes 40992 | tf_op jit(solution)/shard_map/ppermute | solution.py:449
  90.8 3.6 %collective-permute-done.26 = f32[8,256]{1,0:T(8,128)S(1)} collective-permute-done((f32[8,256]{1,0:T(8,128)S(1)}, f32[8,256]{1,0:T(8,128)S(1)}, u32[]{:S(2)}, u32[]{:S(2)}) %collective-permute-start.26) | collective-permute-done | bytes 8224 | tf_op jit(solution)/shard_map/ppermute | solution.py:485
  94.5 4.9 %collective-permute-done.27 = f32[8,256]{1,0:T(8,128)S(1)} collective-permute-done((f32[8,256]{1,0:T(8,128)S(1)}, f32[8,256]{1,0:T(8,128)S(1)}, u32[]{:S(2)}, u32[]{:S(2)}) %collective-permute-start.27) | collective-permute-done | bytes 8224 | tf_op jit(solution)/shard_map/ppermute | solution.py:485
  99.3 2.8 %collective-permute-start.16 = (bf16[20,8,256]{2,1,0:T(8,128)(2,1)S(1)}, bf16[20,8,256]{2,1,0:T(8,128)(2,1)S(1)}, u32[]{:S(2)}, u32[]{:S(2)}) collective-permute-start(bf16[20,8,256]{2,1,0:T(8,128)(2,1)S(1)} %get-tuple-element.55), channel_id=1, source_target_pairs={{0,2},{1,3},{2,0},{3,1},{4,6},{5,7},{6,4},{7,5},{8,10},{9,11},{10,... | collective-permute-start | bytes 245768 | tf_op jit(solution)/shard_map/ppermute | solution.py:386
  104.2 6.5 %collective-permute-start.29 = (f32[8,256]{1,0:T(8,128)S(1)}, f32[8,256]{1,0:T(8,128)S(1)}, u32[]{:S(2)}, u32[]{:S(2)}) collective-permute-start(f32[8,256]{1,0:T(8,128)S(1)} %add.55), channel_id=1, source_target_pairs={{0,64},{4,68},{8,72},{12,76},{16,80},{20,84},{24,88},{28,92},{32,9... | collective-permute-start | bytes 24584 | tf_op jit(solution)/shard_map/ppermute | solution.py:488
  110.6 2.8 %shard_map.110 = (bf16[20,8,256]{2,1,0:T(8,128)(2,1)S(1)}, bf16[20,8,256]{2,1,0:T(8,128)(2,1)S(1)}, bf16[20,8,256]{2,1,0:T(8,128)(2,1)S(1)}, bf16[20,8,256]{2,1,0:T(8,128)(2,1)S(1)}) custom-call(s32[4]{0:T(128)S(1)} %pad_add_fusion.scal.refs_0_, f32[40,256]{1,0:T(8,128)S(1)} %add.52.refs_1_.hs, f32[16,256]{1,0:T(8,128)S(1)} %collective-permute-done.22.refs_2_.h_core, ...), custom_call_target="tpu_custom_call" | custom-call | flops 251658240 | bytes 2039824 | tf_op jit(solution)/shard_map/pallas_call | solution.py:23
  113.4 4.0 %collective-permute-start.23 = (bf16[20,8,256]{2,1,0:T(8,128)(2,1)S(1)}, bf16[20,8,256]{2,1,0:T(8,128)(2,1)S(1)}, u32[]{:S(2)}, u32[]{:S(2)}) collective-permute-start(bf16[20,8,256]{2,1,0:T(8,128)(2,1)S(1)} %get-tuple-element.60), channel_id=1, source_target_pairs={{0,1},{1,0},{2,3},{3,2},{4,5},{5,4},{6,7},{7,6},{8,9},{9,8},{10,11... | collective-permute-start | bytes 245768 | tf_op jit(solution)/shard_map/ppermute | solution.py:386
  121.4 2.2 %collective-permute-done.30 = f32[8,256]{1,0:T(8,128)S(1)} collective-permute-done((f32[8,256]{1,0:T(8,128)S(1)}, f32[8,256]{1,0:T(8,128)S(1)}, u32[]{:S(2)}, u32[]{:S(2)}) %collective-permute-start.30) | collective-permute-done | bytes 8224 | tf_op jit(solution)/shard_map/ppermute | solution.py:488
  (91 shorter events, 28.3 us)
Async XLA Ops:
  2.3 5.3 %collective-permute-start.3 = (bf16[20,8,256]{2,1,0:T(8,128)(2,1)S(1)}, bf16[20,8,256]{2,1,0:T(8,128)(2,1)S(1)}, u32[]{:S(2)}, u32[]{:S(2)}) collective-permute-start(bf16[20,8,256]{2,1,0:T(8,128)(2,1)S(1)} %get-tuple-element.39), channel_id=1, source_target_pairs={{0,1},{1,0},{2,3},{3,2},{4,5},{5,4},{6,7},{7,6},{8,9},{9,8},{10,11... | collective-permute-start | bytes 245768 | tf_op jit(solution)/shard_map/ppermute | solution.py:386
  4.3 9.8 %collective-permute-start.4 = (bf16[20,8,256]{2,1,0:T(8,128)(2,1)S(1)}, bf16[20,8,256]{2,1,0:T(8,128)(2,1)S(1)}, u32[]{:S(2)}, u32[]{:S(2)}) collective-permute-start(bf16[20,8,256]{2,1,0:T(8,128)(2,1)S(1)} %get-tuple-element.40), channel_id=1, source_target_pairs={{0,2},{1,3},{2,0},{3,1},{4,6},{5,7},{6,4},{7,5},{8,10},{9,11},{10,... | collective-permute-start | bytes 245768 | tf_op jit(solution)/shard_map/ppermute | solution.py:386
  7.6 6.5 %collective-permute-start.5 = (bf16[20,8,256]{2,1,0:T(8,128)(2,1)S(1)}, bf16[20,8,256]{2,1,0:T(8,128)(2,1)S(1)}, u32[]{:S(2)}, u32[]{:S(2)}) collective-permute-start(bf16[20,8,256]{2,1,0:T(8,128)(2,1)S(1)} %get-tuple-element.41), channel_id=1, source_target_pairs={{0,3},{1,2},{2,1},{3,0},{4,7},{5,6},{6,5},{7,4},{8,11},{9,10},{10,... | collective-permute-start | bytes 245768 | tf_op jit(solution)/shard_map/ppermute | solution.py:386
  14.7 27.7 %collective-permute-start.7 = (bf16[20,4,8,256]{3,2,1,0:T(8,128)(2,1)S(1)}, bf16[20,4,8,256]{3,2,1,0:T(8,128)(2,1)S(1)}, u32[]{:S(2)}, u32[]{:S(2)}) collective-permute-start(bf16[20,4,8,256]{3,2,1,0:T(8,128)(2,1)S(1)} %shard_map.105.refs_5_.refs_6_.refs_4_), channel_id=1, source_target_pairs={{0,255},{1,254},{2,253},{3,252},{4,8},{5,9},{6,10},{7,11},{8,4},{9... | collective-permute-start | bytes 983048 | tf_op jit(solution)/shard_map/ppermute | solution.py:383
  19.1 23.3 %collective-permute-start.6 = (bf16[20,4,8,256]{3,2,1,0:T(8,128)(2,1)S(1)}, bf16[20,4,8,256]{3,2,1,0:T(8,128)(2,1)S(1)}, u32[]{:S(2)}, u32[]{:S(2)}) collective-permute-start(bf16[20,4,8,256]{3,2,1,0:T(8,128)(2,1)S(1)} %shard_map.105.refs_5_.refs_6_.refs_4_), channel_id=1, source_target_pairs={{0,4},{4,0},{8,12},{12,8},{16,20},{20,16},{24,28},{28,24},{32,36},... | collective-permute-start | bytes 983048 | tf_op jit(solution)/shard_map/ppermute | solution.py:380
  19.9 11.5 %collective-permute-start = (bf16[23,8,256]{2,1,0:T(8,128)(2,1)S(1)}, bf16[23,8,256]{2,1,0:T(8,128)(2,1)S(1)}, u32[]{:S(2)}, u32[]{:S(2)}) collective-permute-start(bf16[23,8,256]{2,1,0:T(8,128)(2,1)S(1)} %get-tuple-element.35), channel_id=1, source_target_pairs={{0,1},{1,0},{2,3},{3,2},{4,5},{5,4},{6,7},{7,6},{8,9},{9,8},{10,11... | collective-permute-start | bytes 282632 | tf_op jit(solution)/shard_map/ppermute | solution.py:386
  23.3 8.2 %collective-permute-start.1 = (bf16[23,8,256]{2,1,0:T(8,128)(2,1)S(1)}, bf16[23,8,256]{2,1,0:T(8,128)(2,1)S(1)}, u32[]{:S(2)}, u32[]{:S(2)}) collective-permute-start(bf16[23,8,256]{2,1,0:T(8,128)(2,1)S(1)} %get-tuple-element.36), channel_id=1, source_target_pairs={{0,2},{1,3},{2,0},{3,1},{4,6},{5,7},{6,4},{7,5},{8,10},{9,11},{10,... | collective-permute-start | bytes 282632 | tf_op jit(solution)/shard_map/ppermute | solution.py:386
  24.8 13.1 %collective-permute-start.8 = (bf16[352,256]{1,0:T(8,128)(2,1)S(1)}, bf16[352,256]{1,0:T(8,128)(2,1)S(1)}, u32[]{:S(2)}, u32[]{:S(2)}) collective-permute-start(bf16[352,256]{1,0:T(8,128)(2,1)S(1)} %get-tuple-element.43), channel_id=1, source_target_pairs={{0,4},{4,0},{8,12},{12,8},{16,20},{20,16},{24,28},{28,24},{32,36},... | collective-permute-start | bytes 540680 | tf_op jit(solution)/shard_map/ppermute | solution.py:380
  31.5 10.9 %collective-permute-start.9 = (bf16[352,256]{1,0:T(8,128)(2,1)S(1)}, bf16[352,256]{1,0:T(8,128)(2,1)S(1)}, u32[]{:S(2)}, u32[]{:S(2)}) collective-permute-start(bf16[352,256]{1,0:T(8,128)(2,1)S(1)} %get-tuple-element.44), channel_id=1, source_target_pairs={{0,255},{1,254},{2,253},{3,252},{4,8},{5,9},{6,10},{7,11},{8,4},{9... | collective-permute-start | bytes 540680 | tf_op jit(solution)/shard_map/ppermute | solution.py:383
  31.5 6.5 %collective-permute-start.2 = (bf16[23,8,256]{2,1,0:T(8,128)(2,1)S(1)}, bf16[23,8,256]{2,1,0:T(8,128)(2,1)S(1)}, u32[]{:S(2)}, u32[]{:S(2)}) collective-permute-start(bf16[23,8,256]{2,1,0:T(8,128)(2,1)S(1)} %get-tuple-element.37), channel_id=1, source_target_pairs={{0,3},{1,2},{2,1},{3,0},{4,7},{5,6},{6,5},{7,4},{8,11},{9,10},{10,... | collective-permute-start | bytes 282632 | tf_op jit(solution)/shard_map/ppermute | solution.py:386
  46.8 8.0 %collective-permute-start.11 = (f32[32,256]{1,0:T(8,128)S(1)}, f32[32,256]{1,0:T(8,128)S(1)}, u32[]{:S(2)}, u32[]{:S(2)}) collective-permute-start(f32[32,256]{1,0:T(8,128)S(1)} %pad_maximum_fusion.1), channel_id=1, source_target_pairs={{0,255},{1,254},{2,253},{3,252},{4,8},{5,9},{6,10},{7,11},{8,4},{9... | collective-permute-start | bytes 98312 | tf_op jit(solution)/shard_map/ppermute | solution.py:383
  58.7 4.8 %collective-permute-start.13 = (f32[32,256]{1,0:T(8,128)S(1)}, f32[32,256]{1,0:T(8,128)S(1)}, u32[]{:S(2)}, u32[]{:S(2)}) collective-permute-start(f32[32,256]{1,0:T(8,128)S(1)} %add.46), channel_id=1, source_target_pairs={{0,2},{1,3},{2,0},{3,1},{4,6},{5,7},{6,4},{7,5},{8,10},{9,11},{10,... | collective-permute-start | bytes 98312 | tf_op jit(solution)/shard_map/ppermute | solution.py:449
  71.5 7.8 %collective-permute-start.19 = (f32[32,256]{1,0:T(8,128)S(1)}, f32[32,256]{1,0:T(8,128)S(1)}, u32[]{:S(2)}, u32[]{:S(2)}) collective-permute-start(f32[32,256]{1,0:T(8,128)S(1)} %pad_maximum_fusion.2), channel_id=1, source_target_pairs={{0,255},{1,254},{2,253},{3,252},{4,8},{5,9},{6,10},{7,11},{8,4},{9... | collective-permute-start | bytes 98312 | tf_op jit(solution)/shard_map/ppermute | solution.py:383
  79.4 5.1 %collective-permute-start.20 = (f32[40,256]{1,0:T(8,128)S(1)}, f32[40,256]{1,0:T(8,128)S(1)}, u32[]{:S(2)}, u32[]{:S(2)}) collective-permute-start(f32[40,256]{1,0:T(8,128)S(1)} %pad_maximum_fusion), channel_id=1, source_target_pairs={{0,1},{1,0},{2,3},{3,2},{4,5},{5,4},{6,7},{7,6},{8,9},{9,8},{10,11... | collective-permute-start | bytes 122888 | tf_op jit(solution)/shard_map/ppermute | solution.py:448
  84.5 4.9 %collective-permute-start.21 = (f32[40,256]{1,0:T(8,128)S(1)}, f32[40,256]{1,0:T(8,128)S(1)}, u32[]{:S(2)}, u32[]{:S(2)}) collective-permute-start(f32[40,256]{1,0:T(8,128)S(1)} %fusion), channel_id=1, source_target_pairs={{0,2},{1,3},{2,0},{3,1},{4,6},{5,7},{6,4},{7,5},{8,10},{9,11},{10,... | collective-permute-start | bytes 122888 | tf_op jit(solution)/shard_map/ppermute | solution.py:449
  87.3 30.2 %collective-permute-start.15 = (bf16[20,8,256]{2,1,0:T(8,128)(2,1)S(1)}, bf16[20,8,256]{2,1,0:T(8,128)(2,1)S(1)}, u32[]{:S(2)}, u32[]{:S(2)}) collective-permute-start(bf16[20,8,256]{2,1,0:T(8,128)(2,1)S(1)} %get-tuple-element.54), channel_id=1, source_target_pairs={{0,1},{1,0},{2,3},{3,2},{4,5},{5,4},{6,7},{7,6},{8,9},{9,8},{10,11... | collective-permute-start | bytes 245768 | tf_op jit(solution)/shard_map/ppermute | solution.py:386
  94.4 4.9 %collective-permute-start.27 = (f32[8,256]{1,0:T(8,128)S(1)}, f32[8,256]{1,0:T(8,128)S(1)}, u32[]{:S(2)}, u32[]{:S(2)}) collective-permute-start(f32[8,256]{1,0:T(8,128)S(1)} %add.53), channel_id=1, source_target_pairs={{0,24},{4,28},{8,16},{12,20},{16,8},{20,12},{24,0},{28,4},{32,56},... | collective-permute-start | bytes 24584 | tf_op jit(solution)/shard_map/ppermute | solution.py:485
  99.3 4.9 %collective-permute-start.28 = (f32[8,256]{1,0:T(8,128)S(1)}, f32[8,256]{1,0:T(8,128)S(1)}, u32[]{:S(2)}, u32[]{:S(2)}) collective-permute-start(f32[8,256]{1,0:T(8,128)S(1)} %add.54), channel_id=1, source_target_pairs={{0,35},{1,34},{2,33},{3,32},{4,39},{5,38},{6,37},{7,36},{8,43},{9,... | collective-permute-start | bytes 24584 | tf_op jit(solution)/shard_map/ppermute | solution.py:486
  99.3 20.6 %collective-permute-start.16 = (bf16[20,8,256]{2,1,0:T(8,128)(2,1)S(1)}, bf16[20,8,256]{2,1,0:T(8,128)(2,1)S(1)}, u32[]{:S(2)}, u32[]{:S(2)}) collective-permute-start(bf16[20,8,256]{2,1,0:T(8,128)(2,1)S(1)} %get-tuple-element.55), channel_id=1, source_target_pairs={{0,2},{1,3},{2,0},{3,1},{4,6},{5,7},{6,4},{7,5},{8,10},{9,11},{10,... | collective-permute-start | bytes 245768 | tf_op jit(solution)/shard_map/ppermute | solution.py:386
  102.1 17.8 %collective-permute-start.17 = (bf16[20,8,256]{2,1,0:T(8,128)(2,1)S(1)}, bf16[20,8,256]{2,1,0:T(8,128)(2,1)S(1)}, u32[]{:S(2)}, u32[]{:S(2)}) collective-permute-start(bf16[20,8,256]{2,1,0:T(8,128)(2,1)S(1)} %get-tuple-element.56), channel_id=1, source_target_pairs={{0,3},{1,2},{2,1},{3,0},{4,7},{5,6},{6,5},{7,4},{8,11},{9,10},{10,... | collective-permute-start | bytes 245768 | tf_op jit(solution)/shard_map/ppermute | solution.py:386
  104.2 14.0 %collective-permute-start.29 = (f32[8,256]{1,0:T(8,128)S(1)}, f32[8,256]{1,0:T(8,128)S(1)}, u32[]{:S(2)}, u32[]{:S(2)}) collective-permute-start(f32[8,256]{1,0:T(8,128)S(1)} %add.55), channel_id=1, source_target_pairs={{0,64},{4,68},{8,72},{12,76},{16,80},{20,84},{24,88},{28,92},{32,9... | collective-permute-start | bytes 24584 | tf_op jit(solution)/shard_map/ppermute | solution.py:488
  113.4 10.2 %collective-permute-start.23 = (bf16[20,8,256]{2,1,0:T(8,128)(2,1)S(1)}, bf16[20,8,256]{2,1,0:T(8,128)(2,1)S(1)}, u32[]{:S(2)}, u32[]{:S(2)}) collective-permute-start(bf16[20,8,256]{2,1,0:T(8,128)(2,1)S(1)} %get-tuple-element.60), channel_id=1, source_target_pairs={{0,1},{1,0},{2,3},{3,2},{4,5},{5,4},{6,7},{7,6},{8,9},{9,8},{10,11... | collective-permute-start | bytes 245768 | tf_op jit(solution)/shard_map/ppermute | solution.py:386
  117.4 6.2 %collective-permute-start.24 = (bf16[20,8,256]{2,1,0:T(8,128)(2,1)S(1)}, bf16[20,8,256]{2,1,0:T(8,128)(2,1)S(1)}, u32[]{:S(2)}, u32[]{:S(2)}) collective-permute-start(bf16[20,8,256]{2,1,0:T(8,128)(2,1)S(1)} %get-tuple-element.61), channel_id=1, source_target_pairs={{0,2},{1,3},{2,0},{3,1},{4,6},{5,7},{6,4},{7,5},{8,10},{9,11},{10,... | collective-permute-start | bytes 245768 | tf_op jit(solution)/shard_map/ppermute | solution.py:386
  118.2 6.3 %collective-permute-start.25 = (bf16[20,8,256]{2,1,0:T(8,128)(2,1)S(1)}, bf16[20,8,256]{2,1,0:T(8,128)(2,1)S(1)}, u32[]{:S(2)}, u32[]{:S(2)}) collective-permute-start(bf16[20,8,256]{2,1,0:T(8,128)(2,1)S(1)} %get-tuple-element.62), channel_id=1, source_target_pairs={{0,3},{1,2},{2,1},{3,0},{4,7},{5,6},{6,5},{7,4},{8,11},{9,10},{10,... | collective-permute-start | bytes 245768 | tf_op jit(solution)/shard_map/ppermute | solution.py:386
  (16 other events, 65.9 us)

commit v2 on v1

--- a/solution.py
+++ b/solution.py
@@ -6,6 +6,7 @@
 from jax.experimental import pallas as pl
 from jax.experimental.pallas import tpu as pltpu
 from jax.sharding import PartitionSpec as P
+
 
 HV = 4
 NS = 2 * HV + 1
@@ -16,15 +17,18 @@
 SM = pl.BlockSpec(memory_space=pltpu.SMEM)
 
 
-def call(body, outs, args, scalars, scratch=(), flops=0):
-    specs = [SM] * scalars + [VM] * (len(args) - scalars)
+def call(body, outs, args, scalars, scratch=(), flops=0, specs=None, out_specs=None):
+    if specs is None:
+        specs = [SM] * scalars + [VM] * (len(args) - scalars)
+    if out_specs is None:
+        out_specs = tuple(VM for _ in outs)
     moved = sum(a.size * a.dtype.itemsize for a in args)
     moved += sum(math.prod(o.shape) * jnp.dtype(o.dtype).itemsize for o in outs)
     return pl.pallas_call(
         body,
         out_shape=tuple(outs),
         in_specs=specs,
-        out_specs=tuple(VM for _ in outs),
+        out_specs=out_specs,
         scratch_shapes=list(scratch),
         cost_estimate=pl.CostEstimate(flops=flops, bytes_accessed=moved, transcendentals=0),
         compiler_params=pltpu.CompilerParams(vmem_limit_bytes=48 * 1024 * 1024),
@@ -47,10 +51,19 @@
     return (hi.astype(F32) + mid.astype(F32)) + lo.astype(F32)
 
 
-def pack_ens_kernel(scal, ens, *outs):
+def pack_ens_kernel(scal, ens, *refs):
+    outs, sems = refs[:4], refs[4]
     share = outs[0].shape[0]
-    for k in range(4):
-        outs[k][...] = ens[pl.ds(share * (scal[2] ^ k), share)]
+    copies = [
+        pltpu.make_async_copy(
+            ens.at[pl.ds(share * (scal[2] ^ k), share)], outs[k], sems.at[k]
+        )
+        for k in range(4)
+    ]
+    for c in copies:
+        c.start()
+    for c in copies:
+        c.wait()
 
 
 def pack_ctl_kernel(scal, ctl, wt, *outs):
@@ -311,26 +324,27 @@
         out[at] = ctl[at] + a[...].astype(F32)
 
 
-def grad_second_kernel(count, scal, g1, a0, a1, a2, a3, sums, out, costs):
+def grad_second_kernel(
+    count, scal, ctl, a0, a1, a2, a3, b0, b1, b2, b3, sums, out, costs
+):
     tot = jnp.sum(sums[...], axis=1, keepdims=True)
     cc, gg, cg = tot[0:1], tot[1:2], tot[2:3]
     dd, qd, rd = tot[3:4], tot[4:5], tot[5:6]
     tau = STEP / jnp.sqrt(gg / count + 1e-06)
-    first = 0.5 * cc + 0.5 * dd
+    first = (0.5 * cc + 0.5 * dd) / count
     second = 0.5 * (cc - 2.0 * tau * cg + tau * tau * gg) + 0.5 * (
         dd - 2.0 * tau * qd + tau * tau * rd
     )
-    costs[0:1, :] = jnp.broadcast_to(first / count, (1, 128))
-    costs[1:2, :] = jnp.broadcast_to(second / count, (1, 128))
-    costs[2:8, :] = jnp.zeros((6, 128), F32)
+    costs[0] = first[0, 0]
+    costs[1] = (second / count)[0, 0]
     tb = jnp.broadcast_to(tau, (8, 256))
     share = a0.shape[0]
-    for k, a in enumerate((a0, a1, a2, a3)):
-
-        def body(m, _, a=a, k=k):
+    for k, (a, b) in enumerate(zip((a0, a1, a2, a3), (b0, b1, b2, b3))):
+
+        def body(m, _, a=a, b=b, k=k):
             at = share * (scal[2] ^ k) + m
-            g = g1[at]
-            out[at] = g - tb * (g + a[m].astype(F32))
+            g = ctl[at] + a[m].astype(F32)
+            out[at] = g - tb * (g + b[m].astype(F32))
             return 0
 
         lax.fori_loop(0, share, body, 0, unroll=4)
@@ -347,8 +361,8 @@
     for t in range(tiles):
         e = (t + 1) % tiles if t & 1 else (t - 1) % tiles
         for g in range(levs):
-            edge.append((flat(t, g), flat(e, g if zh(t) == zh(e) else levs - 1 - g)))
-    far = [(flat(t, g), flat(t ^ 8, levs - 1 - g)) for t in range(tiles) for g in range(levs)]
+            edge.append((flat(t, g), flat(e, g if zh(t) == zh(e) else g ^ 2)))
+    far = [(flat(t, g), flat(t ^ 8, g ^ 2)) for t in range(tiles) for g in range(levs)]
 
     def tile_xor(k):
         return [(t, t ^ k) for t in range(tiles)]
@@ -373,7 +387,7 @@
     both = ("tile", "lev")
     tile_pos = lax.axis_index("tile").astype(jnp.int32)
     lev_pos = lax.axis_index("lev").astype(jnp.int32)
-    mset = lev_pos ^ (3 * ((tile_pos >> 3) & 1))
+    mset = lev_pos ^ (2 * ((tile_pos >> 3) & 1))
     scal = jnp.stack([tile_pos, lev_pos, mset, mset])
 
     def swap_core(x):
@@ -383,10 +397,22 @@
         return lax.ppermute(x, both, edge)
 
     def shuffle(parts):
-        return [parts[0]] + [lax.ppermute(parts[k], "lev", lev_xor(k)) for k in range(1, 4)]
+        return [parts[0]] + [
+            lax.ppermute(parts[k], "lev", lev_xor(k)) for k in range(1, 4)
+        ]
+
+    def sum4(x, axis, pairs, steps):
+        one, two, three = (
+            lax.ppermute(x, axis, pairs(k)) for k in steps
+        )
+        return (x + one) + (two + three)
 
     chunk = sds((share, ldev, pdev), BF16)
-    eparts = call(pack_ens_kernel, [chunk] * 4, (scal, ensemble), 1)
+    eparts = call(
+        pack_ens_kernel, [chunk] * 4, (scal, ensemble), 1,
+        [pltpu.SemaphoreType.DMA((4,))],
+        specs=[SM, pl.BlockSpec(memory_space=pltpu.HBM)],
+    )
     eparts = shuffle(eparts)
     d_own, x_core, x_edge, vw, vwt = call(
         densify_kernel,
@@ -444,9 +470,9 @@
         other = swap_edge(mine)
         tot = mine + jnp.concatenate([other[obs:], other[:obs]], axis=0)
         if core_msg.shape[0] > obs:
-            tot = jnp.concatenate([tot, core_msg[obs:] + got[obs:]], axis=0)
-        tot = tot + lax.ppermute(tot, "lev", lev_xor(1))
-        tot = tot + lax.ppermute(tot, "lev", lev_xor(2))
+            extra = core_msg[obs:] + got[obs:]
+            tot = jnp.concatenate([tot, extra], axis=0)
+        tot = sum4(tot, "lev", lev_xor, (1, 2, 3))
         return tot, swap_core(tot[:obs])
 
     h1_oe, h1_core = reduce_obs(hx_core, hx_oe)
@@ -461,6 +487,7 @@
         [full, half, umat],
         2 * mm,
     )
+    aparts = shuffle(outs[:4])
     hs, hd_core = reduce_obs(outs[4], outs[5])
     sums = call(
         sums_kernel,
@@ -468,7 +495,6 @@
         (hs, hd_core, h1_oe, h1_core, inv_error, innovation, x_core),
         0,
     )[0]
-    aparts = shuffle(outs[:4])
     bparts = call(
         bind(third_kernel, norm),
         [chunk] * 4,
@@ -481,21 +507,20 @@
         mm,
     )
     bparts = shuffle(bparts)
-    for k in (2, 6):
-        sums = sums + lax.ppermute(sums, "tile", tile_xor(k))
+    sums = sum4(sums, "tile", tile_xor, (2, 4, 6))
     sums = sums + lax.ppermute(sums, both, far)
-    for k in (16, 48):
-        sums = sums + lax.ppermute(sums, "tile", tile_xor(k))
+    sums = sum4(sums, "tile", tile_xor, (16, 32, 48))
     whole = sds((members, ldev, pdev), F32)
     (grad_first,) = call(grad_first_kernel, [whole], (scal, control, *aparts), 1)
     count = float(members * lev * pdev * tiles)
     grad_second, costs = call(
         bind(grad_second_kernel, count),
-        [whole, sds((8, 128), F32)],
-        (scal, grad_first, *bparts, sums),
+        [whole, sds((2,), F32)],
+        (scal, control, *aparts, *bparts, sums),
         1,
-    )
-    return grad_first, grad_second, costs[0:2, 0]
+        out_specs=(VM, SM),
+    )
+    return grad_first, grad_second, costs
 
 
 def solution(mesh):

time: 128 us -> 125 us (0.977)
  waiting for transfers between devices: 63 us -> 56.2 us
  starting transfers between devices: 43.8 us -> 48.2 us
  local copies, waits for them, and re-layouts: 2.89 us -> 1.16 us
    ppermute x8 -> x12, waiting for transfers between devices: 20.4 us -> 7.04 us  [sum4(): one, two, three = (lax.ppermute(x, axis, pairs(k)) for k in steps)]
    ppermute x12, waiting for transfers between devices: 17.9 us -> 26.6 us  [shuffle(): lax.ppermute(parts[k], 'lev', lev_xor(k))]
    ppermute x8 -> x12, starting transfers between devices: 15.6 us -> 21.6 us  [sum4(): one, two, three = (lax.ppermute(x, axis, pairs(k)) for k in steps)]
    ppermute x12, starting transfers between devices: 22.4 us -> 18.6 us  [shuffle(): lax.ppermute(parts[k], 'lev', lev_xor(k))]
    ppermute x4, starting transfers between devices: 5.09 us -> 7.32 us  [swap_edge(): return lax.ppermute(x, both, edge)]
    ppermute x4, waiting for transfers between devices: 19.6 us -> 18.1 us  [swap_edge(): return lax.ppermute(x, both, edge)]
  transfers between devices with their start and end apart: 31 -> 35, of which waited for: 20 -> 22; matrix products, arithmetic and copies ran while one was open for 0% -> 0% of each run, Pallas kernels for 5% -> 5%
where the time goes in v2:
time: 125 us
  waiting for transfers between devices  56.2 us (45%)
  starting transfers between devices  48.2 us (39%)
  Pallas kernels  17.8 us (14%)
    ppermute x12, waiting for transfers between devices, shuffle(): lax.ppermute(parts[k], 'lev', lev_xor(k))  26.6 us
    ppermute x12, starting transfers between devices, sum4(): one, two, three = (lax.ppermute(x, axis, pairs(k)) for k in steps)  21.6 us
    ppermute x12, starting transfers between devices, shuffle(): lax.ppermute(parts[k], 'lev', lev_xor(k))  18.6 us
    ppermute x4, waiting for transfers between devices, swap_edge(): return lax.ppermute(x, both, edge)  18.1 us
    pallas_call x10, Pallas kernels, call(): pl.pallas_call(body, out_shape=tuple(outs), in_specs=specs, out_specs=out...  17.8 us
    ppermute x4, starting transfers between devices, swap_edge(): return lax.ppermute(x, both, edge)  7.32 us
    ppermute x12, waiting for transfers between devices, sum4(): one, two, three = (lax.ppermute(x, axis, pairs(k)) for k in steps)  7.04 us
    ppermute x6, waiting for transfers between devices, swap_core(): return lax.ppermute(x, 'tile', tile_xor(1))  4.58 us
  transfers between devices with their start and end apart: 35, of which 22 were waited for; matrix products, arithmetic and copies ran while one was open for 0% of the time, Pallas kernels for 5%

profile of v2, /device:TPU:2, one launch (start us, length us, event | category | flops | bytes accessed | tf_op | source)
XLA Modules:
  0.0 124.6 jit_solution(7465124979774788347)
XLA Ops:
  2.8 2.0 %collective-permute-start.3 = (bf16[20,8,256]{2,1,0:T(8,128)(2,1)S(1)}, bf16[20,8,256]{2,1,0:T(8,128)(2,1)S(1)}, u32[]{:S(2)}, u32[]{:S(2)}) collective-permute-start(bf16[20,8,256]{2,1,0:T(8,128)(2,1)S(1)} %get-tuple-element.39), channel_id=1, source_target_pairs={{0,1},{1,0},{2,3},{3,2},{4,5},{5,4},{6,7},{7,6},{8,9},{9,8},{10,11... | collective-permute-start | bytes 245768 | tf_op jit(solution)/shard_map/ppermute | solution.py:401
  4.8 3.3 %collective-permute-start.4 = (bf16[20,8,256]{2,1,0:T(8,128)(2,1)S(1)}, bf16[20,8,256]{2,1,0:T(8,128)(2,1)S(1)}, u32[]{:S(2)}, u32[]{:S(2)}) collective-permute-start(bf16[20,8,256]{2,1,0:T(8,128)(2,1)S(1)} %get-tuple-element.40), channel_id=1, source_target_pairs={{0,2},{1,3},{2,0},{3,1},{4,6},{5,7},{6,4},{7,5},{8,10},{9,11},{10,... | collective-permute-start | bytes 245768 | tf_op jit(solution)/shard_map/ppermute | solution.py:401
  8.0 6.5 %collective-permute-done.4.e2 = bf16[20,8,256]{2,1,0:T(8,128)(2,1)S(1)} collective-permute-done((bf16[20,8,256]{2,1,0:T(8,128)(2,1)S(1)}, bf16[20,8,256]{2,1,0:T(8,128)(2,1)S(1)}, u32[]{:S(2)}, u32[]{:S(2)}) %collective-permute-start.4) | collective-permute-done | bytes 81952 | tf_op jit(solution)/shard_map/ppermute | solution.py:401
  15.1 6.2 %collective-permute-start.7 = (bf16[20,4,8,256]{3,2,1,0:T(8,128)(2,1)S(1)}, bf16[20,4,8,256]{3,2,1,0:T(8,128)(2,1)S(1)}, u32[]{:S(2)}, u32[]{:S(2)}) collective-permute-start(bf16[20,4,8,256]{3,2,1,0:T(8,128)(2,1)S(1)} %shard_map.105.refs_5_.refs_6_.refs_4_), channel_id=1, source_target_pairs={{0,254},{1,255},{2,252},{3,253},{4,8},{5,9},{6,10},{7,11},{8,4},{9... | collective-permute-start | bytes 983048 | tf_op jit(solution)/shard_map/ppermute | solution.py:397
  22.3 2.5 %collective-permute-start.1 = (bf16[23,8,256]{2,1,0:T(8,128)(2,1)S(1)}, bf16[23,8,256]{2,1,0:T(8,128)(2,1)S(1)}, u32[]{:S(2)}, u32[]{:S(2)}) collective-permute-start(bf16[23,8,256]{2,1,0:T(8,128)(2,1)S(1)} %get-tuple-element.36), channel_id=1, source_target_pairs={{0,2},{1,3},{2,0},{3,1},{4,6},{5,7},{6,4},{7,5},{8,10},{9,11},{10,... | collective-permute-start | bytes 282632 | tf_op jit(solution)/shard_map/ppermute | solution.py:401
  25.8 4.4 %collective-permute-done.refs_2_ = bf16[23,8,256]{2,1,0:T(8,128)(2,1)S(1)} collective-permute-done((bf16[23,8,256]{2,1,0:T(8,128)(2,1)S(1)}, bf16[23,8,256]{2,1,0:T(8,128)(2,1)S(1)}, u32[]{:S(2)}, u32[]{:S(2)}) %collective-permute-start) | collective-permute-done | bytes 94240 | tf_op jit(solution)/shard_map/ppermute | solution.py:401
  30.6 1.9 %collective-permute-start.2 = (bf16[23,8,256]{2,1,0:T(8,128)(2,1)S(1)}, bf16[23,8,256]{2,1,0:T(8,128)(2,1)S(1)}, u32[]{:S(2)}, u32[]{:S(2)}) collective-permute-start(bf16[23,8,256]{2,1,0:T(8,128)(2,1)S(1)} %get-tuple-element.37), channel_id=1, source_target_pairs={{0,3},{1,2},{2,1},{3,0},{4,7},{5,6},{6,5},{7,4},{8,11},{9,10},{10,... | collective-permute-start | bytes 282632 | tf_op jit(solution)/shard_map/ppermute | solution.py:401
  32.5 6.3 %collective-permute-done.2.refs_4_ = bf16[23,8,256]{2,1,0:T(8,128)(2,1)S(1)} collective-permute-done((bf16[23,8,256]{2,1,0:T(8,128)(2,1)S(1)}, bf16[23,8,256]{2,1,0:T(8,128)(2,1)S(1)}, u32[]{:S(2)}, u32[]{:S(2)}) %collective-permute-start.2) | collective-permute-done | bytes 94240 | tf_op jit(solution)/shard_map/ppermute | solution.py:401
  38.8 1.9 %collective-permute-done.9.refs_10_.refs_11_.refs_9_ = bf16[352,256]{1,0:T(8,128)(2,1)S(1)} collective-permute-done((bf16[352,256]{1,0:T(8,128)(2,1)S(1)}, bf16[352,256]{1,0:T(8,128)(2,1)S(1)}, u32[]{:S(2)}, u32[]{:S(2)}) %collective-permute-start.9) | collective-permute-done | bytes 180256 | tf_op jit(solution)/shard_map/ppermute | solution.py:397
  40.7 3.1 %shard_map.107 = (bf16[20,4,8,256]{3,2,1,0:T(8,128)(2,1)S(1)}, f32[16,256]{1,0:T(8,128)S(1)}, f32[32,256]{1,0:T(8,128)S(1)}, f32[16,128]{1,0:T(8,128)S(1)}, f32[32,128]{1,0:T(8,128)S(1)}) custom-call(s32[4]{0:T(128)S(1)} %pad_add_fusion.scal.refs_0_, bf16[23,8,256]{2,1,0:T(8,128)(2,1)S(1)} %get-tuple-element.34.refs_1_, ...), custom_call_target="tpu_custom_call" | custom-call | flops 251658240 | bytes 2400272 | tf_op jit(solution)/shard_map/pallas_call | solution.py:27
  46.0 7.6 %collective-permute-done.11 = f32[32,256]{1,0:T(8,128)S(1)} collective-permute-done((f32[32,256]{1,0:T(8,128)S(1)}, f32[32,256]{1,0:T(8,128)S(1)}, u32[]{:S(2)}, u32[]{:S(2)}) %collective-permute-start.11) | collective-permute-done | bytes 32800 | tf_op jit(solution)/shard_map/ppermute | solution.py:397
  53.6 2.0 %collective-permute-start.14 = (f32[32,256]{1,0:T(8,128)S(1)}, f32[32,256]{1,0:T(8,128)S(1)}, u32[]{:S(2)}, u32[]{:S(2)}) collective-permute-start(f32[32,256]{1,0:T(8,128)S(1)} %maximum_add_fusion), channel_id=1, source_target_pairs={{0,3},{1,2},{2,1},{3,0},{4,7},{5,6},{6,5},{7,4},{8,11},{9,10},{10,... | collective-permute-start | bytes 98312 | tf_op jit(solution)/shard_map/ppermute | solution.py:406
  55.6 2.0 %collective-permute-start.13 = (f32[32,256]{1,0:T(8,128)S(1)}, f32[32,256]{1,0:T(8,128)S(1)}, u32[]{:S(2)}, u32[]{:S(2)}) collective-permute-start(f32[32,256]{1,0:T(8,128)S(1)} %maximum_add_fusion), channel_id=1, source_target_pairs={{0,2},{1,3},{2,0},{3,1},{4,6},{5,7},{6,4},{7,5},{8,10},{9,11},{10,... | collective-permute-start | bytes 98312 | tf_op jit(solution)/shard_map/ppermute | solution.py:406
  62.8 5.5 %shard_map.108 = (bf16[20,8,256]{2,1,0:T(8,128)(2,1)S(1)}, bf16[20,8,256]{2,1,0:T(8,128)(2,1)S(1)}, bf16[20,8,256]{2,1,0:T(8,128)(2,1)S(1)}, bf16[20,8,256]{2,1,...) custom-call(s32[4]{0:T(128)S(1)} %pad_add_fusion.scal.refs_0_, ...), custom_call_target="tpu_custom_call" | custom-call | flops 503316480 | bytes 2596880 | tf_op jit(solution)/shard_map/pallas_call | solution.py:27
  69.8 8.5 %collective-permute-done.20 = f32[32,256]{1,0:T(8,128)S(1)} collective-permute-done((f32[32,256]{1,0:T(8,128)S(1)}, f32[32,256]{1,0:T(8,128)S(1)}, u32[]{:S(2)}, u32[]{:S(2)}) %collective-permute-start.20) | collective-permute-done | bytes 32800 | tf_op jit(solution)/shard_map/ppermute | solution.py:397
  79.3 1.9 %collective-permute-start.23 = (f32[40,256]{1,0:T(8,128)S(1)}, f32[40,256]{1,0:T(8,128)S(1)}, u32[]{:S(2)}, u32[]{:S(2)}) collective-permute-start(f32[40,256]{1,0:T(8,128)S(1)} %pad_maximum_fusion), channel_id=1, source_target_pairs={{0,3},{1,2},{2,1},{3,0},{4,7},{5,6},{6,5},{7,4},{8,11},{9,10},{10,... | collective-permute-start | bytes 122888 | tf_op jit(solution)/shard_map/ppermute | solution.py:406
  87.1 4.0 %collective-permute-start.28 = (f32[8,256]{1,0:T(8,128)S(1)}, f32[8,256]{1,0:T(8,128)S(1)}, u32[]{:S(2)}, u32[]{:S(2)}) collective-permute-start(f32[8,256]{1,0:T(8,128)S(1)} %shard_map.111), channel_id=1, source_target_pairs={{0,8},{4,12},{8,0},{12,4},{16,24},{20,28},{24,16},{28,20},{32,40},... | collective-permute-start | bytes 24584 | tf_op jit(solution)/shard_map/ppermute | solution.py:406
  91.5 2.1 %collective-permute-start.17 = (bf16[20,8,256]{2,1,0:T(8,128)(2,1)S(1)}, bf16[20,8,256]{2,1,0:T(8,128)(2,1)S(1)}, u32[]{:S(2)}, u32[]{:S(2)}) collective-permute-start(bf16[20,8,256]{2,1,0:T(8,128)(2,1)S(1)} %get-tuple-element.55), channel_id=1, source_target_pairs={{0,2},{1,3},{2,0},{3,1},{4,6},{5,7},{6,4},{7,5},{8,10},{9,11},{10,... | collective-permute-start | bytes 245768 | tf_op jit(solution)/shard_map/ppermute | solution.py:401
  93.5 1.9 %collective-permute-start.18 = (bf16[20,8,256]{2,1,0:T(8,128)(2,1)S(1)}, bf16[20,8,256]{2,1,0:T(8,128)(2,1)S(1)}, u32[]{:S(2)}, u32[]{:S(2)}) collective-permute-start(bf16[20,8,256]{2,1,0:T(8,128)(2,1)S(1)} %get-tuple-element.56), channel_id=1, source_target_pairs={{0,3},{1,2},{2,1},{3,0},{4,7},{5,6},{6,5},{7,4},{8,11},{9,10},{10,... | collective-permute-start | bytes 245768 | tf_op jit(solution)/shard_map/ppermute | solution.py:401
  95.8 4.3 %collective-permute-done.17.a2.refs_4_ = bf16[20,8,256]{2,1,0:T(8,128)(2,1)S(1)} collective-permute-done((bf16[20,8,256]{2,1,0:T(8,128)(2,1)S(1)}, bf16[20,8,256]{2,1,0:T(8,128)(2,1)S(1)}, u32[]{:S(2)}, u32[]{:S(2)}) %collective-permute-start.17) | collective-permute-done | bytes 81952 | tf_op jit(solution)/shard_map/ppermute | solution.py:401
  103.1 7.8 %collective-permute-start.33 = (f32[8,256]{1,0:T(8,128)S(1)}, f32[8,256]{1,0:T(8,128)S(1)}, u32[]{:S(2)}, u32[]{:S(2)}) collective-permute-start(f32[8,256]{1,0:T(8,128)S(1)} %add.70), channel_id=1, source_target_pairs={{0,128},{4,132},{8,136},{12,140},{16,144},{20,148},{24,152},{28,15... | collective-permute-start | bytes 24584 | tf_op jit(solution)/shard_map/ppermute | solution.py:406
  110.9 2.8 %shard_map.110 = (bf16[20,8,256]{2,1,0:T(8,128)(2,1)S(1)}, bf16[20,8,256]{2,1,0:T(8,128)(2,1)S(1)}, bf16[20,8,256]{2,1,0:T(8,128)(2,1)S(1)}, bf16[20,8,256]{2,1,0:T(8,128)(2,1)S(1)}) custom-call(s32[4]{0:T(128)S(1)} %pad_add_fusion.scal.refs_0_, f32[40,256]{1,0:T(8,128)S(1)} %add_add_fusion.refs_1_.hs, f32[16,256]{1,0:T(8,128)S(1)} %collective-permute-done.24.refs_2_.h_core, ...), custom_call_target="tpu_custom_call" | custom-call | flops 251658240 | bytes 2039824 | tf_op jit(solution)/shard_map/pallas_call | solution.py:27
  116.3 1.9 %collective-permute-start.27 = (bf16[20,8,256]{2,1,0:T(8,128)(2,1)S(1)}, bf16[20,8,256]{2,1,0:T(8,128)(2,1)S(1)}, u32[]{:S(2)}, u32[]{:S(2)}) collective-permute-start(bf16[20,8,256]{2,1,0:T(8,128)(2,1)S(1)} %get-tuple-element.62), channel_id=1, source_target_pairs={{0,3},{1,2},{2,1},{3,0},{4,7},{5,6},{6,5},{7,4},{8,11},{9,10},{10,... | collective-permute-start | bytes 245768 | tf_op jit(solution)/shard_map/ppermute | solution.py:401
  119.2 2.3 %collective-permute-done.26.refs_8_ = bf16[20,8,256]{2,1,0:T(8,128)(2,1)S(1)} collective-permute-done((bf16[20,8,256]{2,1,0:T(8,128)(2,1)S(1)}, bf16[20,8,256]{2,1,0:T(8,128)(2,1)S(1)}, u32[]{:S(2)}, u32[]{:S(2)}) %collective-permute-start.26) | collective-permute-done | bytes 81952 | tf_op jit(solution)/shard_map/ppermute | solution.py:401
  (92 shorter events, 30.9 us)
Async XLA Ops:
  4.8 9.8 %collective-permute-start.4 = (bf16[20,8,256]{2,1,0:T(8,128)(2,1)S(1)}, bf16[20,8,256]{2,1,0:T(8,128)(2,1)S(1)}, u32[]{:S(2)}, u32[]{:S(2)}) collective-permute-start(bf16[20,8,256]{2,1,0:T(8,128)(2,1)S(1)} %get-tuple-element.40), channel_id=1, source_target_pairs={{0,2},{1,3},{2,0},{3,1},{4,6},{5,7},{6,4},{7,5},{8,10},{9,11},{10,... | collective-permute-start | bytes 245768 | tf_op jit(solution)/shard_map/ppermute | solution.py:401
  8.0 6.5 %collective-permute-start.5 = (bf16[20,8,256]{2,1,0:T(8,128)(2,1)S(1)}, bf16[20,8,256]{2,1,0:T(8,128)(2,1)S(1)}, u32[]{:S(2)}, u32[]{:S(2)}) collective-permute-start(bf16[20,8,256]{2,1,0:T(8,128)(2,1)S(1)} %get-tuple-element.41), channel_id=1, source_target_pairs={{0,3},{1,2},{2,1},{3,0},{4,7},{5,6},{6,5},{7,4},{8,11},{9,10},{10,... | collective-permute-start | bytes 245768 | tf_op jit(solution)/shard_map/ppermute | solution.py:401
  15.1 25.6 %collective-permute-start.7 = (bf16[20,4,8,256]{3,2,1,0:T(8,128)(2,1)S(1)}, bf16[20,4,8,256]{3,2,1,0:T(8,128)(2,1)S(1)}, u32[]{:S(2)}, u32[]{:S(2)}) collective-permute-start(bf16[20,4,8,256]{3,2,1,0:T(8,128)(2,1)S(1)} %shard_map.105.refs_5_.refs_6_.refs_4_), channel_id=1, source_target_pairs={{0,254},{1,255},{2,252},{3,253},{4,8},{5,9},{6,10},{7,11},{8,4},{9... | collective-permute-start | bytes 983048 | tf_op jit(solution)/shard_map/ppermute | solution.py:397
  21.4 19.4 %collective-permute-start.6 = (bf16[20,4,8,256]{3,2,1,0:T(8,128)(2,1)S(1)}, bf16[20,4,8,256]{3,2,1,0:T(8,128)(2,1)S(1)}, u32[]{:S(2)}, u32[]{:S(2)}) collective-permute-start(bf16[20,4,8,256]{3,2,1,0:T(8,128)(2,1)S(1)} %shard_map.105.refs_5_.refs_6_.refs_4_), channel_id=1, source_target_pairs={{0,4},{4,0},{8,12},{12,8},{16,20},{20,16},{24,28},{28,24},{32,36},... | collective-permute-start | bytes 983048 | tf_op jit(solution)/shard_map/ppermute | solution.py:394
  22.1 8.0 %collective-permute-start = (bf16[23,8,256]{2,1,0:T(8,128)(2,1)S(1)}, bf16[23,8,256]{2,1,0:T(8,128)(2,1)S(1)}, u32[]{:S(2)}, u32[]{:S(2)}) collective-permute-start(bf16[23,8,256]{2,1,0:T(8,128)(2,1)S(1)} %get-tuple-element.35), channel_id=1, source_target_pairs={{0,1},{1,0},{2,3},{3,2},{4,5},{5,4},{6,7},{7,6},{8,9},{9,8},{10,11... | collective-permute-start | bytes 282632 | tf_op jit(solution)/shard_map/ppermute | solution.py:401
  22.3 8.3 %collective-permute-start.1 = (bf16[23,8,256]{2,1,0:T(8,128)(2,1)S(1)}, bf16[23,8,256]{2,1,0:T(8,128)(2,1)S(1)}, u32[]{:S(2)}, u32[]{:S(2)}) collective-permute-start(bf16[23,8,256]{2,1,0:T(8,128)(2,1)S(1)} %get-tuple-element.36), channel_id=1, source_target_pairs={{0,2},{1,3},{2,0},{3,1},{4,6},{5,7},{6,4},{7,5},{8,10},{9,11},{10,... | collective-permute-start | bytes 282632 | tf_op jit(solution)/shard_map/ppermute | solution.py:401
  25.7 13.1 %collective-permute-start.8 = (bf16[352,256]{1,0:T(8,128)(2,1)S(1)}, bf16[352,256]{1,0:T(8,128)(2,1)S(1)}, u32[]{:S(2)}, u32[]{:S(2)}) collective-permute-start(bf16[352,256]{1,0:T(8,128)(2,1)S(1)} %get-tuple-element.43), channel_id=1, source_target_pairs={{0,4},{4,0},{8,12},{12,8},{16,20},{20,16},{24,28},{28,24},{32,36},... | collective-permute-start | bytes 540680 | tf_op jit(solution)/shard_map/ppermute | solution.py:394
  30.2 10.6 %collective-permute-start.9 = (bf16[352,256]{1,0:T(8,128)(2,1)S(1)}, bf16[352,256]{1,0:T(8,128)(2,1)S(1)}, u32[]{:S(2)}, u32[]{:S(2)}) collective-permute-start(bf16[352,256]{1,0:T(8,128)(2,1)S(1)} %get-tuple-element.44), channel_id=1, source_target_pairs={{0,254},{1,255},{2,252},{3,253},{4,8},{5,9},{6,10},{7,11},{8,4},{9... | collective-permute-start | bytes 540680 | tf_op jit(solution)/shard_map/ppermute | solution.py:397
  30.6 8.2 %collective-permute-start.2 = (bf16[23,8,256]{2,1,0:T(8,128)(2,1)S(1)}, bf16[23,8,256]{2,1,0:T(8,128)(2,1)S(1)}, u32[]{:S(2)}, u32[]{:S(2)}) collective-permute-start(bf16[23,8,256]{2,1,0:T(8,128)(2,1)S(1)} %get-tuple-element.37), channel_id=1, source_target_pairs={{0,3},{1,2},{2,1},{3,0},{4,7},{5,6},{6,5},{7,4},{8,11},{9,10},{10,... | collective-permute-start | bytes 282632 | tf_op jit(solution)/shard_map/ppermute | solution.py:401
  45.1 8.5 %collective-permute-start.11 = (f32[32,256]{1,0:T(8,128)S(1)}, f32[32,256]{1,0:T(8,128)S(1)}, u32[]{:S(2)}, u32[]{:S(2)}) collective-permute-start(f32[32,256]{1,0:T(8,128)S(1)} %pad_maximum_fusion.1), channel_id=1, source_target_pairs={{0,254},{1,255},{2,252},{3,253},{4,8},{5,9},{6,10},{7,11},{8,4},{9... | collective-permute-start | bytes 98312 | tf_op jit(solution)/shard_map/ppermute | solution.py:397
  53.6 5.8 %collective-permute-start.14 = (f32[32,256]{1,0:T(8,128)S(1)}, f32[32,256]{1,0:T(8,128)S(1)}, u32[]{:S(2)}, u32[]{:S(2)}) collective-permute-start(f32[32,256]{1,0:T(8,128)S(1)} %maximum_add_fusion), channel_id=1, source_target_pairs={{0,3},{1,2},{2,1},{3,0},{4,7},{5,6},{6,5},{7,4},{8,11},{9,10},{10,... | collective-permute-start | bytes 98312 | tf_op jit(solution)/shard_map/ppermute | solution.py:406
  69.7 8.7 %collective-permute-start.20 = (f32[32,256]{1,0:T(8,128)S(1)}, f32[32,256]{1,0:T(8,128)S(1)}, u32[]{:S(2)}, u32[]{:S(2)}) collective-permute-start(f32[32,256]{1,0:T(8,128)S(1)} %pad_maximum_fusion.2), channel_id=1, source_target_pairs={{0,254},{1,255},{2,252},{3,253},{4,8},{5,9},{6,10},{7,11},{8,4},{9... | collective-permute-start | bytes 98312 | tf_op jit(solution)/shard_map/ppermute | solution.py:397
  79.3 5.8 %collective-permute-start.23 = (f32[40,256]{1,0:T(8,128)S(1)}, f32[40,256]{1,0:T(8,128)S(1)}, u32[]{:S(2)}, u32[]{:S(2)}) collective-permute-start(f32[40,256]{1,0:T(8,128)S(1)} %pad_maximum_fusion), channel_id=1, source_target_pairs={{0,3},{1,2},{2,1},{3,0},{4,7},{5,6},{6,5},{7,4},{8,11},{9,10},{10,... | collective-permute-start | bytes 122888 | tf_op jit(solution)/shard_map/ppermute | solution.py:406
  86.9 6.7 %collective-permute-start.30 = (f32[8,256]{1,0:T(8,128)S(1)}, f32[8,256]{1,0:T(8,128)S(1)}, u32[]{:S(2)}, u32[]{:S(2)}) collective-permute-start(f32[8,256]{1,0:T(8,128)S(1)} %shard_map.111), channel_id=1, source_target_pairs={{0,24},{4,28},{8,16},{12,20},{16,8},{20,12},{24,0},{28,4},{32,56},... | collective-permute-start | bytes 24584 | tf_op jit(solution)/shard_map/ppermute | solution.py:406
  87.0 8.5 %collective-permute-start.29 = (f32[8,256]{1,0:T(8,128)S(1)}, f32[8,256]{1,0:T(8,128)S(1)}, u32[]{:S(2)}, u32[]{:S(2)}) collective-permute-start(f32[8,256]{1,0:T(8,128)S(1)} %shard_map.111), channel_id=1, source_target_pairs={{0,16},{4,20},{8,24},{12,28},{16,0},{20,4},{24,8},{28,12},{32,48},... | collective-permute-start | bytes 24584 | tf_op jit(solution)/shard_map/ppermute | solution.py:406
  87.1 8.4 %collective-permute-start.28 = (f32[8,256]{1,0:T(8,128)S(1)}, f32[8,256]{1,0:T(8,128)S(1)}, u32[]{:S(2)}, u32[]{:S(2)}) collective-permute-start(f32[8,256]{1,0:T(8,128)S(1)} %shard_map.111), channel_id=1, source_target_pairs={{0,8},{4,12},{8,0},{12,4},{16,24},{20,28},{24,16},{28,20},{32,40},... | collective-permute-start | bytes 24584 | tf_op jit(solution)/shard_map/ppermute | solution.py:406
  91.5 8.7 %collective-permute-start.17 = (bf16[20,8,256]{2,1,0:T(8,128)(2,1)S(1)}, bf16[20,8,256]{2,1,0:T(8,128)(2,1)S(1)}, u32[]{:S(2)}, u32[]{:S(2)}) collective-permute-start(bf16[20,8,256]{2,1,0:T(8,128)(2,1)S(1)} %get-tuple-element.55), channel_id=1, source_target_pairs={{0,2},{1,3},{2,0},{3,1},{4,6},{5,7},{6,4},{7,5},{8,10},{9,11},{10,... | collective-permute-start | bytes 245768 | tf_op jit(solution)/shard_map/ppermute | solution.py:401
  93.5 6.6 %collective-permute-start.18 = (bf16[20,8,256]{2,1,0:T(8,128)(2,1)S(1)}, bf16[20,8,256]{2,1,0:T(8,128)(2,1)S(1)}, u32[]{:S(2)}, u32[]{:S(2)}) collective-permute-start(bf16[20,8,256]{2,1,0:T(8,128)(2,1)S(1)} %get-tuple-element.56), channel_id=1, source_target_pairs={{0,3},{1,2},{2,1},{3,0},{4,7},{5,6},{6,5},{7,4},{8,11},{9,10},{10,... | collective-permute-start | bytes 245768 | tf_op jit(solution)/shard_map/ppermute | solution.py:401
  95.4 6.1 %collective-permute-start.31 = (f32[8,256]{1,0:T(8,128)S(1)}, f32[8,256]{1,0:T(8,128)S(1)}, u32[]{:S(2)}, u32[]{:S(2)}) collective-permute-start(f32[8,256]{1,0:T(8,128)S(1)} %add_add_fusion.3), channel_id=1, source_target_pairs={{0,34},{1,35},{2,32},{3,33},{4,38},{5,39},{6,36},{7,37},{8,42},{9,... | collective-permute-start | bytes 24584 | tf_op jit(solution)/shard_map/ppermute | solution.py:511
  101.6 14.7 %collective-permute-start.34 = (f32[8,256]{1,0:T(8,128)S(1)}, f32[8,256]{1,0:T(8,128)S(1)}, u32[]{:S(2)}, u32[]{:S(2)}) collective-permute-start(f32[8,256]{1,0:T(8,128)S(1)} %add.70), channel_id=1, source_target_pairs={{0,192},{4,196},{8,200},{12,204},{16,208},{20,212},{24,216},{28,22... | collective-permute-start | bytes 24584 | tf_op jit(solution)/shard_map/ppermute | solution.py:406
  103.1 15.1 %collective-permute-start.33 = (f32[8,256]{1,0:T(8,128)S(1)}, f32[8,256]{1,0:T(8,128)S(1)}, u32[]{:S(2)}, u32[]{:S(2)}) collective-permute-start(f32[8,256]{1,0:T(8,128)S(1)} %add.70), channel_id=1, source_target_pairs={{0,128},{4,132},{8,136},{12,140},{16,144},{20,148},{24,152},{28,15... | collective-permute-start | bytes 24584 | tf_op jit(solution)/shard_map/ppermute | solution.py:406
  110.9 7.3 %collective-permute-start.32 = (f32[8,256]{1,0:T(8,128)S(1)}, f32[8,256]{1,0:T(8,128)S(1)}, u32[]{:S(2)}, u32[]{:S(2)}) collective-permute-start(f32[8,256]{1,0:T(8,128)S(1)} %add.70), channel_id=1, source_target_pairs={{0,64},{4,68},{8,72},{12,76},{16,80},{20,84},{24,88},{28,92},{32,9... | collective-permute-start | bytes 24584 | tf_op jit(solution)/shard_map/ppermute | solution.py:406
  115.3 6.2 %collective-permute-start.26 = (bf16[20,8,256]{2,1,0:T(8,128)(2,1)S(1)}, bf16[20,8,256]{2,1,0:T(8,128)(2,1)S(1)}, u32[]{:S(2)}, u32[]{:S(2)}) collective-permute-start(bf16[20,8,256]{2,1,0:T(8,128)(2,1)S(1)} %get-tuple-element.61), channel_id=1, source_target_pairs={{0,2},{1,3},{2,0},{3,1},{4,6},{5,7},{6,4},{7,5},{8,10},{9,11},{10,... | collective-permute-start | bytes 245768 | tf_op jit(solution)/shard_map/ppermute | solution.py:401
  116.3 6.3 %collective-permute-start.27 = (bf16[20,8,256]{2,1,0:T(8,128)(2,1)S(1)}, bf16[20,8,256]{2,1,0:T(8,128)(2,1)S(1)}, u32[]{:S(2)}, u32[]{:S(2)}) collective-permute-start(bf16[20,8,256]{2,1,0:T(8,128)(2,1)S(1)} %get-tuple-element.62), channel_id=1, source_target_pairs={{0,3},{1,2},{2,1},{3,0},{4,7},{5,6},{6,5},{7,4},{8,11},{9,10},{10,... | collective-permute-start | bytes 245768 | tf_op jit(solution)/shard_map/ppermute | solution.py:401
  (19 other events, 89.8 us)

commit v3 on v2

--- a/solution.py
+++ b/solution.py
@@ -11,6 +11,7 @@
 HV = 4
 NS = 2 * HV + 1
 STEP = 0.5
+GRP = 160
 F32 = jnp.float32
 BF16 = jnp.bfloat16
 VM = pl.BlockSpec(memory_space=pltpu.VMEM)
@@ -82,11 +83,37 @@
     outs[4][...] = lax.fori_loop(0, ctl.shape[0], body, sq, unroll=4)
 
 
-def densify_kernel(scal, nb, loc, inv, inn, vb, d_own, x_core, x_edge, vw, vwt, acc):
+def densify_kernel(
+    scal, nb, loc_hbm, inv_hbm, inn_hbm, band, d_own, x_core, x_edge, bands, acc, loc, obs, mat,
+    sems,
+):
+    copies = [
+        pltpu.make_async_copy(loc_hbm.at[0], loc.at[0], sems.at[0]),
+        pltpu.make_async_copy(loc_hbm.at[1], loc.at[1], sems.at[1]),
+        pltpu.make_async_copy(inv_hbm, obs.at[0], sems.at[2]),
+        pltpu.make_async_copy(inn_hbm, obs.at[1], sems.at[3]),
+    ]
+    for c in copies:
+        c.start()
+    row = lax.broadcasted_iota(jnp.int32, (256, 256), 0)
+    col = lax.broadcasted_iota(jnp.int32, (256, 256), 1)
+    shift = row - col
+    same = (row >> 5) == (col >> 5)
+    tot = jnp.zeros((256, 256), F32)
+    for s in range(NS):
+        tot = jnp.where(same & (shift == s - HV), band[s : s + 1, :], tot)
+    mat[...] = tot
+    back = mat[...]
+    fwd = mat[...].T
+    for i, m in enumerate((fwd, back)):
+        hi = m.astype(BF16)
+        bands[2 * i] = hi[0:GRP, 0:GRP]
+        bands[2 * i + 1] = (m - hi.astype(F32)).astype(BF16)[0:GRP, 0:GRP]
     tile = scal[0]
     core_rel = 2 - 2 * (tile & 1)
     acc[...] = jnp.zeros(acc.shape, F32)
     for b in range(2):
+        copies[b].wait()
         for j in range(loc.shape[1]):
             n = nb[b, j]
             rel = ((n >> 1) - tile + 65) & 63
@@ -99,18 +126,11 @@
                 out[128 * b : 128 * b + 128, 128 * h : 128 * h + 128] = acc[
                     b * 6 + role * 2 + h
                 ].astype(BF16)
+    copies[2].wait()
+    copies[3].wait()
     for out in (x_core, x_edge):
-        for i, v in enumerate(split3(inv[...]) + split3(inn[...])):
+        for i, v in enumerate(split3(obs[0]) + split3(obs[1])):
             out[256 + 16 * i : 272 + 16 * i, :] = v
-    lev = vb.shape[0]
-    row = lax.broadcasted_iota(jnp.int32, (lev, 128), 0)
-    for s in range(NS):
-        col = jnp.broadcast_to(vb[:, s : s + 1], (lev, 128))
-        src = row + (s - HV)
-        vw[s] = jnp.where((src >= 0) & (src < lev), col, 0.0)
-        src = row + (HV - s)
-        moved = pltpu.roll(col, (s - HV) % lev, 0)
-        vwt[s] = jnp.where((src >= 0) & (src < lev), moved, 0.0)
 
 
 def assemble_kernel(scal, e0, e1, e2, e3, out):
@@ -118,26 +138,25 @@
         out[:, scal[1] ^ k] = e[...]
 
 
-def forward_part(src, vw, avb, umat, ens3, dmats, w, hxs, norm):
-    ms = src.shape[0]
+def band_apply(mats, x, exact):
+    hi, lo = mats
+
+    def mul(a, b):
+        return jnp.dot(a, b, preferred_element_type=F32)
+
+    if exact:
+        return mul(hi, x) + mul(lo, x)
+    xh = x.astype(BF16)
+    xl = (x - xh.astype(F32)).astype(BF16)
+    return mul(hi, xh) + (mul(lo, xh) + mul(hi, xl))
+
+
+def forward_part(src, exact, mats, avb, umat, ens3, dmats, w, hxs, norm):
+    rows = avb.shape[0]
     lev = 32
-
-    def smooth(m, _):
-        block = src[m].reshape(lev, 256)
-        cols = []
-        for h in range(2):
-            a = block[:, 128 * h : 128 * h + 128]
-            tot = vw[HV] * a
-            for s in range(NS):
-                if s != HV:
-                    tot = tot + vw[s] * pltpu.roll(a, (HV - s) % lev, 0)
-            cols.append(tot)
-        avb[pl.ds(pl.multiple_of(lev * m, lev), lev), :] = jnp.concatenate(cols, axis=1).astype(
-            BF16
-        )
-        return 0
-
-    lax.fori_loop(0, ms, smooth, 0)
+    ms = rows // lev
+    for r in range(0, rows, GRP):
+        avb[r : r + GRP, :] = band_apply(mats, src(r), exact).astype(BF16)
     for ens, d, hx in zip(ens3, dmats, hxs):
         umat[...] = lax.dot_general(
             avb[...], d, (((1,), (1,)), ((), ())), preferred_element_type=F32
@@ -147,7 +166,7 @@
             e = ens[m].astype(F32).reshape(lev, 256)
             return acc + e * umat[pl.ds(pl.multiple_of(lev * m, lev), lev), :]
 
-        dx = lax.fori_loop(0, ms, member, jnp.zeros((lev, 256), F32), unroll=2)
+        dx = lax.fori_loop(0, ms, member, jnp.zeros((lev, 256), F32), unroll=4)
         hx(
             jnp.dot(
                 w[:, 0:lev], dx * norm, precision=lax.Precision.HIGHEST, preferred_element_type=F32
@@ -155,7 +174,7 @@
         )
 
 
-def adjoint_part(qs, wt, vwt, ens3, dmats, ua, umat, out, norm):
+def adjoint_part(qs, wt, mats, ens3, dmats, ua, umat, out, norm):
     ms = out.shape[0]
     lev = 32
     for r, (q, ens, d) in enumerate(zip(qs, ens3, dmats)):
@@ -171,27 +190,16 @@
             ua[pl.ds(pl.multiple_of(lev * m, lev), lev), :] = (e * dxa).astype(BF16)
             return 0
 
-        lax.fori_loop(0, ms, member, 0, unroll=2)
+        lax.fori_loop(0, ms, member, 0, unroll=4)
         part = jnp.dot(ua[...], d, preferred_element_type=F32)
         if r == 0:
             umat[...] = part
         else:
             umat[...] = umat[...] + part
-
-    def spread(m, _):
-        block = umat[pl.ds(pl.multiple_of(lev * m, lev), lev), :]
-        cols = []
-        for h in range(2):
-            a = block[:, 128 * h : 128 * h + 128]
-            tot = vwt[HV] * a
-            for s in range(NS):
-                if s != HV:
-                    tot = tot + vwt[s] * pltpu.roll(a, (s - HV) % lev, 0)
-            cols.append(tot)
-        out[m] = jnp.concatenate(cols, axis=1).reshape(4, 8, 256)
-        return 0
-
-    lax.fori_loop(0, ms, spread, 0)
+    five = GRP // lev
+    for i in range(0, ms, five):
+        got = band_apply(mats, umat[lev * i : lev * i + GRP, :], False)
+        out[i : i + five] = got.reshape(five, 4, 8, 256)
 
 
 def dmats_of(d_own, x_core, x_edge):
@@ -206,7 +214,7 @@
 
 
 def first_kernel(
-    norm, scal, c0, c1, c2, c3, e_own, e_core, e_edge, d_own, x_core, x_edge, vw,
+    norm, scal, c0, c1, c2, c3, e_own, e_core, e_edge, d_own, x_core, x_edge, bands,
     cm, hx_core, hx_oe, w, wt, src, wsq, avb, umat,
 ):
     share = src.shape[0]
@@ -231,15 +239,19 @@
     def put_edge(v):
         hx_oe[16:32, :] = v
 
+    def rows_of(r):
+        five = GRP // 32
+        return src[r // 32 : r // 32 + five].reshape(GRP, 256).astype(BF16)
+
     forward_part(
-        src, vw, avb, umat, (e_own, e_core, e_edge), dmats_of(d_own, x_core, x_edge), w,
-        (put_own, put_core, put_edge), norm,
+        rows_of, True, (bands[0], bands[1]), avb, umat, (e_own, e_core, e_edge),
+        dmats_of(d_own, x_core, x_edge), w, (put_own, put_core, put_edge), norm,
     )
 
 
 def second_kernel(
     norm, scal, h_oe, h_core, inv, inn, cm, e_own, e_core, e_edge, d_own, x_core, x_edge,
-    vw, vwt, w, wt, s0, a0, a1, a2, a3, hx_core, hx_oe, adj, ua, umat,
+    bands, w, wt, s0, a0, a1, a2, a3, hx_core, hx_oe, adj, ua, umat,
 ):
     share = adj.shape[0]
     ic, yc = obs_of(x_core)
@@ -251,7 +263,7 @@
     )
     ens3 = (e_own, e_core, e_edge)
     dmats = dmats_of(d_own, x_core, x_edge)
-    adjoint_part(qs, wt, vwt, ens3, dmats, ua, umat, adj, norm)
+    adjoint_part(qs, wt, (bands[2], bands[3]), ens3, dmats, ua, umat, adj, norm)
     for k, a in enumerate((a0, a1, a2, a3)):
         a[...] = adj[:, scal[1] ^ k].astype(BF16)
 
@@ -274,8 +286,13 @@
     def put_edge(v):
         hx_oe[16:32, :] = v
 
+    def rows_of(r):
+        five = GRP // 32
+        return adj[r // 32 : r // 32 + five].reshape(GRP, 256)
+
     forward_part(
-        adj, vw, ua, umat, ens3, dmats, w, (put_own, put_core, put_edge), norm
+        rows_of, False, (bands[0], bands[1]), ua, umat, ens3, dmats, w,
+        (put_own, put_core, put_edge), norm,
     )
     hx_core[16:24, :] = jnp.zeros((8, 256), F32)
     hx_core[16:17, :] = jnp.sum(s0[...], axis=0, keepdims=True)
@@ -304,28 +321,33 @@
 
 def third_kernel(
     norm, scal, h_oe, h_core, inv, e_own, e_core, e_edge, d_own, x_core, x_edge,
-    vwt, wt, a0, a1, a2, a3, adj, ua, umat,
+    bands, wt, a0, a1, a2, a3, adj, ua, umat,
 ):
     ic, _ = obs_of(x_core)
     ie, _ = obs_of(x_edge)
     qs = (inv[...] * h_oe[0:16, :], ic * h_core[...], ie * h_oe[16:32, :])
     adjoint_part(
-        qs, wt, vwt, (e_own, e_core, e_edge), dmats_of(d_own, x_core, x_edge), ua, umat, adj,
-        norm,
+        qs, wt, (bands[2], bands[3]), (e_own, e_core, e_edge), dmats_of(d_own, x_core, x_edge),
+        ua, umat, adj, norm,
     )
     for k, a in enumerate((a0, a1, a2, a3)):
         a[...] = adj[:, scal[1] ^ k].astype(BF16)
 
 
-def grad_first_kernel(scal, ctl, a0, a1, a2, a3, out):
+def grad_first_kernel(scal, ctl, a0, a1, a2, a3, out, buf, sems):
     share = a0.shape[0]
+    copies = []
     for k, a in enumerate((a0, a1, a2, a3)):
         at = pl.ds(share * (scal[2] ^ k), share)
-        out[at] = ctl[at] + a[...].astype(F32)
+        buf[k] = ctl[at] + a[...].astype(F32)
+        copies.append(pltpu.make_async_copy(buf.at[k], out.at[at], sems.at[k]))
+        copies[k].start()
+    for c in copies:
+        c.wait()
 
 
 def grad_second_kernel(
-    count, scal, ctl, a0, a1, a2, a3, b0, b1, b2, b3, sums, out, costs
+    count, scal, ctl, a0, a1, a2, a3, b0, b1, b2, b3, sums, out, costs, buf, sems
 ):
     tot = jnp.sum(sums[...], axis=1, keepdims=True)
     cc, gg, cg = tot[0:1], tot[1:2], tot[2:3]
@@ -335,19 +357,26 @@
     second = 0.5 * (cc - 2.0 * tau * cg + tau * tau * gg) + 0.5 * (
         dd - 2.0 * tau * qd + tau * tau * rd
     )
+    tb = jnp.broadcast_to(tau, (8, 256))
+    share = a0.shape[0]
+    copies = []
+    for k, (a, b) in enumerate(zip((a0, a1, a2, a3), (b0, b1, b2, b3))):
+        base = share * (scal[2] ^ k)
+
+        def body(m, _, a=a, b=b, k=k, base=base):
+            g = ctl[base + m] + a[m].astype(F32)
+            buf[k, m] = g - tb * (g + b[m].astype(F32))
+            return 0
+
+        lax.fori_loop(0, share, body, 0, unroll=5)
+        copies.append(
+            pltpu.make_async_copy(buf.at[k], out.at[pl.ds(base, share)], sems.at[k])
+        )
+        copies[k].start()
     costs[0] = first[0, 0]
     costs[1] = (second / count)[0, 0]
-    tb = jnp.broadcast_to(tau, (8, 256))
-    share = a0.shape[0]
-    for k, (a, b) in enumerate(zip((a0, a1, a2, a3), (b0, b1, b2, b3))):
-
-        def body(m, _, a=a, b=b, k=k):
-            at = share * (scal[2] ^ k) + m
-            g = ctl[at] + a[m].astype(F32)
-            out[at] = g - tb * (g + b[m].astype(F32))
-            return 0
-
-        lax.fori_loop(0, share, body, 0, unroll=4)
+    for c in copies:
+        c.wait()
 
 
 def make_pairs(tiles, levs):
@@ -408,21 +437,34 @@
         return (x + one) + (two + three)
 
     chunk = sds((share, ldev, pdev), BF16)
+    hbm = pl.BlockSpec(memory_space=pltpu.HBM)
+
+    def far_off(x):
+        return pltpu.with_memory_space_constraint(x, pltpu.HBM)
+
     eparts = call(
-        pack_ens_kernel, [chunk] * 4, (scal, ensemble), 1,
+        pack_ens_kernel, [chunk] * 4, (scal, far_off(ensemble)), 1,
         [pltpu.SemaphoreType.DMA((4,))],
-        specs=[SM, pl.BlockSpec(memory_space=pltpu.HBM)],
+        specs=[SM, hbm],
     )
     eparts = shuffle(eparts)
-    d_own, x_core, x_edge, vw, vwt = call(
+    band = jnp.tile(vert_band.T, (1, 8))
+    d_own, x_core, x_edge, bands = call(
         densify_kernel,
         [
             sds((256, 256), BF16), sds((352, 256), BF16), sds((352, 256), BF16),
-            sds((NS, lev, 128), F32), sds((NS, lev, 128), F32),
+            sds((4, GRP, GRP), BF16),
         ],
-        (scal, neighbours, loc_blocks, inv_error, innovation, vert_band),
+        (
+            scal, neighbours, far_off(loc_blocks), far_off(inv_error), far_off(innovation), band,
+        ),
         2,
-        [pltpu.VMEM((12, 128, 128), F32)],
+        [
+            pltpu.VMEM((12, 128, 128), F32), pltpu.VMEM(loc_blocks.shape, BF16),
+            pltpu.VMEM((2,) + inv_error.shape, F32), pltpu.VMEM((256, 256), F32),
+            pltpu.SemaphoreType.DMA((4,)),
+        ],
+        specs=[SM, SM, hbm, hbm, hbm, VM],
     )
     wt_own = jnp.pad(channel_weights.T, ((0, 0), (0, pdev - channel_weights.shape[0])))
     packed = call(
@@ -458,7 +500,7 @@
             field, sds((obs, pdev), F32), sds((2 * obs, pdev), F32),
             sds((obs, 128), F32), sds((lev, 128), F32),
         ],
-        (scal, *cparts, e_own, e_core, e_edge, d_own, x_core, x_edge, vw),
+        (scal, *cparts, e_own, e_core, e_edge, d_own, x_core, x_edge, bands),
         1,
         [full, pltpu.VMEM((128, 128), F32), half, umat],
         mm,
@@ -481,7 +523,7 @@
         [chunk] * 4 + [sds((obs + 8, pdev), F32), sds((2 * obs, pdev), F32)],
         (
             scal, h1_oe, h1_core, inv_error, innovation, cm, e_own, e_core, e_edge,
-            d_own, x_core, x_edge, vw, vwt, w, wt, s0,
+            d_own, x_core, x_edge, bands, w, wt, s0,
         ),
         1,
         [full, half, umat],
@@ -500,7 +542,7 @@
         [chunk] * 4,
         (
             scal, hs, hd_core, inv_error, e_own, e_core, e_edge, d_own, x_core, x_edge,
-            vwt, wt,
+            bands, wt,
         ),
         1,
         [full, half, umat],
@@ -511,14 +553,20 @@
     sums = sums + lax.ppermute(sums, both, far)
     sums = sum4(sums, "tile", tile_xor, (16, 32, 48))
     whole = sds((members, ldev, pdev), F32)
-    (grad_first,) = call(grad_first_kernel, [whole], (scal, control, *aparts), 1)
+    anywhere = pl.BlockSpec(memory_space=pl.ANY)
+    outbuf = [pltpu.VMEM((4, share, ldev, pdev), F32), pltpu.SemaphoreType.DMA((4,))]
+    (grad_first,) = call(
+        grad_first_kernel, [whole], (scal, control, *aparts), 1, outbuf,
+        out_specs=(anywhere,),
+    )
     count = float(members * lev * pdev * tiles)
     grad_second, costs = call(
         bind(grad_second_kernel, count),
         [whole, sds((2,), F32)],
         (scal, control, *aparts, *bparts, sums),
         1,
-        out_specs=(VM, SM),
+        outbuf,
+        out_specs=(anywhere, SM),
     )
     return grad_first, grad_second, costs
 

time: 125 us -> 123 us (0.984)
  waiting for transfers between devices: 56.2 us -> 54.8 us
    ppermute x12, waiting for transfers between devices: 26.6 us -> 25 us  [shuffle(): lax.ppermute(parts[k], 'lev', lev_xor(k))]
where the time goes in v3:
time: 123 us; the launch traced here: 122 us
  waiting for transfers between devices  54.8 us (45%)
  starting transfers between devices  48.3 us (39%)
  Pallas kernels  16.7 us (14%)
    ppermute x12, waiting for transfers between devices, shuffle(): lax.ppermute(parts[k], 'lev', lev_xor(k))  25 us
    ppermute x12, starting transfers between devices, sum4(): one, two, three = (lax.ppermute(x, axis, pairs(k)) for k in steps)  21.6 us
    ppermute x12, starting transfers between devices, shuffle(): lax.ppermute(parts[k], 'lev', lev_xor(k))  18.6 us
    ppermute x4, waiting for transfers between devices, swap_edge(): return lax.ppermute(x, both, edge)  18.2 us
    pallas_call x10, Pallas kernels, call(): pl.pallas_call(body, out_shape=tuple(outs), in_specs=specs, out_specs=out...  16.7 us
    ppermute x4, starting transfers between devices, swap_edge(): return lax.ppermute(x, both, edge)  7.28 us
    ppermute x12, waiting for transfers between devices, sum4(): one, two, three = (lax.ppermute(x, axis, pairs(k)) for k in steps)  6.99 us
    ppermute x6, waiting for transfers between devices, swap_core(): return lax.ppermute(x, 'tile', tile_xor(1))  4.58 us
  transfers between devices with their start and end apart: 35, of which 22 were waited for; matrix products, arithmetic and copies ran while one was open for 0% of the time, Pallas kernels for 5%

profile of v3, /device:TPU:2, one launch (start us, length us, event | category | flops | bytes accessed | tf_op | source)
XLA Modules:
  0.0 121.7 jit_solution(256122915591969386)
XLA Ops:
  2.3 2.0 %collective-permute-start.3 = (bf16[20,8,256]{2,1,0:T(8,128)(2,1)S(1)}, bf16[20,8,256]{2,1,0:T(8,128)(2,1)S(1)}, u32[]{:S(2)}, u32[]{:S(2)}) collective-permute-start(bf16[20,8,256]{2,1,0:T(8,128)(2,1)S(1)} %get-tuple-element.38), channel_id=1, source_target_pairs={{0,1},{1,0},{2,3},{3,2},{4,5},{5,4},{6,7},{7,6},{8,9},{9,8},{10,11... | collective-permute-start | bytes 245768 | tf_op jit(solution)/shard_map/ppermute | solution.py:430
  4.3 3.3 %collective-permute-start.4 = (bf16[20,8,256]{2,1,0:T(8,128)(2,1)S(1)}, bf16[20,8,256]{2,1,0:T(8,128)(2,1)S(1)}, u32[]{:S(2)}, u32[]{:S(2)}) collective-permute-start(bf16[20,8,256]{2,1,0:T(8,128)(2,1)S(1)} %get-tuple-element.39), channel_id=1, source_target_pairs={{0,2},{1,3},{2,0},{3,1},{4,6},{5,7},{6,4},{7,5},{8,10},{9,11},{10,... | collective-permute-start | bytes 245768 | tf_op jit(solution)/shard_map/ppermute | solution.py:430
  7.6 6.5 %collective-permute-done.4.e2 = bf16[20,8,256]{2,1,0:T(8,128)(2,1)S(1)} collective-permute-done((bf16[20,8,256]{2,1,0:T(8,128)(2,1)S(1)}, bf16[20,8,256]{2,1,0:T(8,128)(2,1)S(1)}, u32[]{:S(2)}, u32[]{:S(2)}) %collective-permute-start.4) | collective-permute-done | bytes 81952 | tf_op jit(solution)/shard_map/ppermute | solution.py:430
  14.7 6.2 %collective-permute-start.7 = (bf16[20,4,8,256]{3,2,1,0:T(8,128)(2,1)S(1)}, bf16[20,4,8,256]{3,2,1,0:T(8,128)(2,1)S(1)}, u32[]{:S(2)}, u32[]{:S(2)}) collective-permute-start(bf16[20,4,8,256]{3,2,1,0:T(8,128)(2,1)S(1)} %shard_map.105.refs_5_.refs_6_.refs_4_), channel_id=1, source_target_pairs={{0,254},{1,255},{2,252},{3,253},{4,8},{5,9},{6,10},{7,11},{8,4},{9... | collective-permute-start | bytes 983048 | tf_op jit(solution)/shard_map/ppermute | solution.py:426
  21.8 2.5 %collective-permute-start.1 = (bf16[23,8,256]{2,1,0:T(8,128)(2,1)S(1)}, bf16[23,8,256]{2,1,0:T(8,128)(2,1)S(1)}, u32[]{:S(2)}, u32[]{:S(2)}) collective-permute-start(bf16[23,8,256]{2,1,0:T(8,128)(2,1)S(1)} %get-tuple-element.35), channel_id=1, source_target_pairs={{0,2},{1,3},{2,0},{3,1},{4,6},{5,7},{6,4},{7,5},{8,10},{9,11},{10,... | collective-permute-start | bytes 282632 | tf_op jit(solution)/shard_map/ppermute | solution.py:430
  26.8 2.9 %collective-permute-done.refs_2_ = bf16[23,8,256]{2,1,0:T(8,128)(2,1)S(1)} collective-permute-done((bf16[23,8,256]{2,1,0:T(8,128)(2,1)S(1)}, bf16[23,8,256]{2,1,0:T(8,128)(2,1)S(1)}, u32[]{:S(2)}, u32[]{:S(2)}) %collective-permute-start) | collective-permute-done | bytes 94240 | tf_op jit(solution)/shard_map/ppermute | solution.py:430
  30.1 1.9 %collective-permute-start.2 = (bf16[23,8,256]{2,1,0:T(8,128)(2,1)S(1)}, bf16[23,8,256]{2,1,0:T(8,128)(2,1)S(1)}, u32[]{:S(2)}, u32[]{:S(2)}) collective-permute-start(bf16[23,8,256]{2,1,0:T(8,128)(2,1)S(1)} %get-tuple-element.36), channel_id=1, source_target_pairs={{0,3},{1,2},{2,1},{3,0},{4,7},{5,6},{6,5},{7,4},{8,11},{9,10},{10,... | collective-permute-start | bytes 282632 | tf_op jit(solution)/shard_map/ppermute | solution.py:430
  32.0 6.3 %collective-permute-done.2.refs_4_ = bf16[23,8,256]{2,1,0:T(8,128)(2,1)S(1)} collective-permute-done((bf16[23,8,256]{2,1,0:T(8,128)(2,1)S(1)}, bf16[23,8,256]{2,1,0:T(8,128)(2,1)S(1)}, u32[]{:S(2)}, u32[]{:S(2)}) %collective-permute-start.2) | collective-permute-done | bytes 94240 | tf_op jit(solution)/shard_map/ppermute | solution.py:430
  38.3 2.0 %collective-permute-done.9.refs_10_.refs_11_.refs_9_ = bf16[352,256]{1,0:T(8,128)(2,1)S(1)} collective-permute-done((bf16[352,256]{1,0:T(8,128)(2,1)S(1)}, bf16[352,256]{1,0:T(8,128)(2,1)S(1)}, u32[]{:S(2)}, u32[]{:S(2)}) %collective-permute-start.9) | collective-permute-done | bytes 180256 | tf_op jit(solution)/shard_map/ppermute | solution.py:426
  40.3 2.2 %shard_map.107 = (bf16[20,4,8,256]{3,2,1,0:T(8,128)(2,1)S(1)}, f32[16,256]{1,0:T(8,128)S(1)}, f32[32,256]{1,0:T(8,128)S(1)}, f32[16,128]{1,0:T(8,128)S(1)}, f32[32,128]{1,0:T(8,128)S(1)}) custom-call(s32[4]{0:T(128)S(1)} %pad_add_fusion.scal.refs_0_, bf16[23,8,256]{2,1,0:T(8,128)(2,1)S(1)} %get-tuple-element.33.refs_1_, ...), custom_call_target="tpu_custom_call" | custom-call | flops 251658240 | bytes 2457616 | tf_op jit(solution)/shard_map/pallas_call | solution.py:28
  44.7 7.6 %collective-permute-done.11 = f32[32,256]{1,0:T(8,128)S(1)} collective-permute-done((f32[32,256]{1,0:T(8,128)S(1)}, f32[32,256]{1,0:T(8,128)S(1)}, u32[]{:S(2)}, u32[]{:S(2)}) %collective-permute-start.11) | collective-permute-done | bytes 32800 | tf_op jit(solution)/shard_map/ppermute | solution.py:426
  52.3 2.0 %collective-permute-start.14 = (f32[32,256]{1,0:T(8,128)S(1)}, f32[32,256]{1,0:T(8,128)S(1)}, u32[]{:S(2)}, u32[]{:S(2)}) collective-permute-start(f32[32,256]{1,0:T(8,128)S(1)} %maximum_add_fusion), channel_id=1, source_target_pairs={{0,3},{1,2},{2,1},{3,0},{4,7},{5,6},{6,5},{7,4},{8,11},{9,10},{10,... | collective-permute-start | bytes 98312 | tf_op jit(solution)/shard_map/ppermute | solution.py:435
  54.3 2.0 %collective-permute-start.13 = (f32[32,256]{1,0:T(8,128)S(1)}, f32[32,256]{1,0:T(8,128)S(1)}, u32[]{:S(2)}, u32[]{:S(2)}) collective-permute-start(f32[32,256]{1,0:T(8,128)S(1)} %maximum_add_fusion), channel_id=1, source_target_pairs={{0,2},{1,3},{2,0},{3,1},{4,6},{5,7},{6,4},{7,5},{8,10},{9,11},{10,... | collective-permute-start | bytes 98312 | tf_op jit(solution)/shard_map/ppermute | solution.py:435
  61.7 4.2 %shard_map.108 = (bf16[20,8,256]{2,1,0:T(8,128)(2,1)S(1)}, bf16[20,8,256]{2,1,0:T(8,128)(2,1)S(1)}, bf16[20,8,256]{2,1,0:T(8,128)(2,1)S(1)}, bf16[20,8,256]{2,1,...) custom-call(s32[4]{0:T(128)S(1)} %pad_add_fusion.scal.refs_0_, ...), custom_call_target="tpu_custom_call" | custom-call | flops 503316480 | bytes 2506768 | tf_op jit(solution)/shard_map/pallas_call | solution.py:28
  67.2 8.6 %collective-permute-done.20 = f32[32,256]{1,0:T(8,128)S(1)} collective-permute-done((f32[32,256]{1,0:T(8,128)S(1)}, f32[32,256]{1,0:T(8,128)S(1)}, u32[]{:S(2)}, u32[]{:S(2)}) %collective-permute-start.20) | collective-permute-done | bytes 32800 | tf_op jit(solution)/shard_map/ppermute | solution.py:426
  76.7 1.9 %collective-permute-start.23 = (f32[40,256]{1,0:T(8,128)S(1)}, f32[40,256]{1,0:T(8,128)S(1)}, u32[]{:S(2)}, u32[]{:S(2)}) collective-permute-start(f32[40,256]{1,0:T(8,128)S(1)} %pad_maximum_fusion), channel_id=1, source_target_pairs={{0,3},{1,2},{2,1},{3,0},{4,7},{5,6},{6,5},{7,4},{8,11},{9,10},{10,... | collective-permute-start | bytes 122888 | tf_op jit(solution)/shard_map/ppermute | solution.py:435
  84.5 4.0 %collective-permute-start.28 = (f32[8,256]{1,0:T(8,128)S(1)}, f32[8,256]{1,0:T(8,128)S(1)}, u32[]{:S(2)}, u32[]{:S(2)}) collective-permute-start(f32[8,256]{1,0:T(8,128)S(1)} %shard_map.111), channel_id=1, source_target_pairs={{0,8},{4,12},{8,0},{12,4},{16,24},{20,28},{24,16},{28,20},{32,40},... | collective-permute-start | bytes 24584 | tf_op jit(solution)/shard_map/ppermute | solution.py:435
  88.9 2.1 %collective-permute-start.17 = (bf16[20,8,256]{2,1,0:T(8,128)(2,1)S(1)}, bf16[20,8,256]{2,1,0:T(8,128)(2,1)S(1)}, u32[]{:S(2)}, u32[]{:S(2)}) collective-permute-start(bf16[20,8,256]{2,1,0:T(8,128)(2,1)S(1)} %get-tuple-element.53), channel_id=1, source_target_pairs={{0,2},{1,3},{2,0},{3,1},{4,6},{5,7},{6,4},{7,5},{8,10},{9,11},{10,... | collective-permute-start | bytes 245768 | tf_op jit(solution)/shard_map/ppermute | solution.py:430
  93.3 4.3 %collective-permute-done.17.a2.refs_4_ = bf16[20,8,256]{2,1,0:T(8,128)(2,1)S(1)} collective-permute-done((bf16[20,8,256]{2,1,0:T(8,128)(2,1)S(1)}, bf16[20,8,256]{2,1,0:T(8,128)(2,1)S(1)}, u32[]{:S(2)}, u32[]{:S(2)}) %collective-permute-start.17) | collective-permute-done | bytes 81952 | tf_op jit(solution)/shard_map/ppermute | solution.py:430
  100.6 7.8 %collective-permute-start.33 = (f32[8,256]{1,0:T(8,128)S(1)}, f32[8,256]{1,0:T(8,128)S(1)}, u32[]{:S(2)}, u32[]{:S(2)}) collective-permute-start(f32[8,256]{1,0:T(8,128)S(1)} %add.70), channel_id=1, source_target_pairs={{0,128},{4,132},{8,136},{12,140},{16,144},{20,148},{24,152},{28,15... | collective-permute-start | bytes 24584 | tf_op jit(solution)/shard_map/ppermute | solution.py:435
  108.5 2.1 %shard_map.110 = (bf16[20,8,256]{2,1,0:T(8,128)(2,1)S(1)}, bf16[20,8,256]{2,1,0:T(8,128)(2,1)S(1)}, bf16[20,8,256]{2,1,0:T(8,128)(2,1)S(1)}, bf16[20,8,256]{2,1,0:T(8,128)(2,1)S(1)}) custom-call(s32[4]{0:T(128)S(1)} %pad_add_fusion.scal.refs_0_, f32[40,256]{1,0:T(8,128)S(1)} %add_add_fusion.refs_1_.hs, f32[16,256]{1,0:T(8,128)S(1)} %collective-permute-done.24.refs_2_.h_core, ...), custom_call_target="tpu_custom_call" | custom-call | flops 251658240 | bytes 2097168 | tf_op jit(solution)/shard_map/pallas_call | solution.py:28
  113.2 1.9 %collective-permute-start.27 = (bf16[20,8,256]{2,1,0:T(8,128)(2,1)S(1)}, bf16[20,8,256]{2,1,0:T(8,128)(2,1)S(1)}, u32[]{:S(2)}, u32[]{:S(2)}) collective-permute-start(bf16[20,8,256]{2,1,0:T(8,128)(2,1)S(1)} %get-tuple-element.60), channel_id=1, source_target_pairs={{0,3},{1,2},{2,1},{3,0},{4,7},{5,6},{6,5},{7,4},{8,11},{9,10},{10,... | collective-permute-start | bytes 245768 | tf_op jit(solution)/shard_map/ppermute | solution.py:430
  116.0 2.3 %collective-permute-done.26.refs_8_ = bf16[20,8,256]{2,1,0:T(8,128)(2,1)S(1)} collective-permute-done((bf16[20,8,256]{2,1,0:T(8,128)(2,1)S(1)}, bf16[20,8,256]{2,1,0:T(8,128)(2,1)S(1)}, u32[]{:S(2)}, u32[]{:S(2)}) %collective-permute-start.26) | collective-permute-done | bytes 81952 | tf_op jit(solution)/shard_map/ppermute | solution.py:430
  119.5 2.1 %shard_map.112 = (f32[80,8,256]{2,1,0:T(8,128)}, f32[2]{0:T(128)}) custom-call(s32[4]{0:T(128)S(1)} %pad_add_fusion.scal.refs_0_, f32[80,8,256]{2,1,0:T(8,128)S(1)} %copy-done, bf16[20,8,256]{2,1,0:T(8,128)(2,1)S(1)} %get-tuple-element.51.a0.refs_2_, bf16[20,8,256]{2,1,0:T(8,128)(2,1)S(1)} %collective-permute-done.16.a1.refs_3_, ...), custom_call_target="tpu_custom_call" | custom-call | bytes 1974296 | tf_op jit(solution)/shard_map/pallas_call | solution.py:28
  (89 shorter events, 32.0 us)
Async XLA Ops:
  4.3 9.8 %collective-permute-start.4 = (bf16[20,8,256]{2,1,0:T(8,128)(2,1)S(1)}, bf16[20,8,256]{2,1,0:T(8,128)(2,1)S(1)}, u32[]{:S(2)}, u32[]{:S(2)}) collective-permute-start(bf16[20,8,256]{2,1,0:T(8,128)(2,1)S(1)} %get-tuple-element.39), channel_id=1, source_target_pairs={{0,2},{1,3},{2,0},{3,1},{4,6},{5,7},{6,4},{7,5},{8,10},{9,11},{10,... | collective-permute-start | bytes 245768 | tf_op jit(solution)/shard_map/ppermute | solution.py:430
  7.6 6.5 %collective-permute-start.5 = (bf16[20,8,256]{2,1,0:T(8,128)(2,1)S(1)}, bf16[20,8,256]{2,1,0:T(8,128)(2,1)S(1)}, u32[]{:S(2)}, u32[]{:S(2)}) collective-permute-start(bf16[20,8,256]{2,1,0:T(8,128)(2,1)S(1)} %get-tuple-element.40), channel_id=1, source_target_pairs={{0,3},{1,2},{2,1},{3,0},{4,7},{5,6},{6,5},{7,4},{8,11},{9,10},{10,... | collective-permute-start | bytes 245768 | tf_op jit(solution)/shard_map/ppermute | solution.py:430
  14.7 25.6 %collective-permute-start.7 = (bf16[20,4,8,256]{3,2,1,0:T(8,128)(2,1)S(1)}, bf16[20,4,8,256]{3,2,1,0:T(8,128)(2,1)S(1)}, u32[]{:S(2)}, u32[]{:S(2)}) collective-permute-start(bf16[20,4,8,256]{3,2,1,0:T(8,128)(2,1)S(1)} %shard_map.105.refs_5_.refs_6_.refs_4_), channel_id=1, source_target_pairs={{0,254},{1,255},{2,252},{3,253},{4,8},{5,9},{6,10},{7,11},{8,4},{9... | collective-permute-start | bytes 983048 | tf_op jit(solution)/shard_map/ppermute | solution.py:426
  20.9 19.4 %collective-permute-start.6 = (bf16[20,4,8,256]{3,2,1,0:T(8,128)(2,1)S(1)}, bf16[20,4,8,256]{3,2,1,0:T(8,128)(2,1)S(1)}, u32[]{:S(2)}, u32[]{:S(2)}) collective-permute-start(bf16[20,4,8,256]{3,2,1,0:T(8,128)(2,1)S(1)} %shard_map.105.refs_5_.refs_6_.refs_4_), channel_id=1, source_target_pairs={{0,4},{4,0},{8,12},{12,8},{16,20},{20,16},{24,28},{28,24},{32,36},... | collective-permute-start | bytes 983048 | tf_op jit(solution)/shard_map/ppermute | solution.py:423
  21.7 8.0 %collective-permute-start = (bf16[23,8,256]{2,1,0:T(8,128)(2,1)S(1)}, bf16[23,8,256]{2,1,0:T(8,128)(2,1)S(1)}, u32[]{:S(2)}, u32[]{:S(2)}) collective-permute-start(bf16[23,8,256]{2,1,0:T(8,128)(2,1)S(1)} %get-tuple-element.34), channel_id=1, source_target_pairs={{0,1},{1,0},{2,3},{3,2},{4,5},{5,4},{6,7},{7,6},{8,9},{9,8},{10,11... | collective-permute-start | bytes 282632 | tf_op jit(solution)/shard_map/ppermute | solution.py:430
  21.8 8.3 %collective-permute-start.1 = (bf16[23,8,256]{2,1,0:T(8,128)(2,1)S(1)}, bf16[23,8,256]{2,1,0:T(8,128)(2,1)S(1)}, u32[]{:S(2)}, u32[]{:S(2)}) collective-permute-start(bf16[23,8,256]{2,1,0:T(8,128)(2,1)S(1)} %get-tuple-element.35), channel_id=1, source_target_pairs={{0,2},{1,3},{2,0},{3,1},{4,6},{5,7},{6,4},{7,5},{8,10},{9,11},{10,... | collective-permute-start | bytes 282632 | tf_op jit(solution)/shard_map/ppermute | solution.py:430
  26.7 11.6 %collective-permute-start.8 = (bf16[352,256]{1,0:T(8,128)(2,1)S(1)}, bf16[352,256]{1,0:T(8,128)(2,1)S(1)}, u32[]{:S(2)}, u32[]{:S(2)}) collective-permute-start(bf16[352,256]{1,0:T(8,128)(2,1)S(1)} %get-tuple-element.42), channel_id=1, source_target_pairs={{0,4},{4,0},{8,12},{12,8},{16,20},{20,16},{24,28},{28,24},{32,36},... | collective-permute-start | bytes 540680 | tf_op jit(solution)/shard_map/ppermute | solution.py:423
  29.7 10.6 %collective-permute-start.9 = (bf16[352,256]{1,0:T(8,128)(2,1)S(1)}, bf16[352,256]{1,0:T(8,128)(2,1)S(1)}, u32[]{:S(2)}, u32[]{:S(2)}) collective-permute-start(bf16[352,256]{1,0:T(8,128)(2,1)S(1)} %get-tuple-element.43), channel_id=1, source_target_pairs={{0,254},{1,255},{2,252},{3,253},{4,8},{5,9},{6,10},{7,11},{8,4},{9... | collective-permute-start | bytes 540680 | tf_op jit(solution)/shard_map/ppermute | solution.py:426
  30.1 8.2 %collective-permute-start.2 = (bf16[23,8,256]{2,1,0:T(8,128)(2,1)S(1)}, bf16[23,8,256]{2,1,0:T(8,128)(2,1)S(1)}, u32[]{:S(2)}, u32[]{:S(2)}) collective-permute-start(bf16[23,8,256]{2,1,0:T(8,128)(2,1)S(1)} %get-tuple-element.36), channel_id=1, source_target_pairs={{0,3},{1,2},{2,1},{3,0},{4,7},{5,6},{6,5},{7,4},{8,11},{9,10},{10,... | collective-permute-start | bytes 282632 | tf_op jit(solution)/shard_map/ppermute | solution.py:430
  43.7 8.5 %collective-permute-start.11 = (f32[32,256]{1,0:T(8,128)S(1)}, f32[32,256]{1,0:T(8,128)S(1)}, u32[]{:S(2)}, u32[]{:S(2)}) collective-permute-start(f32[32,256]{1,0:T(8,128)S(1)} %pad_maximum_fusion.1), channel_id=1, source_target_pairs={{0,254},{1,255},{2,252},{3,253},{4,8},{5,9},{6,10},{7,11},{8,4},{9... | collective-permute-start | bytes 98312 | tf_op jit(solution)/shard_map/ppermute | solution.py:426
  52.3 5.8 %collective-permute-start.14 = (f32[32,256]{1,0:T(8,128)S(1)}, f32[32,256]{1,0:T(8,128)S(1)}, u32[]{:S(2)}, u32[]{:S(2)}) collective-permute-start(f32[32,256]{1,0:T(8,128)S(1)} %maximum_add_fusion), channel_id=1, source_target_pairs={{0,3},{1,2},{2,1},{3,0},{4,7},{5,6},{6,5},{7,4},{8,11},{9,10},{10,... | collective-permute-start | bytes 98312 | tf_op jit(solution)/shard_map/ppermute | solution.py:435
  67.1 8.7 %collective-permute-start.20 = (f32[32,256]{1,0:T(8,128)S(1)}, f32[32,256]{1,0:T(8,128)S(1)}, u32[]{:S(2)}, u32[]{:S(2)}) collective-permute-start(f32[32,256]{1,0:T(8,128)S(1)} %pad_maximum_fusion.2), channel_id=1, source_target_pairs={{0,254},{1,255},{2,252},{3,253},{4,8},{5,9},{6,10},{7,11},{8,4},{9... | collective-permute-start | bytes 98312 | tf_op jit(solution)/shard_map/ppermute | solution.py:426
  76.7 5.8 %collective-permute-start.23 = (f32[40,256]{1,0:T(8,128)S(1)}, f32[40,256]{1,0:T(8,128)S(1)}, u32[]{:S(2)}, u32[]{:S(2)}) collective-permute-start(f32[40,256]{1,0:T(8,128)S(1)} %pad_maximum_fusion), channel_id=1, source_target_pairs={{0,3},{1,2},{2,1},{3,0},{4,7},{5,6},{6,5},{7,4},{8,11},{9,10},{10,... | collective-permute-start | bytes 122888 | tf_op jit(solution)/shard_map/ppermute | solution.py:435
  84.3 6.7 %collective-permute-start.30 = (f32[8,256]{1,0:T(8,128)S(1)}, f32[8,256]{1,0:T(8,128)S(1)}, u32[]{:S(2)}, u32[]{:S(2)}) collective-permute-start(f32[8,256]{1,0:T(8,128)S(1)} %shard_map.111), channel_id=1, source_target_pairs={{0,24},{4,28},{8,16},{12,20},{16,8},{20,12},{24,0},{28,4},{32,56},... | collective-permute-start | bytes 24584 | tf_op jit(solution)/shard_map/ppermute | solution.py:435
  84.4 8.5 %collective-permute-start.29 = (f32[8,256]{1,0:T(8,128)S(1)}, f32[8,256]{1,0:T(8,128)S(1)}, u32[]{:S(2)}, u32[]{:S(2)}) collective-permute-start(f32[8,256]{1,0:T(8,128)S(1)} %shard_map.111), channel_id=1, source_target_pairs={{0,16},{4,20},{8,24},{12,28},{16,0},{20,4},{24,8},{28,12},{32,48},... | collective-permute-start | bytes 24584 | tf_op jit(solution)/shard_map/ppermute | solution.py:435
  84.5 8.4 %collective-permute-start.28 = (f32[8,256]{1,0:T(8,128)S(1)}, f32[8,256]{1,0:T(8,128)S(1)}, u32[]{:S(2)}, u32[]{:S(2)}) collective-permute-start(f32[8,256]{1,0:T(8,128)S(1)} %shard_map.111), channel_id=1, source_target_pairs={{0,8},{4,12},{8,0},{12,4},{16,24},{20,28},{24,16},{28,20},{32,40},... | collective-permute-start | bytes 24584 | tf_op jit(solution)/shard_map/ppermute | solution.py:435
  88.9 8.7 %collective-permute-start.17 = (bf16[20,8,256]{2,1,0:T(8,128)(2,1)S(1)}, bf16[20,8,256]{2,1,0:T(8,128)(2,1)S(1)}, u32[]{:S(2)}, u32[]{:S(2)}) collective-permute-start(bf16[20,8,256]{2,1,0:T(8,128)(2,1)S(1)} %get-tuple-element.53), channel_id=1, source_target_pairs={{0,2},{1,3},{2,0},{3,1},{4,6},{5,7},{6,4},{7,5},{8,10},{9,11},{10,... | collective-permute-start | bytes 245768 | tf_op jit(solution)/shard_map/ppermute | solution.py:430
  91.0 6.6 %collective-permute-start.18 = (bf16[20,8,256]{2,1,0:T(8,128)(2,1)S(1)}, bf16[20,8,256]{2,1,0:T(8,128)(2,1)S(1)}, u32[]{:S(2)}, u32[]{:S(2)}) collective-permute-start(bf16[20,8,256]{2,1,0:T(8,128)(2,1)S(1)} %get-tuple-element.54), channel_id=1, source_target_pairs={{0,3},{1,2},{2,1},{3,0},{4,7},{5,6},{6,5},{7,4},{8,11},{9,10},{10,... | collective-permute-start | bytes 245768 | tf_op jit(solution)/shard_map/ppermute | solution.py:430
  92.9 6.1 %collective-permute-start.31 = (f32[8,256]{1,0:T(8,128)S(1)}, f32[8,256]{1,0:T(8,128)S(1)}, u32[]{:S(2)}, u32[]{:S(2)}) collective-permute-start(f32[8,256]{1,0:T(8,128)S(1)} %add_add_fusion.3), channel_id=1, source_target_pairs={{0,34},{1,35},{2,32},{3,33},{4,38},{5,39},{6,36},{7,37},{8,42},{9,... | collective-permute-start | bytes 24584 | tf_op jit(solution)/shard_map/ppermute | solution.py:553
  99.0 14.1 %collective-permute-start.34 = (f32[8,256]{1,0:T(8,128)S(1)}, f32[8,256]{1,0:T(8,128)S(1)}, u32[]{:S(2)}, u32[]{:S(2)}) collective-permute-start(f32[8,256]{1,0:T(8,128)S(1)} %add.70), channel_id=1, source_target_pairs={{0,192},{4,196},{8,200},{12,204},{16,208},{20,212},{24,216},{28,22... | collective-permute-start | bytes 24584 | tf_op jit(solution)/shard_map/ppermute | solution.py:435
  100.6 14.5 %collective-permute-start.33 = (f32[8,256]{1,0:T(8,128)S(1)}, f32[8,256]{1,0:T(8,128)S(1)}, u32[]{:S(2)}, u32[]{:S(2)}) collective-permute-start(f32[8,256]{1,0:T(8,128)S(1)} %add.70), channel_id=1, source_target_pairs={{0,128},{4,132},{8,136},{12,140},{16,144},{20,148},{24,152},{28,15... | collective-permute-start | bytes 24584 | tf_op jit(solution)/shard_map/ppermute | solution.py:435
  108.5 6.6 %collective-permute-start.32 = (f32[8,256]{1,0:T(8,128)S(1)}, f32[8,256]{1,0:T(8,128)S(1)}, u32[]{:S(2)}, u32[]{:S(2)}) collective-permute-start(f32[8,256]{1,0:T(8,128)S(1)} %add.70), channel_id=1, source_target_pairs={{0,64},{4,68},{8,72},{12,76},{16,80},{20,84},{24,88},{28,92},{32,9... | collective-permute-start | bytes 24584 | tf_op jit(solution)/shard_map/ppermute | solution.py:435
  112.1 6.2 %collective-permute-start.26 = (bf16[20,8,256]{2,1,0:T(8,128)(2,1)S(1)}, bf16[20,8,256]{2,1,0:T(8,128)(2,1)S(1)}, u32[]{:S(2)}, u32[]{:S(2)}) collective-permute-start(bf16[20,8,256]{2,1,0:T(8,128)(2,1)S(1)} %get-tuple-element.59), channel_id=1, source_target_pairs={{0,2},{1,3},{2,0},{3,1},{4,6},{5,7},{6,4},{7,5},{8,10},{9,11},{10,... | collective-permute-start | bytes 245768 | tf_op jit(solution)/shard_map/ppermute | solution.py:430
  113.2 6.3 %collective-permute-start.27 = (bf16[20,8,256]{2,1,0:T(8,128)(2,1)S(1)}, bf16[20,8,256]{2,1,0:T(8,128)(2,1)S(1)}, u32[]{:S(2)}, u32[]{:S(2)}) collective-permute-start(bf16[20,8,256]{2,1,0:T(8,128)(2,1)S(1)} %get-tuple-element.60), channel_id=1, source_target_pairs={{0,3},{1,2},{2,1},{3,0},{4,7},{5,6},{6,5},{7,4},{8,11},{9,10},{10,... | collective-permute-start | bytes 245768 | tf_op jit(solution)/shard_map/ppermute | solution.py:430
  (17 other events, 73.0 us)

commit v4 on v3

--- a/solution.py
+++ b/solution.py
@@ -151,13 +151,15 @@
     return mul(hi, xh) + (mul(lo, xh) + mul(hi, xl))
 
 
-def forward_part(src, exact, mats, avb, umat, ens3, dmats, w, hxs, norm):
-    rows = avb.shape[0]
+def smooth_rows(src, exact, mats, avb):
+    for r in range(0, avb.shape[0], GRP):
+        avb[r : r + GRP, :] = band_apply(mats, src(r), exact).astype(BF16)
+
+
+def obs_rows(avb, umat, ens3, dmats, w, dxs, norm):
     lev = 32
-    ms = rows // lev
-    for r in range(0, rows, GRP):
-        avb[r : r + GRP, :] = band_apply(mats, src(r), exact).astype(BF16)
-    for ens, d, hx in zip(ens3, dmats, hxs):
+    ms = avb.shape[0] // lev
+    for i, (ens, d) in enumerate(zip(ens3, dmats)):
         umat[...] = lax.dot_general(
             avb[...], d, (((1,), (1,)), ((), ())), preferred_element_type=F32
         )
@@ -167,45 +169,43 @@
             return acc + e * umat[pl.ds(pl.multiple_of(lev * m, lev), lev), :]
 
         dx = lax.fori_loop(0, ms, member, jnp.zeros((lev, 256), F32), unroll=4)
-        hx(
-            jnp.dot(
-                w[:, 0:lev], dx * norm, precision=lax.Precision.HIGHEST, preferred_element_type=F32
-            )
-        )
-
-
-def adjoint_part(qs, wt, mats, ens3, dmats, ua, umat, out, norm):
+        dxs[:, 256 * i : 256 * i + 256] = dx * norm
+    return jnp.dot(
+        w[:, 0:lev], dxs[...], precision=lax.Precision.HIGHEST, preferred_element_type=F32
+    )
+
+
+def adjoint_rows(q, wt, ens3, dmats, ua, norm):
+    lev = 32
+    ms = ua.shape[0] // lev
+    dxa = (
+        jnp.dot(wt[:, 0:16], q, precision=lax.Precision.HIGHEST, preferred_element_type=F32)
+        * norm
+    )
+    total = None
+    for i, (ens, d) in enumerate(zip(ens3, dmats)):
+        mine = dxa[:, 256 * i : 256 * i + 256]
+
+        def member(m, _, ens=ens, mine=mine):
+            e = ens[m].astype(F32).reshape(lev, 256)
+            ua[pl.ds(pl.multiple_of(lev * m, lev), lev), :] = (e * mine).astype(BF16)
+            return 0
+
+        lax.fori_loop(0, ms, member, 0, unroll=4)
+        part = jnp.dot(ua[...], d, preferred_element_type=F32)
+        total = part if total is None else total + part
+    return total
+
+
+def adjoint_finish(mats, umat, out):
     ms = out.shape[0]
     lev = 32
-    for r, (q, ens, d) in enumerate(zip(qs, ens3, dmats)):
-        dxa = (
-            jnp.dot(
-                wt[:, 0:16], q, precision=lax.Precision.HIGHEST, preferred_element_type=F32
-            )
-            * norm
-        )
-
-        def member(m, _):
-            e = ens[m].astype(F32).reshape(lev, 256)
-            ua[pl.ds(pl.multiple_of(lev * m, lev), lev), :] = (e * dxa).astype(BF16)
-            return 0
-
-        lax.fori_loop(0, ms, member, 0, unroll=4)
-        part = jnp.dot(ua[...], d, preferred_element_type=F32)
-        if r == 0:
-            umat[...] = part
-        else:
-            umat[...] = umat[...] + part
     five = GRP // lev
     for i in range(0, ms, five):
         got = band_apply(mats, umat[lev * i : lev * i + GRP, :], False)
         out[i : i + five] = got.reshape(five, 4, 8, 256)
 
 
-def dmats_of(d_own, x_core, x_edge):
-    return d_own[...], x_core[0:256, :], x_edge[0:256, :]
-
-
 def obs_of(x):
     return (
         join3(x[256:272, :], x[272:288, :], x[288:304, :]),
@@ -214,8 +214,8 @@
 
 
 def first_kernel(
-    norm, scal, c0, c1, c2, c3, e_own, e_core, e_edge, d_own, x_core, x_edge, bands,
-    cm, hx_core, hx_oe, w, wt, src, wsq, avb, umat,
+    norm, scal, c0, c1, c2, c3, e_own, e_core, d_own, x_core, bands,
+    cm, avb, hx_core, hx_own, w, wt, src, wsq, umat, dxs,
 ):
     share = src.shape[0]
     wsq[...] = jnp.zeros(wsq.shape, F32)
@@ -230,40 +230,41 @@
     w[...] = wsq[...].T[0:16, :]
     wt[...] = wsq[0:32, :]
 
-    def put_own(v):
-        hx_oe[0:16, :] = v
-
-    def put_core(v):
-        hx_core[...] = v
-
-    def put_edge(v):
-        hx_oe[16:32, :] = v
-
     def rows_of(r):
         five = GRP // 32
         return src[r // 32 : r // 32 + five].reshape(GRP, 256).astype(BF16)
 
-    forward_part(
-        rows_of, True, (bands[0], bands[1]), avb, umat, (e_own, e_core, e_edge),
-        dmats_of(d_own, x_core, x_edge), w, (put_own, put_core, put_edge), norm,
+    smooth_rows(rows_of, True, (bands[0], bands[1]), avb)
+    hx = obs_rows(avb, umat, (e_own, e_core), (d_own[...], x_core[0:256, :]), w, dxs, norm)
+    hx_own[...] = hx[:, 0:256]
+    hx_core[...] = hx[:, 256:512]
+
+
+def edge_kernel(norm, avb, e_edge, x_edge, w, hx_edge, umat, dxs):
+    hx_edge[...] = obs_rows(avb, umat, (e_edge,), (x_edge[0:256, :],), w, dxs, norm)
+
+
+def partial_kernel(norm, affine, h_oe, inv, inn, e_own, e_edge, d_own, x_edge, wt, out, ua):
+    ie, ye = obs_of(x_edge)
+    own, edge = h_oe[0:16, :], h_oe[16:32, :]
+    if affine:
+        own, edge = own - inn[...], edge - ye
+    q = jnp.concatenate([inv[...] * own, ie * edge], axis=1)
+    out[...] = adjoint_rows(
+        q, wt, (e_own, e_edge), (d_own[...], x_edge[0:256, :]), ua, norm
     )
 
 
 def second_kernel(
-    norm, scal, h_oe, h_core, inv, inn, cm, e_own, e_core, e_edge, d_own, x_core, x_edge,
-    bands, w, wt, s0, a0, a1, a2, a3, hx_core, hx_oe, adj, ua, umat,
+    norm, scal, part, h_core, cm, e_own, e_core, d_own, x_core, bands, w, wt, s0,
+    a0, a1, a2, a3, avb, hx_core, hx_own, adj, ua, umat, dxs,
 ):
     share = adj.shape[0]
     ic, yc = obs_of(x_core)
-    ie, ye = obs_of(x_edge)
-    qs = (
-        inv[...] * (h_oe[0:16, :] - inn[...]),
-        ic * (h_core[...] - yc),
-        ie * (h_oe[16:32, :] - ye),
-    )
-    ens3 = (e_own, e_core, e_edge)
-    dmats = dmats_of(d_own, x_core, x_edge)
-    adjoint_part(qs, wt, (bands[2], bands[3]), ens3, dmats, ua, umat, adj, norm)
+    dcore = x_core[0:256, :]
+    q = ic * (h_core[...] - yc)
+    umat[...] = part[...] + adjoint_rows(q, wt, (e_core,), (dcore,), ua, norm)
+    adjoint_finish((bands[2], bands[3]), umat, adj)
     for k, a in enumerate((a0, a1, a2, a3)):
         a[...] = adj[:, scal[1] ^ k].astype(BF16)
 
@@ -275,25 +276,16 @@
         return gg + jnp.sum(g * g, axis=0), cg + jnp.sum(c * g, axis=0)
 
     zero = jnp.zeros((8, 256), F32)
-    gg, cg = lax.fori_loop(0, share, total, (zero, zero))
-
-    def put_own(v):
-        hx_oe[0:16, :] = v
-
-    def put_core(v):
-        hx_core[0:16, :] = v
-
-    def put_edge(v):
-        hx_oe[16:32, :] = v
+    gg, cg = lax.fori_loop(0, share, total, (zero, zero), unroll=2)
 
     def rows_of(r):
         five = GRP // 32
         return adj[r // 32 : r // 32 + five].reshape(GRP, 256)
 
-    forward_part(
-        rows_of, False, (bands[0], bands[1]), ua, umat, ens3, dmats, w,
-        (put_own, put_core, put_edge), norm,
-    )
+    smooth_rows(rows_of, False, (bands[0], bands[1]), avb)
+    hx = obs_rows(avb, umat, (e_own, e_core), (d_own[...], dcore), w, dxs, norm)
+    hx_own[...] = hx[:, 0:256]
+    hx_core[0:16, :] = hx[:, 256:512]
     hx_core[16:24, :] = jnp.zeros((8, 256), F32)
     hx_core[16:17, :] = jnp.sum(s0[...], axis=0, keepdims=True)
     hx_core[17:18, :] = jnp.sum(gg, axis=0, keepdims=True)
@@ -320,28 +312,30 @@
 
 
 def third_kernel(
-    norm, scal, h_oe, h_core, inv, e_own, e_core, e_edge, d_own, x_core, x_edge,
-    bands, wt, a0, a1, a2, a3, adj, ua, umat,
+    norm, scal, part, h_core, e_core, x_core, bands, wt, a0, a1, a2, a3, adj, ua, umat
 ):
     ic, _ = obs_of(x_core)
-    ie, _ = obs_of(x_edge)
-    qs = (inv[...] * h_oe[0:16, :], ic * h_core[...], ie * h_oe[16:32, :])
-    adjoint_part(
-        qs, wt, (bands[2], bands[3]), (e_own, e_core, e_edge), dmats_of(d_own, x_core, x_edge),
-        ua, umat, adj, norm,
-    )
+    umat[...] = part[...] + adjoint_rows(
+        ic * h_core[...], wt, (e_core,), (x_core[0:256, :],), ua, norm
+    )
+    adjoint_finish((bands[2], bands[3]), umat, adj)
     for k, a in enumerate((a0, a1, a2, a3)):
         a[...] = adj[:, scal[1] ^ k].astype(BF16)
 
 
 def grad_first_kernel(scal, ctl, a0, a1, a2, a3, out, buf, sems):
     share = a0.shape[0]
+    few = share // 4
     copies = []
     for k, a in enumerate((a0, a1, a2, a3)):
-        at = pl.ds(share * (scal[2] ^ k), share)
-        buf[k] = ctl[at] + a[...].astype(F32)
-        copies.append(pltpu.make_async_copy(buf.at[k], out.at[at], sems.at[k]))
-        copies[k].start()
+        for i in range(4):
+            here = pl.ds(few * i, few)
+            at = pl.ds(share * (scal[2] ^ k) + few * i, few)
+            buf[k, here] = ctl[at] + a[here].astype(F32)
+            copies.append(
+                pltpu.make_async_copy(buf.at[k, here], out.at[at], sems.at[4 * k + i])
+            )
+            copies[-1].start()
     for c in copies:
         c.wait()
 
@@ -360,19 +354,17 @@
     tb = jnp.broadcast_to(tau, (8, 256))
     share = a0.shape[0]
     copies = []
+    few = share // 4
     for k, (a, b) in enumerate(zip((a0, a1, a2, a3), (b0, b1, b2, b3))):
-        base = share * (scal[2] ^ k)
-
-        def body(m, _, a=a, b=b, k=k, base=base):
-            g = ctl[base + m] + a[m].astype(F32)
-            buf[k, m] = g - tb * (g + b[m].astype(F32))
-            return 0
-
-        lax.fori_loop(0, share, body, 0, unroll=5)
-        copies.append(
-            pltpu.make_async_copy(buf.at[k], out.at[pl.ds(base, share)], sems.at[k])
-        )
-        copies[k].start()
+        for i in range(4):
+            here = pl.ds(few * i, few)
+            at = pl.ds(share * (scal[2] ^ k) + few * i, few)
+            g = ctl[at] + a[here].astype(F32)
+            buf[k, here] = g - tb * (g + b[here].astype(F32))
+            copies.append(
+                pltpu.make_async_copy(buf.at[k, here], out.at[at], sems.at[4 * k + i])
+            )
+            copies[-1].start()
     costs[0] = first[0, 0]
     costs[1] = (second / count)[0, 0]
     for c in copies:
@@ -486,51 +478,65 @@
     half = pltpu.VMEM((rows, pdev), BF16)
     full = pltpu.VMEM((share, levs, ldev, pdev), F32)
     obs = channel_weights.shape[0]
-    mm = 2 * rows * pdev * pdev * 3
-
-    def bind(fn, arg):
-        def body(*refs):
-            fn(arg, *refs)
-
-        return body
-
-    cm, hx_core, hx_oe, w, wt = call(
+    mm = 2 * rows * pdev * pdev
+    row = sds((obs, pdev), F32)
+    flat = sds((rows, pdev), BF16)
+    wide = sds((rows, pdev), F32)
+
+    def bind(fn, *given):
+        def kernel(*refs):
+            fn(*given, *refs)
+
+        return kernel
+
+    cm, avb, hx_core, hx_own, w, wt = call(
         bind(first_kernel, norm),
-        [
-            field, sds((obs, pdev), F32), sds((2 * obs, pdev), F32),
-            sds((obs, 128), F32), sds((lev, 128), F32),
-        ],
-        (scal, *cparts, e_own, e_core, e_edge, d_own, x_core, x_edge, bands),
+        [field, flat, row, row, sds((obs, 128), F32), sds((lev, 128), F32)],
+        (scal, *cparts, e_own, e_core, d_own, x_core, bands),
         1,
-        [full, pltpu.VMEM((128, 128), F32), half, umat],
-        mm,
-    )
-
-    def reduce_obs(core_msg, oe):
+        [full, pltpu.VMEM((128, 128), F32), umat, pltpu.VMEM((lev, 2 * pdev), F32)],
+        3 * mm,
+    )
+
+    def reduce_obs(tag, core_msg, own, smooth):
         got = swap_core(core_msg)
-        mine = jnp.concatenate([oe[:obs] + got[:obs], oe[obs:]], axis=0)
+        (edge_row,) = call(
+            bind(edge_kernel, norm),
+            [row],
+            (smooth, e_edge, x_edge, w),
+            0,
+            [umat, pltpu.VMEM((lev, pdev), F32)],
+            mm,
+        )
+        mine = jnp.concatenate([own + got[:obs], edge_row], axis=0)
         other = swap_edge(mine)
         tot = mine + jnp.concatenate([other[obs:], other[:obs]], axis=0)
         if core_msg.shape[0] > obs:
             extra = core_msg[obs:] + got[obs:]
             tot = jnp.concatenate([tot, extra], axis=0)
         tot = sum4(tot, "lev", lev_xor, (1, 2, 3))
-        return tot, swap_core(tot[:obs])
-
-    h1_oe, h1_core = reduce_obs(hx_core, hx_oe)
+        core = swap_core(tot[:obs])
+        (part,) = call(
+            bind(partial_kernel, norm, tag == "a"),
+            [wide],
+            (tot, inv_error, innovation, e_own, e_edge, d_own, x_edge, wt),
+            0,
+            [half],
+            2 * mm,
+        )
+        return tot, core, part
+
+    h1_oe, h1_core, part = reduce_obs("a", hx_core, hx_own, avb)
     outs = call(
         bind(second_kernel, norm),
-        [chunk] * 4 + [sds((obs + 8, pdev), F32), sds((2 * obs, pdev), F32)],
-        (
-            scal, h1_oe, h1_core, inv_error, innovation, cm, e_own, e_core, e_edge,
-            d_own, x_core, x_edge, bands, w, wt, s0,
-        ),
+        [chunk] * 4 + [flat, sds((obs + 8, pdev), F32), row],
+        (scal, part, h1_core, cm, e_own, e_core, d_own, x_core, bands, w, wt, s0),
         1,
-        [full, half, umat],
-        2 * mm,
+        [full, half, umat, pltpu.VMEM((lev, 2 * pdev), F32)],
+        6 * mm,
     )
     aparts = shuffle(outs[:4])
-    hs, hd_core = reduce_obs(outs[4], outs[5])
+    hs, hd_core, part = reduce_obs("b", outs[5], outs[6], outs[4])
     sums = call(
         sums_kernel,
         [sds((8, pdev), F32)],
@@ -540,21 +546,20 @@
     bparts = call(
         bind(third_kernel, norm),
         [chunk] * 4,
-        (
-            scal, hs, hd_core, inv_error, e_own, e_core, e_edge, d_own, x_core, x_edge,
-            bands, wt,
-        ),
+        (scal, part, hd_core, e_core, x_core, bands, wt),
         1,
         [full, half, umat],
-        mm,
+        3 * mm,
     )
     bparts = shuffle(bparts)
-    sums = sum4(sums, "tile", tile_xor, (2, 4, 6))
+    sums = sums + lax.ppermute(sums, "tile", tile_xor(2))
+    sums = sums + lax.ppermute(sums, "tile", tile_xor(6))
     sums = sums + lax.ppermute(sums, both, far)
-    sums = sum4(sums, "tile", tile_xor, (16, 32, 48))
+    sums = sums + lax.ppermute(sums, "tile", tile_xor(16))
+    sums = sums + lax.ppermute(sums, "tile", tile_xor(48))
     whole = sds((members, ldev, pdev), F32)
     anywhere = pl.BlockSpec(memory_space=pl.ANY)
-    outbuf = [pltpu.VMEM((4, share, ldev, pdev), F32), pltpu.SemaphoreType.DMA((4,))]
+    outbuf = [pltpu.VMEM((4, share, ldev, pdev), F32), pltpu.SemaphoreType.DMA((16,))]
     (grad_first,) = call(
         grad_first_kernel, [whole], (scal, control, *aparts), 1, outbuf,
         out_specs=(anywhere,),

time: 123 us -> 115 us (0.935)
  waiting for transfers between devices: 54.8 us -> 48.9 us
  starting transfers between devices: 48.3 us -> 46.5 us
    ppermute x12 -> x6, starting transfers between devices: 21.6 us -> 8.09 us  [sum4(): one, two, three = (lax.ppermute(x, axis, pairs(k)) for k in steps)]
    ppermute x12, waiting for transfers between devices: 25 us -> 14.8 us  [shuffle(): lax.ppermute(parts[k], 'lev', lev_xor(k))]
    ppermute x0 -> x4, waiting for transfers between devices: none -> 8.25 us  [the longest x1 3.64 us: per_device(): sums = sums + lax.ppermute(sums, 'tile', tile_xor(2))]
    ppermute x0 -> x4, starting transfers between devices: none -> 6.65 us  [the longest x1 6.56 us: per_device(): sums = sums + lax.ppermute(sums, 'tile', tile_xor(16))]
    ppermute x4, starting transfers between devices: 7.28 us -> 12.5 us  [swap_edge(): return lax.ppermute(x, both, edge)]
    ppermute x1, waiting for transfers between devices: 0.01 us -> 5.01 us  [per_device(): sums = sums + lax.ppermute(sums, both, far)]
    ppermute x4, waiting for transfers between devices: 18.2 us -> 14.3 us  [swap_edge(): return lax.ppermute(x, both, edge)]
    ppermute x6, waiting for transfers between devices: 4.58 us -> 1.73 us  [swap_core(): return lax.ppermute(x, 'tile', tile_xor(1))]
  transfers between devices with their start and end apart: 35 -> 33, of which waited for: 22 -> 17; matrix products, arithmetic and copies ran while one was open for 0% -> 0% of each run, Pallas kernels for 5% -> 9%
where the time goes in v4:
time: 115 us
  waiting for transfers between devices  48.9 us (43%)
  starting transfers between devices  46.5 us (40%)
  Pallas kernels  17.2 us (15%)
    ppermute x12, starting transfers between devices, shuffle(): lax.ppermute(parts[k], 'lev', lev_xor(k))  18.6 us
    pallas_call x14, Pallas kernels, call(): pl.pallas_call(body, out_shape=tuple(outs), in_specs=specs, out_specs=out...  17.2 us
    ppermute x12, waiting for transfers between devices, shuffle(): lax.ppermute(parts[k], 'lev', lev_xor(k))  14.8 us
    ppermute x4, waiting for transfers between devices, swap_edge(): return lax.ppermute(x, both, edge)  14.3 us
    ppermute x4, starting transfers between devices, swap_edge(): return lax.ppermute(x, both, edge)  12.5 us
    ppermute x6, starting transfers between devices, sum4(): one, two, three = (lax.ppermute(x, axis, pairs(k)) for k in steps)  8.09 us
    ppermute x1, starting transfers between devices, per_device(): sums = sums + lax.ppermute(sums, 'tile', tile_xor(16))  6.56 us
    ppermute x1, waiting for transfers between devices, per_device(): sums = sums + lax.ppermute(sums, both, far)  5.01 us
  transfers between devices with their start and end apart: 33, of which 17 were waited for; matrix products, arithmetic and copies ran while one was open for 0% of the time, Pallas kernels for 9%

profile of v4, /device:TPU:2, one launch (start us, length us, event | category | flops | bytes accessed | tf_op | source)
XLA Modules:
  0.0 115.0 jit_solution(4079606223396605118)
XLA Ops:
  2.3 2.0 %collective-permute-start.3 = (bf16[20,8,256]{2,1,0:T(8,128)(2,1)S(1)}, bf16[20,8,256]{2,1,0:T(8,128)(2,1)S(1)}, u32[]{:S(2)}, u32[]{:S(2)}) collective-permute-start(bf16[20,8,256]{2,1,0:T(8,128)(2,1)S(1)} %get-tuple-element.40), channel_id=1, source_target_pairs={{0,1},{1,0},{2,3},{3,2},{4,5},{5,4},{6,7},{7,6},{8,9},{9,8},{10,11... | collective-permute-start | bytes 245768 | tf_op jit(solution)/shard_map/ppermute | solution.py:422
  4.3 3.3 %collective-permute-start.4 = (bf16[20,8,256]{2,1,0:T(8,128)(2,1)S(1)}, bf16[20,8,256]{2,1,0:T(8,128)(2,1)S(1)}, u32[]{:S(2)}, u32[]{:S(2)}) collective-permute-start(bf16[20,8,256]{2,1,0:T(8,128)(2,1)S(1)} %get-tuple-element.41), channel_id=1, source_target_pairs={{0,2},{1,3},{2,0},{3,1},{4,6},{5,7},{6,4},{7,5},{8,10},{9,11},{10,... | collective-permute-start | bytes 245768 | tf_op jit(solution)/shard_map/ppermute | solution.py:422
  7.6 6.5 %collective-permute-done.4.e2 = bf16[20,8,256]{2,1,0:T(8,128)(2,1)S(1)} collective-permute-done((bf16[20,8,256]{2,1,0:T(8,128)(2,1)S(1)}, bf16[20,8,256]{2,1,0:T(8,128)(2,1)S(1)}, u32[]{:S(2)}, u32[]{:S(2)}) %collective-permute-start.4) | collective-permute-done | bytes 81952 | tf_op jit(solution)/shard_map/ppermute | solution.py:422
  14.8 7.8 %collective-permute-start.9 = (bf16[20,4,8,256]{3,2,1,0:T(8,128)(2,1)S(1)}, bf16[20,4,8,256]{3,2,1,0:T(8,128)(2,1)S(1)}, u32[]{:S(2)}, u32[]{:S(2)}) collective-permute-start(bf16[20,4,8,256]{3,2,1,0:T(8,128)(2,1)S(1)} %shard_map.105.refs_5_.refs_3_.refs_4_), channel_id=1, source_target_pairs={{0,254},{1,255},{2,252},{3,253},{4,8},{5,9},{6,10},{7,11},{8,4},{9... | collective-permute-start | bytes 983048 | tf_op jit(solution)/shard_map/ppermute | solution.py:418
  24.0 1.9 %collective-permute-start.1 = (bf16[23,8,256]{2,1,0:T(8,128)(2,1)S(1)}, bf16[23,8,256]{2,1,0:T(8,128)(2,1)S(1)}, u32[]{:S(2)}, u32[]{:S(2)}) collective-permute-start(bf16[23,8,256]{2,1,0:T(8,128)(2,1)S(1)} %get-tuple-element.37), channel_id=1, source_target_pairs={{0,2},{1,3},{2,0},{3,1},{4,6},{5,7},{6,4},{7,5},{8,10},{9,11},{10,... | collective-permute-start | bytes 282632 | tf_op jit(solution)/shard_map/ppermute | solution.py:422
  30.7 1.9 %collective-permute-start.2 = (bf16[23,8,256]{2,1,0:T(8,128)(2,1)S(1)}, bf16[23,8,256]{2,1,0:T(8,128)(2,1)S(1)}, u32[]{:S(2)}, u32[]{:S(2)}) collective-permute-start(bf16[23,8,256]{2,1,0:T(8,128)(2,1)S(1)} %get-tuple-element.38), channel_id=1, source_target_pairs={{0,3},{1,2},{2,1},{3,0},{4,7},{5,6},{6,5},{7,4},{8,11},{9,10},{10,... | collective-permute-start | bytes 282632 | tf_op jit(solution)/shard_map/ppermute | solution.py:422
  32.6 5.9 %collective-permute-done.2.refs_4_ = bf16[23,8,256]{2,1,0:T(8,128)(2,1)S(1)} collective-permute-done((bf16[23,8,256]{2,1,0:T(8,128)(2,1)S(1)}, bf16[23,8,256]{2,1,0:T(8,128)(2,1)S(1)}, u32[]{:S(2)}, u32[]{:S(2)}) %collective-permute-start.2) | collective-permute-done | bytes 94240 | tf_op jit(solution)/shard_map/ppermute | solution.py:422
  41.8 2.8 %collective-permute-start.11 = (f32[32,256]{1,0:T(8,128)S(1)}, f32[32,256]{1,0:T(8,128)S(1)}, u32[]{:S(2)}, u32[]{:S(2)}) collective-permute-start(f32[32,256]{1,0:T(8,128)S(1)} %pad_maximum_fusion.1), channel_id=1, source_target_pairs={{0,254},{1,255},{2,252},{3,253},{4,8},{5,9},{6,10},{7,11},{8,4},{9... | collective-permute-start | bytes 98312 | tf_op jit(solution)/shard_map/ppermute | solution.py:418
  44.7 5.7 %collective-permute-done.11 = f32[32,256]{1,0:T(8,128)S(1)} collective-permute-done((f32[32,256]{1,0:T(8,128)S(1)}, f32[32,256]{1,0:T(8,128)S(1)}, u32[]{:S(2)}, u32[]{:S(2)}) %collective-permute-start.11) | collective-permute-done | bytes 32800 | tf_op jit(solution)/shard_map/ppermute | solution.py:418
  50.4 2.0 %collective-permute-start.14 = (f32[32,256]{1,0:T(8,128)S(1)}, f32[32,256]{1,0:T(8,128)S(1)}, u32[]{:S(2)}, u32[]{:S(2)}) collective-permute-start(f32[32,256]{1,0:T(8,128)S(1)} %maximum_add_fusion), channel_id=1, source_target_pairs={{0,3},{1,2},{2,1},{3,0},{4,7},{5,6},{6,5},{7,4},{8,11},{9,10},{10,... | collective-permute-start | bytes 98312 | tf_op jit(solution)/shard_map/ppermute | solution.py:427
  52.4 2.5 %collective-permute-start.12 = (f32[32,256]{1,0:T(8,128)S(1)}, f32[32,256]{1,0:T(8,128)S(1)}, u32[]{:S(2)}, u32[]{:S(2)}) collective-permute-start(f32[32,256]{1,0:T(8,128)S(1)} %maximum_add_fusion), channel_id=1, source_target_pairs={{0,1},{1,0},{2,3},{3,2},{4,5},{5,4},{6,7},{7,6},{8,9},{9,8},{10,11... | collective-permute-start | bytes 98312 | tf_op jit(solution)/shard_map/ppermute | solution.py:427
  58.7 3.0 %shard_map.110 = (bf16[20,8,256]{2,1,0:T(8,128)(2,1)S(1)}, bf16[20,8,256]{2,1,0:T(8,128)(2,1)S(1)}, bf16[20,8,256]{2,1,0:T(8,128)(2,1)S(1)}, bf16[20,8,256]{2,1,...) custom-call(s32[4]{0:T(128)S(1)} %pad_add_fusion.scal.refs_0_, ...), custom_call_target="tpu_custom_call" | custom-call | flops 503316480 | bytes 2899984 | tf_op jit(solution)/shard_map/pallas_call | solution.py:28
  64.5 7.5 %collective-permute-done.20 = f32[32,256]{1,0:T(8,128)S(1)} collective-permute-done((f32[32,256]{1,0:T(8,128)S(1)}, f32[32,256]{1,0:T(8,128)S(1)}, u32[]{:S(2)}, u32[]{:S(2)}) %collective-permute-start.20) | collective-permute-done | bytes 32800 | tf_op jit(solution)/shard_map/ppermute | solution.py:418
  72.0 2.0 %collective-permute-start.22 = (f32[40,256]{1,0:T(8,128)S(1)}, f32[40,256]{1,0:T(8,128)S(1)}, u32[]{:S(2)}, u32[]{:S(2)}) collective-permute-start(f32[40,256]{1,0:T(8,128)S(1)} %pad_maximum_fusion), channel_id=1, source_target_pairs={{0,2},{1,3},{2,0},{3,1},{4,6},{5,7},{6,4},{7,5},{8,10},{9,11},{10,... | collective-permute-start | bytes 122888 | tf_op jit(solution)/shard_map/ppermute | solution.py:427
  75.7 2.0 %collective-permute-start.16 = (bf16[20,8,256]{2,1,0:T(8,128)(2,1)S(1)}, bf16[20,8,256]{2,1,0:T(8,128)(2,1)S(1)}, u32[]{:S(2)}, u32[]{:S(2)}) collective-permute-start(bf16[20,8,256]{2,1,0:T(8,128)(2,1)S(1)} %get-tuple-element.55), channel_id=1, source_target_pairs={{0,1},{1,0},{2,3},{3,2},{4,5},{5,4},{6,7},{7,6},{8,9},{9,8},{10,11... | collective-permute-start | bytes 245768 | tf_op jit(solution)/shard_map/ppermute | solution.py:422
  77.7 2.3 %collective-permute-done.23 = f32[40,256]{1,0:T(8,128)S(1)} collective-permute-done((f32[40,256]{1,0:T(8,128)S(1)}, f32[40,256]{1,0:T(8,128)S(1)}, u32[]{:S(2)}, u32[]{:S(2)}) %collective-permute-start.23) | collective-permute-done | bytes 40992 | tf_op jit(solution)/shard_map/ppermute | solution.py:427
  81.5 3.6 %collective-permute-done.28 = f32[8,256]{1,0:T(8,128)S(1)} collective-permute-done((f32[8,256]{1,0:T(8,128)S(1)}, f32[8,256]{1,0:T(8,128)S(1)}, u32[]{:S(2)}, u32[]{:S(2)}) %collective-permute-start.28) | collective-permute-done | bytes 8224 | tf_op jit(solution)/shard_map/ppermute | solution.py:555
  87.5 2.5 %collective-permute-done.29 = f32[8,256]{1,0:T(8,128)S(1)} collective-permute-done((f32[8,256]{1,0:T(8,128)S(1)}, f32[8,256]{1,0:T(8,128)S(1)}, u32[]{:S(2)}, u32[]{:S(2)}) %collective-permute-start.29) | collective-permute-done | bytes 8224 | tf_op jit(solution)/shard_map/ppermute | solution.py:556
  90.8 5.0 %collective-permute-done.30 = f32[8,256]{1,0:T(8,128)S(1)} collective-permute-done((f32[8,256]{1,0:T(8,128)S(1)}, f32[8,256]{1,0:T(8,128)S(1)}, u32[]{:S(2)}, u32[]{:S(2)}) %collective-permute-start.30) | collective-permute-done | bytes 8224 | tf_op jit(solution)/shard_map/ppermute | solution.py:557
  95.8 6.6 %collective-permute-start.31 = (f32[8,256]{1,0:T(8,128)S(1)}, f32[8,256]{1,0:T(8,128)S(1)}, u32[]{:S(2)}, u32[]{:S(2)}) collective-permute-start(f32[8,256]{1,0:T(8,128)S(1)} %add.63), channel_id=1, source_target_pairs={{0,64},{4,68},{8,72},{12,76},{16,80},{20,84},{24,88},{28,92},{32,9... | collective-permute-start | bytes 24584 | tf_op jit(solution)/shard_map/ppermute | solution.py:558
  104.0 2.4 %collective-permute-start.26 = (bf16[20,8,256]{2,1,0:T(8,128)(2,1)S(1)}, bf16[20,8,256]{2,1,0:T(8,128)(2,1)S(1)}, u32[]{:S(2)}, u32[]{:S(2)}) collective-permute-start(bf16[20,8,256]{2,1,0:T(8,128)(2,1)S(1)} %get-tuple-element.63), channel_id=1, source_target_pairs={{0,2},{1,3},{2,0},{3,1},{4,6},{5,7},{6,4},{7,5},{8,10},{9,11},{10,... | collective-permute-start | bytes 245768 | tf_op jit(solution)/shard_map/ppermute | solution.py:422
  106.4 1.9 %collective-permute-start.27 = (bf16[20,8,256]{2,1,0:T(8,128)(2,1)S(1)}, bf16[20,8,256]{2,1,0:T(8,128)(2,1)S(1)}, u32[]{:S(2)}, u32[]{:S(2)}) collective-permute-start(bf16[20,8,256]{2,1,0:T(8,128)(2,1)S(1)} %get-tuple-element.64), channel_id=1, source_target_pairs={{0,3},{1,2},{2,1},{3,0},{4,7},{5,6},{6,5},{7,4},{8,11},{9,10},{10,... | collective-permute-start | bytes 245768 | tf_op jit(solution)/shard_map/ppermute | solution.py:422
  109.9 2.1 %collective-permute-done.32 = f32[8,256]{1,0:T(8,128)S(1)} collective-permute-done((f32[8,256]{1,0:T(8,128)S(1)}, f32[8,256]{1,0:T(8,128)S(1)}, u32[]{:S(2)}, u32[]{:S(2)}) %collective-permute-start.32) | collective-permute-done | bytes 8224 | tf_op jit(solution)/shard_map/ppermute | solution.py:559
  112.7 2.1 %shard_map.116 = (f32[80,8,256]{2,1,0:T(8,128)}, f32[2]{0:T(128)}) custom-call(s32[4]{0:T(128)S(1)} %pad_add_fusion.scal.refs_0_, f32[80,8,256]{2,1,0:T(8,128)S(1)} %copy-done, bf16[20,8,256]{2,1,0:T(8,128)(2,1)S(1)} %get-tuple-element.54.a0.refs_2_, bf16[20,8,256]{2,1,0:T(8,128)(2,1)S(1)} %collective-permute-done.16.a1.refs_3_, ...), custom_call_target="tpu_custom_call" | custom-call | bytes 1974296 | tf_op jit(solution)/shard_map/pallas_call | solution.py:28
  (91 shorter events, 28.6 us)
Async XLA Ops:
  2.3 5.3 %collective-permute-start.3 = (bf16[20,8,256]{2,1,0:T(8,128)(2,1)S(1)}, bf16[20,8,256]{2,1,0:T(8,128)(2,1)S(1)}, u32[]{:S(2)}, u32[]{:S(2)}) collective-permute-start(bf16[20,8,256]{2,1,0:T(8,128)(2,1)S(1)} %get-tuple-element.40), channel_id=1, source_target_pairs={{0,1},{1,0},{2,3},{3,2},{4,5},{5,4},{6,7},{7,6},{8,9},{9,8},{10,11... | collective-permute-start | bytes 245768 | tf_op jit(solution)/shard_map/ppermute | solution.py:422
  4.3 9.8 %collective-permute-start.4 = (bf16[20,8,256]{2,1,0:T(8,128)(2,1)S(1)}, bf16[20,8,256]{2,1,0:T(8,128)(2,1)S(1)}, u32[]{:S(2)}, u32[]{:S(2)}) collective-permute-start(bf16[20,8,256]{2,1,0:T(8,128)(2,1)S(1)} %get-tuple-element.41), channel_id=1, source_target_pairs={{0,2},{1,3},{2,0},{3,1},{4,6},{5,7},{6,4},{7,5},{8,10},{9,11},{10,... | collective-permute-start | bytes 245768 | tf_op jit(solution)/shard_map/ppermute | solution.py:422
  7.6 6.5 %collective-permute-start.5 = (bf16[20,8,256]{2,1,0:T(8,128)(2,1)S(1)}, bf16[20,8,256]{2,1,0:T(8,128)(2,1)S(1)}, u32[]{:S(2)}, u32[]{:S(2)}) collective-permute-start(bf16[20,8,256]{2,1,0:T(8,128)(2,1)S(1)} %get-tuple-element.42), channel_id=1, source_target_pairs={{0,3},{1,2},{2,1},{3,0},{4,7},{5,6},{6,5},{7,4},{8,11},{9,10},{10,... | collective-permute-start | bytes 245768 | tf_op jit(solution)/shard_map/ppermute | solution.py:422
  14.7 23.8 %collective-permute-start.6 = (bf16[20,4,8,256]{3,2,1,0:T(8,128)(2,1)S(1)}, bf16[20,4,8,256]{3,2,1,0:T(8,128)(2,1)S(1)}, u32[]{:S(2)}, u32[]{:S(2)}) collective-permute-start(bf16[20,4,8,256]{3,2,1,0:T(8,128)(2,1)S(1)} %shard_map.105.refs_5_.refs_3_.refs_4_), channel_id=1, source_target_pairs={{0,4},{4,0},{8,12},{12,8},{16,20},{20,16},{24,28},{28,24},{32,36},... | collective-permute-start | bytes 983048 | tf_op jit(solution)/shard_map/ppermute | solution.py:415
  14.8 26.5 %collective-permute-start.9 = (bf16[20,4,8,256]{3,2,1,0:T(8,128)(2,1)S(1)}, bf16[20,4,8,256]{3,2,1,0:T(8,128)(2,1)S(1)}, u32[]{:S(2)}, u32[]{:S(2)}) collective-permute-start(bf16[20,4,8,256]{3,2,1,0:T(8,128)(2,1)S(1)} %shard_map.105.refs_5_.refs_3_.refs_4_), channel_id=1, source_target_pairs={{0,254},{1,255},{2,252},{3,253},{4,8},{5,9},{6,10},{7,11},{8,4},{9... | collective-permute-start | bytes 983048 | tf_op jit(solution)/shard_map/ppermute | solution.py:418
  23.3 7.0 %collective-permute-start = (bf16[23,8,256]{2,1,0:T(8,128)(2,1)S(1)}, bf16[23,8,256]{2,1,0:T(8,128)(2,1)S(1)}, u32[]{:S(2)}, u32[]{:S(2)}) collective-permute-start(bf16[23,8,256]{2,1,0:T(8,128)(2,1)S(1)} %get-tuple-element.36), channel_id=1, source_target_pairs={{0,1},{1,0},{2,3},{3,2},{4,5},{5,4},{6,7},{7,6},{8,9},{9,8},{10,11... | collective-permute-start | bytes 282632 | tf_op jit(solution)/shard_map/ppermute | solution.py:422
  24.0 6.7 %collective-permute-start.1 = (bf16[23,8,256]{2,1,0:T(8,128)(2,1)S(1)}, bf16[23,8,256]{2,1,0:T(8,128)(2,1)S(1)}, u32[]{:S(2)}, u32[]{:S(2)}) collective-permute-start(bf16[23,8,256]{2,1,0:T(8,128)(2,1)S(1)} %get-tuple-element.37), channel_id=1, source_target_pairs={{0,2},{1,3},{2,0},{3,1},{4,6},{5,7},{6,4},{7,5},{8,10},{9,11},{10,... | collective-permute-start | bytes 282632 | tf_op jit(solution)/shard_map/ppermute | solution.py:422
  28.3 10.1 %collective-permute-start.7 = (bf16[352,256]{1,0:T(8,128)(2,1)S(1)}, bf16[352,256]{1,0:T(8,128)(2,1)S(1)}, u32[]{:S(2)}, u32[]{:S(2)}) collective-permute-start(bf16[352,256]{1,0:T(8,128)(2,1)S(1)} %get-tuple-element.44), channel_id=1, source_target_pairs={{0,4},{4,0},{8,12},{12,8},{16,20},{20,16},{24,28},{28,24},{32,36},... | collective-permute-start | bytes 540680 | tf_op jit(solution)/shard_map/ppermute | solution.py:415
  30.2 11.0 %collective-permute-start.10 = (bf16[352,256]{1,0:T(8,128)(2,1)S(1)}, bf16[352,256]{1,0:T(8,128)(2,1)S(1)}, u32[]{:S(2)}, u32[]{:S(2)}) collective-permute-start(bf16[352,256]{1,0:T(8,128)(2,1)S(1)} %get-tuple-element.49), channel_id=1, source_target_pairs={{0,254},{1,255},{2,252},{3,253},{4,8},{5,9},{6,10},{7,11},{8,4},{9... | collective-permute-start | bytes 540680 | tf_op jit(solution)/shard_map/ppermute | solution.py:418
  30.7 7.8 %collective-permute-start.2 = (bf16[23,8,256]{2,1,0:T(8,128)(2,1)S(1)}, bf16[23,8,256]{2,1,0:T(8,128)(2,1)S(1)}, u32[]{:S(2)}, u32[]{:S(2)}) collective-permute-start(bf16[23,8,256]{2,1,0:T(8,128)(2,1)S(1)} %get-tuple-element.38), channel_id=1, source_target_pairs={{0,3},{1,2},{2,1},{3,0},{4,7},{5,6},{6,5},{7,4},{8,11},{9,10},{10,... | collective-permute-start | bytes 282632 | tf_op jit(solution)/shard_map/ppermute | solution.py:422
  41.8 8.5 %collective-permute-start.11 = (f32[32,256]{1,0:T(8,128)S(1)}, f32[32,256]{1,0:T(8,128)S(1)}, u32[]{:S(2)}, u32[]{:S(2)}) collective-permute-start(f32[32,256]{1,0:T(8,128)S(1)} %pad_maximum_fusion.1), channel_id=1, source_target_pairs={{0,254},{1,255},{2,252},{3,253},{4,8},{5,9},{6,10},{7,11},{8,4},{9... | collective-permute-start | bytes 98312 | tf_op jit(solution)/shard_map/ppermute | solution.py:418
  50.4 5.8 %collective-permute-start.14 = (f32[32,256]{1,0:T(8,128)S(1)}, f32[32,256]{1,0:T(8,128)S(1)}, u32[]{:S(2)}, u32[]{:S(2)}) collective-permute-start(f32[32,256]{1,0:T(8,128)S(1)} %maximum_add_fusion), channel_id=1, source_target_pairs={{0,3},{1,2},{2,1},{3,0},{4,7},{5,6},{6,5},{7,4},{8,11},{9,10},{10,... | collective-permute-start | bytes 98312 | tf_op jit(solution)/shard_map/ppermute | solution.py:427
  63.0 9.0 %collective-permute-start.20 = (f32[32,256]{1,0:T(8,128)S(1)}, f32[32,256]{1,0:T(8,128)S(1)}, u32[]{:S(2)}, u32[]{:S(2)}) collective-permute-start(f32[32,256]{1,0:T(8,128)S(1)} %pad_maximum_fusion.2), channel_id=1, source_target_pairs={{0,254},{1,255},{2,252},{3,253},{4,8},{5,9},{6,10},{7,11},{8,4},{9... | collective-permute-start | bytes 98312 | tf_op jit(solution)/shard_map/ppermute | solution.py:418
  72.0 5.6 %collective-permute-start.22 = (f32[40,256]{1,0:T(8,128)S(1)}, f32[40,256]{1,0:T(8,128)S(1)}, u32[]{:S(2)}, u32[]{:S(2)}) collective-permute-start(f32[40,256]{1,0:T(8,128)S(1)} %pad_maximum_fusion), channel_id=1, source_target_pairs={{0,2},{1,3},{2,0},{3,1},{4,6},{5,7},{6,4},{7,5},{8,10},{9,11},{10,... | collective-permute-start | bytes 122888 | tf_op jit(solution)/shard_map/ppermute | solution.py:427
  74.0 5.9 %collective-permute-start.23 = (f32[40,256]{1,0:T(8,128)S(1)}, f32[40,256]{1,0:T(8,128)S(1)}, u32[]{:S(2)}, u32[]{:S(2)}) collective-permute-start(f32[40,256]{1,0:T(8,128)S(1)} %pad_maximum_fusion), channel_id=1, source_target_pairs={{0,3},{1,2},{2,1},{3,0},{4,7},{5,6},{6,5},{7,4},{8,11},{9,10},{10,... | collective-permute-start | bytes 122888 | tf_op jit(solution)/shard_map/ppermute | solution.py:427
  75.7 28.3 %collective-permute-start.16 = (bf16[20,8,256]{2,1,0:T(8,128)(2,1)S(1)}, bf16[20,8,256]{2,1,0:T(8,128)(2,1)S(1)}, u32[]{:S(2)}, u32[]{:S(2)}) collective-permute-start(bf16[20,8,256]{2,1,0:T(8,128)(2,1)S(1)} %get-tuple-element.55), channel_id=1, source_target_pairs={{0,1},{1,0},{2,3},{3,2},{4,5},{5,4},{6,7},{7,6},{8,9},{9,8},{10,11... | collective-permute-start | bytes 245768 | tf_op jit(solution)/shard_map/ppermute | solution.py:422
  85.2 4.9 %collective-permute-start.29 = (f32[8,256]{1,0:T(8,128)S(1)}, f32[8,256]{1,0:T(8,128)S(1)}, u32[]{:S(2)}, u32[]{:S(2)}) collective-permute-start(f32[8,256]{1,0:T(8,128)S(1)} %add.61), channel_id=1, source_target_pairs={{0,24},{4,28},{8,16},{12,20},{16,8},{20,12},{24,0},{28,4},{32,56},... | collective-permute-start | bytes 24584 | tf_op jit(solution)/shard_map/ppermute | solution.py:556
  85.2 23.2 %collective-permute-start.17 = (bf16[20,8,256]{2,1,0:T(8,128)(2,1)S(1)}, bf16[20,8,256]{2,1,0:T(8,128)(2,1)S(1)}, u32[]{:S(2)}, u32[]{:S(2)}) collective-permute-start(bf16[20,8,256]{2,1,0:T(8,128)(2,1)S(1)} %get-tuple-element.56), channel_id=1, source_target_pairs={{0,2},{1,3},{2,0},{3,1},{4,6},{5,7},{6,4},{7,5},{8,10},{9,11},{10,... | collective-permute-start | bytes 245768 | tf_op jit(solution)/shard_map/ppermute | solution.py:422
  85.9 22.4 %collective-permute-start.18 = (bf16[20,8,256]{2,1,0:T(8,128)(2,1)S(1)}, bf16[20,8,256]{2,1,0:T(8,128)(2,1)S(1)}, u32[]{:S(2)}, u32[]{:S(2)}) collective-permute-start(bf16[20,8,256]{2,1,0:T(8,128)(2,1)S(1)} %get-tuple-element.57), channel_id=1, source_target_pairs={{0,3},{1,2},{2,1},{3,0},{4,7},{5,6},{6,5},{7,4},{8,11},{9,10},{10,... | collective-permute-start | bytes 245768 | tf_op jit(solution)/shard_map/ppermute | solution.py:422
  90.0 5.8 %collective-permute-start.30 = (f32[8,256]{1,0:T(8,128)S(1)}, f32[8,256]{1,0:T(8,128)S(1)}, u32[]{:S(2)}, u32[]{:S(2)}) collective-permute-start(f32[8,256]{1,0:T(8,128)S(1)} %add.62), channel_id=1, source_target_pairs={{0,34},{1,35},{2,32},{3,33},{4,38},{5,39},{6,36},{7,37},{8,42},{9,... | collective-permute-start | bytes 24584 | tf_op jit(solution)/shard_map/ppermute | solution.py:557
  95.8 10.6 %collective-permute-start.31 = (f32[8,256]{1,0:T(8,128)S(1)}, f32[8,256]{1,0:T(8,128)S(1)}, u32[]{:S(2)}, u32[]{:S(2)}) collective-permute-start(f32[8,256]{1,0:T(8,128)S(1)} %add.63), channel_id=1, source_target_pairs={{0,64},{4,68},{8,72},{12,76},{16,80},{20,84},{24,88},{28,92},{32,9... | collective-permute-start | bytes 24584 | tf_op jit(solution)/shard_map/ppermute | solution.py:558
  103.9 8.1 %collective-permute-start.25 = (bf16[20,8,256]{2,1,0:T(8,128)(2,1)S(1)}, bf16[20,8,256]{2,1,0:T(8,128)(2,1)S(1)}, u32[]{:S(2)}, u32[]{:S(2)}) collective-permute-start(bf16[20,8,256]{2,1,0:T(8,128)(2,1)S(1)} %get-tuple-element.62), channel_id=1, source_target_pairs={{0,1},{1,0},{2,3},{3,2},{4,5},{5,4},{6,7},{7,6},{8,9},{9,8},{10,11... | collective-permute-start | bytes 245768 | tf_op jit(solution)/shard_map/ppermute | solution.py:422
  104.0 8.0 %collective-permute-start.26 = (bf16[20,8,256]{2,1,0:T(8,128)(2,1)S(1)}, bf16[20,8,256]{2,1,0:T(8,128)(2,1)S(1)}, u32[]{:S(2)}, u32[]{:S(2)}) collective-permute-start(bf16[20,8,256]{2,1,0:T(8,128)(2,1)S(1)} %get-tuple-element.63), channel_id=1, source_target_pairs={{0,2},{1,3},{2,0},{3,1},{4,6},{5,7},{6,4},{7,5},{8,10},{9,11},{10,... | collective-permute-start | bytes 245768 | tf_op jit(solution)/shard_map/ppermute | solution.py:422
  106.4 6.2 %collective-permute-start.27 = (bf16[20,8,256]{2,1,0:T(8,128)(2,1)S(1)}, bf16[20,8,256]{2,1,0:T(8,128)(2,1)S(1)}, u32[]{:S(2)}, u32[]{:S(2)}) collective-permute-start(bf16[20,8,256]{2,1,0:T(8,128)(2,1)S(1)} %get-tuple-element.64), channel_id=1, source_target_pairs={{0,3},{1,2},{2,1},{3,0},{4,7},{5,6},{6,5},{7,4},{8,11},{9,10},{10,... | collective-permute-start | bytes 245768 | tf_op jit(solution)/shard_map/ppermute | solution.py:422
  (15 other events, 62.8 us)

commit v5 on v4

--- a/solution.py
+++ b/solution.py
@@ -84,17 +84,26 @@
 
 
 def densify_kernel(
-    scal, nb, loc_hbm, inv_hbm, inn_hbm, band, d_own, x_core, x_edge, bands, acc, loc, obs, mat,
-    sems,
+    scal, nb_hbm, loc_hbm, inv_hbm, inn_hbm, vbt_hbm, d_own, x_core, x_edge, bands, obs, acc, loc, mat,
+    narrow, nb, vbt, sems,
 ):
     copies = [
         pltpu.make_async_copy(loc_hbm.at[0], loc.at[0], sems.at[0]),
         pltpu.make_async_copy(loc_hbm.at[1], loc.at[1], sems.at[1]),
         pltpu.make_async_copy(inv_hbm, obs.at[0], sems.at[2]),
         pltpu.make_async_copy(inn_hbm, obs.at[1], sems.at[3]),
+        pltpu.make_async_copy(nb_hbm, nb, sems.at[4]),
+        pltpu.make_async_copy(vbt_hbm, vbt, sems.at[5]),
     ]
     for c in copies:
         c.start()
+    narrow[...] = jnp.zeros(narrow.shape, F32)
+    copies[5].wait()
+    narrow[0:NS, 0:32] = vbt[...]
+    band = narrow[...]
+    band = band + pltpu.roll(band, 32, 1)
+    band = band + pltpu.roll(band, 64, 1)
+    band = jnp.concatenate([band, band], axis=1)
     row = lax.broadcasted_iota(jnp.int32, (256, 256), 0)
     col = lax.broadcasted_iota(jnp.int32, (256, 256), 1)
     shift = row - col
@@ -112,6 +121,7 @@
     tile = scal[0]
     core_rel = 2 - 2 * (tile & 1)
     acc[...] = jnp.zeros(acc.shape, F32)
+    copies[4].wait()
     for b in range(2):
         copies[b].wait()
         for j in range(loc.shape[1]):
@@ -244,12 +254,12 @@
     hx_edge[...] = obs_rows(avb, umat, (e_edge,), (x_edge[0:256, :],), w, dxs, norm)
 
 
-def partial_kernel(norm, affine, h_oe, inv, inn, e_own, e_edge, d_own, x_edge, wt, out, ua):
+def partial_kernel(norm, affine, h_oe, obs, e_own, e_edge, d_own, x_edge, wt, out, ua):
     ie, ye = obs_of(x_edge)
     own, edge = h_oe[0:16, :], h_oe[16:32, :]
     if affine:
-        own, edge = own - inn[...], edge - ye
-    q = jnp.concatenate([inv[...] * own, ie * edge], axis=1)
+        own, edge = own - obs[1], edge - ye
+    q = jnp.concatenate([obs[0] * own, ie * edge], axis=1)
     out[...] = adjoint_rows(
         q, wt, (e_own, e_edge), (d_own[...], x_edge[0:256, :]), ua, norm
     )
@@ -292,23 +302,31 @@
     hx_core[18:19, :] = jnp.sum(cg, axis=0, keepdims=True)
 
 
-def sums_kernel(hs, h_core, h1_oe, h1_core, inv, inn, x_core, out):
+def misfit_kernel(h1_oe, h1_core, obs, x_core, out):
     ic, yc = obs_of(x_core)
-
-    def rows(h1, i, y, d):
-        diff = h1 - y
-        q = i * diff
-        return [
-            jnp.sum(q * diff, axis=0, keepdims=True),
-            jnp.sum(q * d, axis=0, keepdims=True),
-            jnp.sum(i * d * d, axis=0, keepdims=True),
-        ]
-
-    own = rows(h1_oe[0:16, :], inv[...], inn[...], hs[0:16, :])
-    core = rows(h1_core[...], ic, yc, h_core[...])
+    own = h1_oe[0:16, :] - obs[1]
+    core = h1_core[...] - yc
+    qo = obs[0] * own
+    qc = ic * core
+    out[0:16, :] = qo
+    out[16:32, :] = qc
+    out[32:40, :] = jnp.zeros((8, 256), F32)
+    out[32:33, :] = jnp.sum(qo * own, axis=0, keepdims=True) + jnp.sum(
+        qc * core, axis=0, keepdims=True
+    )
+
+
+def sums_kernel(hs, h_core, misfit, obs, x_core, out):
+    ic, _ = obs_of(x_core)
+    do, dc = hs[0:16, :], h_core[...]
+
+    def both(own, core):
+        return jnp.sum(own, axis=0, keepdims=True) + jnp.sum(core, axis=0, keepdims=True)
+
     out[...] = hs[32:40, :]
-    for i in range(3):
-        out[3 + i : 4 + i, :] = own[i] + core[i]
+    out[3:4, :] = misfit[32:33, :]
+    out[4:5, :] = both(misfit[0:16, :] * do, misfit[16:32, :] * dc)
+    out[5:6, :] = both(obs[0] * do * do, ic * dc * dc)
 
 
 def third_kernel(
@@ -323,25 +341,15 @@
         a[...] = adj[:, scal[1] ^ k].astype(BF16)
 
 
-def grad_first_kernel(scal, ctl, a0, a1, a2, a3, out, buf, sems):
+def grad_first_kernel(scal, ctl, a0, a1, a2, a3, out):
     share = a0.shape[0]
-    few = share // 4
-    copies = []
     for k, a in enumerate((a0, a1, a2, a3)):
-        for i in range(4):
-            here = pl.ds(few * i, few)
-            at = pl.ds(share * (scal[2] ^ k) + few * i, few)
-            buf[k, here] = ctl[at] + a[here].astype(F32)
-            copies.append(
-                pltpu.make_async_copy(buf.at[k, here], out.at[at], sems.at[4 * k + i])
-            )
-            copies[-1].start()
-    for c in copies:
-        c.wait()
+        at = pl.ds(share * (scal[2] ^ k), share)
+        out[at] = ctl[at] + a[...].astype(F32)
 
 
 def grad_second_kernel(
-    count, scal, ctl, a0, a1, a2, a3, b0, b1, b2, b3, sums, out, costs, buf, sems
+    count, scal, ctl, a0, a1, a2, a3, b0, b1, b2, b3, sums, out, costs
 ):
     tot = jnp.sum(sums[...], axis=1, keepdims=True)
     cc, gg, cg = tot[0:1], tot[1:2], tot[2:3]
@@ -353,22 +361,17 @@
     )
     tb = jnp.broadcast_to(tau, (8, 256))
     share = a0.shape[0]
-    copies = []
-    few = share // 4
     for k, (a, b) in enumerate(zip((a0, a1, a2, a3), (b0, b1, b2, b3))):
-        for i in range(4):
-            here = pl.ds(few * i, few)
-            at = pl.ds(share * (scal[2] ^ k) + few * i, few)
-            g = ctl[at] + a[here].astype(F32)
-            buf[k, here] = g - tb * (g + b[here].astype(F32))
-            copies.append(
-                pltpu.make_async_copy(buf.at[k, here], out.at[at], sems.at[4 * k + i])
-            )
-            copies[-1].start()
+        base = share * (scal[2] ^ k)
+
+        def body(m, _, a=a, b=b, base=base):
+            g = ctl[base + m] + a[m].astype(F32)
+            out[base + m] = g - tb * (g + b[m].astype(F32))
+            return 0
+
+        lax.fori_loop(0, share, body, 0, unroll=10)
     costs[0] = first[0, 0]
     costs[1] = (second / count)[0, 0]
-    for c in copies:
-        c.wait()
 
 
 def make_pairs(tiles, levs):
@@ -440,23 +443,25 @@
         specs=[SM, hbm],
     )
     eparts = shuffle(eparts)
-    band = jnp.tile(vert_band.T, (1, 8))
-    d_own, x_core, x_edge, bands = call(
+    obs_n = channel_weights.shape[0]
+    d_own, x_core, x_edge, bands, obs_own = call(
         densify_kernel,
         [
             sds((256, 256), BF16), sds((352, 256), BF16), sds((352, 256), BF16),
-            sds((4, GRP, GRP), BF16),
+            sds((4, GRP, GRP), BF16), sds((2, obs_n, pdev), F32),
         ],
         (
-            scal, neighbours, far_off(loc_blocks), far_off(inv_error), far_off(innovation), band,
+            scal, far_off(neighbours), far_off(loc_blocks), far_off(inv_error),
+            far_off(innovation), far_off(vert_band.T),
         ),
-        2,
+        1,
         [
             pltpu.VMEM((12, 128, 128), F32), pltpu.VMEM(loc_blocks.shape, BF16),
-            pltpu.VMEM((2,) + inv_error.shape, F32), pltpu.VMEM((256, 256), F32),
-            pltpu.SemaphoreType.DMA((4,)),
+            pltpu.VMEM((256, 256), F32), pltpu.VMEM((16, 128), F32),
+            pltpu.SMEM(neighbours.shape, jnp.int32), pltpu.VMEM((NS, lev), F32),
+            pltpu.SemaphoreType.DMA((6,)),
         ],
-        specs=[SM, SM, hbm, hbm, hbm, VM],
+        specs=[SM, hbm, hbm, hbm, hbm, hbm],
     )
     wt_own = jnp.pad(channel_weights.T, ((0, 0), (0, pdev - channel_weights.shape[0])))
     packed = call(
@@ -519,7 +524,7 @@
         (part,) = call(
             bind(partial_kernel, norm, tag == "a"),
             [wide],
-            (tot, inv_error, innovation, e_own, e_edge, d_own, x_edge, wt),
+            (tot, obs_own, e_own, e_edge, d_own, x_edge, wt),
             0,
             [half],
             2 * mm,
@@ -536,12 +541,12 @@
         6 * mm,
     )
     aparts = shuffle(outs[:4])
+    (misfit,) = call(
+        misfit_kernel, [sds((40, pdev), F32)], (h1_oe, h1_core, obs_own, x_core), 0
+    )
     hs, hd_core, part = reduce_obs("b", outs[5], outs[6], outs[4])
     sums = call(
-        sums_kernel,
-        [sds((8, pdev), F32)],
-        (hs, hd_core, h1_oe, h1_core, inv_error, innovation, x_core),
-        0,
+        sums_kernel, [sds((8, pdev), F32)], (hs, hd_core, misfit, obs_own, x_core), 0
     )[0]
     bparts = call(
         bind(third_kernel, norm),
@@ -558,20 +563,14 @@
     sums = sums + lax.ppermute(sums, "tile", tile_xor(16))
     sums = sums + lax.ppermute(sums, "tile", tile_xor(48))
     whole = sds((members, ldev, pdev), F32)
-    anywhere = pl.BlockSpec(memory_space=pl.ANY)
-    outbuf = [pltpu.VMEM((4, share, ldev, pdev), F32), pltpu.SemaphoreType.DMA((16,))]
-    (grad_first,) = call(
-        grad_first_kernel, [whole], (scal, control, *aparts), 1, outbuf,
-        out_specs=(anywhere,),
-    )
+    (grad_first,) = call(grad_first_kernel, [whole], (scal, control, *aparts), 1)
     count = float(members * lev * pdev * tiles)
     grad_second, costs = call(
         bind(grad_second_kernel, count),
         [whole, sds((2,), F32)],
         (scal, control, *aparts, *bparts, sums),
         1,
-        outbuf,
-        out_specs=(anywhere, SM),
+        out_specs=(VM, SM),
     )
     return grad_first, grad_second, costs
 

time: 115 us -> 114 us (level)
    pallas_call x14 -> x15, Pallas kernels: 17.2 us -> 17 us  [call(): pl.pallas_call(body, out_shape=tuple(outs), in_specs=specs, out_specs=out...]
  transfers between devices with their start and end apart: 33 -> 33, of which waited for: 17 -> 19; matrix products, arithmetic and copies ran while one was open for 0% -> 0% of each run, Pallas kernels for 9% -> 9%
where the time goes in v5:
time: 114 us
  waiting for transfers between devices  48.9 us (43%)
  starting transfers between devices  46.6 us (41%)
  Pallas kernels  17 us (15%)
    ppermute x12, starting transfers between devices, shuffle(): lax.ppermute(parts[k], 'lev', lev_xor(k))  18.7 us
    pallas_call x15, Pallas kernels, call(): pl.pallas_call(body, out_shape=tuple(outs), in_specs=specs, out_specs=out...  17 us
    ppermute x12, waiting for transfers between devices, shuffle(): lax.ppermute(parts[k], 'lev', lev_xor(k))  15.4 us
    ppermute x4, waiting for transfers between devices, swap_edge(): return lax.ppermute(x, both, edge)  13.2 us
    ppermute x4, starting transfers between devices, swap_edge(): return lax.ppermute(x, both, edge)  13.2 us
    ppermute x6, starting transfers between devices, sum4(): one, two, three = (lax.ppermute(x, axis, pairs(k)) for k in steps)  7.5 us
    ppermute x1, starting transfers between devices, per_device(): sums = sums + lax.ppermute(sums, 'tile', tile_xor(16))  6.3 us
    ppermute x1, waiting for transfers between devices, per_device(): sums = sums + lax.ppermute(sums, both, far)  5.01 us
  transfers between devices with their start and end apart: 33, of which 19 were waited for; matrix products, arithmetic and copies ran while one was open for 0% of the time, Pallas kernels for 9%

profile of v5, /device:TPU:2, one launch (start us, length us, event | category | flops | bytes accessed | tf_op | source)
XLA Modules:
  0.0 113.7 jit_solution(11463583001593063890)
XLA Ops:
  2.3 2.0 %collective-permute-start.3 = (bf16[20,8,256]{2,1,0:T(8,128)(2,1)S(1)}, bf16[20,8,256]{2,1,0:T(8,128)(2,1)S(1)}, u32[]{:S(2)}, u32[]{:S(2)}) collective-permute-start(bf16[20,8,256]{2,1,0:T(8,128)(2,1)S(1)} %get-tuple-element.41), channel_id=1, source_target_pairs={{0,1},{1,0},{2,3},{3,2},{4,5},{5,4},{6,7},{7,6},{8,9},{9,8},{10,11... | collective-permute-start | bytes 245768 | tf_op jit(solution)/shard_map/ppermute | solution.py:425
  4.3 3.3 %collective-permute-start.4 = (bf16[20,8,256]{2,1,0:T(8,128)(2,1)S(1)}, bf16[20,8,256]{2,1,0:T(8,128)(2,1)S(1)}, u32[]{:S(2)}, u32[]{:S(2)}) collective-permute-start(bf16[20,8,256]{2,1,0:T(8,128)(2,1)S(1)} %get-tuple-element.42), channel_id=1, source_target_pairs={{0,2},{1,3},{2,0},{3,1},{4,6},{5,7},{6,4},{7,5},{8,10},{9,11},{10,... | collective-permute-start | bytes 245768 | tf_op jit(solution)/shard_map/ppermute | solution.py:425
  7.6 6.5 %collective-permute-done.4.e2 = bf16[20,8,256]{2,1,0:T(8,128)(2,1)S(1)} collective-permute-done((bf16[20,8,256]{2,1,0:T(8,128)(2,1)S(1)}, bf16[20,8,256]{2,1,0:T(8,128)(2,1)S(1)}, u32[]{:S(2)}, u32[]{:S(2)}) %collective-permute-start.4) | collective-permute-done | bytes 81952 | tf_op jit(solution)/shard_map/ppermute | solution.py:425
  14.8 7.8 %collective-permute-start.9 = (bf16[20,4,8,256]{3,2,1,0:T(8,128)(2,1)S(1)}, bf16[20,4,8,256]{3,2,1,0:T(8,128)(2,1)S(1)}, u32[]{:S(2)}, u32[]{:S(2)}) collective-permute-start(bf16[20,4,8,256]{3,2,1,0:T(8,128)(2,1)S(1)} %shard_map.105.refs_5_.refs_2_.refs_4_), channel_id=1, source_target_pairs={{0,254},{1,255},{2,252},{3,253},{4,8},{5,9},{6,10},{7,11},{8,4},{9... | collective-permute-start | bytes 983048 | tf_op jit(solution)/shard_map/ppermute | solution.py:421
  25.8 2.1 %shard_map.106 = (bf16[256,256]{1,0:T(8,128)(2,1)S(1)}, bf16[352,256]{1,0:T(8,128)(2,1)S(1)}, bf16[352,256]{1,0:T(8,128)(2,1)S(1)}, bf16[4,160,160]{2,1,0:T(8,128)(2,1)S(1)}, f32[2,16,256]{2,1,0:T(8,128)S(1)}) custom-call(s32[4]{0:T(128)S(1)} %pad_add_fusion.scal.refs_0_, s32[2,9]{1,0:T(2,128)} %nb_hbm.1, bf16[2,9,128,128]{3,2,1,0:T(8,128)(2,1)} %loc_hbm.1, ...), custom_call_target="tpu_custom_call" | custom-call | bytes 1352920 | tf_op jit(solution)/shard_map/pallas_call | solution.py:28
  28.1 2.2 %collective-permute-done.refs_2_ = bf16[23,8,256]{2,1,0:T(8,128)(2,1)S(1)} collective-permute-done((bf16[23,8,256]{2,1,0:T(8,128)(2,1)S(1)}, bf16[23,8,256]{2,1,0:T(8,128)(2,1)S(1)}, u32[]{:S(2)}, u32[]{:S(2)}) %collective-permute-start) | collective-permute-done | bytes 94240 | tf_op jit(solution)/shard_map/ppermute | solution.py:425
  30.7 1.9 %collective-permute-start.2 = (bf16[23,8,256]{2,1,0:T(8,128)(2,1)S(1)}, bf16[23,8,256]{2,1,0:T(8,128)(2,1)S(1)}, u32[]{:S(2)}, u32[]{:S(2)}) collective-permute-start(bf16[23,8,256]{2,1,0:T(8,128)(2,1)S(1)} %get-tuple-element.39), channel_id=1, source_target_pairs={{0,3},{1,2},{2,1},{3,0},{4,7},{5,6},{6,5},{7,4},{8,11},{9,10},{10,... | collective-permute-start | bytes 282632 | tf_op jit(solution)/shard_map/ppermute | solution.py:425
  32.6 5.9 %collective-permute-done.2.refs_4_ = bf16[23,8,256]{2,1,0:T(8,128)(2,1)S(1)} collective-permute-done((bf16[23,8,256]{2,1,0:T(8,128)(2,1)S(1)}, bf16[23,8,256]{2,1,0:T(8,128)(2,1)S(1)}, u32[]{:S(2)}, u32[]{:S(2)}) %collective-permute-start.2) | collective-permute-done | bytes 94240 | tf_op jit(solution)/shard_map/ppermute | solution.py:425
  41.9 2.8 %collective-permute-start.11 = (f32[32,256]{1,0:T(8,128)S(1)}, f32[32,256]{1,0:T(8,128)S(1)}, u32[]{:S(2)}, u32[]{:S(2)}) collective-permute-start(f32[32,256]{1,0:T(8,128)S(1)} %pad_maximum_fusion.1), channel_id=1, source_target_pairs={{0,254},{1,255},{2,252},{3,253},{4,8},{5,9},{6,10},{7,11},{8,4},{9... | collective-permute-start | bytes 98312 | tf_op jit(solution)/shard_map/ppermute | solution.py:421
  44.7 5.7 %collective-permute-done.11 = f32[32,256]{1,0:T(8,128)S(1)} collective-permute-done((f32[32,256]{1,0:T(8,128)S(1)}, f32[32,256]{1,0:T(8,128)S(1)}, u32[]{:S(2)}, u32[]{:S(2)}) %collective-permute-start.11) | collective-permute-done | bytes 32800 | tf_op jit(solution)/shard_map/ppermute | solution.py:421
  50.5 2.0 %collective-permute-start.14 = (f32[32,256]{1,0:T(8,128)S(1)}, f32[32,256]{1,0:T(8,128)S(1)}, u32[]{:S(2)}, u32[]{:S(2)}) collective-permute-start(f32[32,256]{1,0:T(8,128)S(1)} %maximum_add_fusion), channel_id=1, source_target_pairs={{0,3},{1,2},{2,1},{3,0},{4,7},{5,6},{6,5},{7,4},{8,11},{9,10},{10,... | collective-permute-start | bytes 98312 | tf_op jit(solution)/shard_map/ppermute | solution.py:430
  58.1 3.0 %shard_map.110 = (bf16[20,8,256]{2,1,0:T(8,128)(2,1)S(1)}, bf16[20,8,256]{2,1,0:T(8,128)(2,1)S(1)}, bf16[20,8,256]{2,1,0:T(8,128)(2,1)S(1)}, bf16[20,8,256]{2,1,...) custom-call(s32[4]{0:T(128)S(1)} %pad_add_fusion.scal.refs_0_, ...), custom_call_target="tpu_custom_call" | custom-call | flops 503316480 | bytes 2899984 | tf_op jit(solution)/shard_map/pallas_call | solution.py:28
  62.4 2.2 %collective-permute-start.20 = (f32[32,256]{1,0:T(8,128)S(1)}, f32[32,256]{1,0:T(8,128)S(1)}, u32[]{:S(2)}, u32[]{:S(2)}) collective-permute-start(f32[32,256]{1,0:T(8,128)S(1)} %pad_maximum_fusion.2), channel_id=1, source_target_pairs={{0,254},{1,255},{2,252},{3,253},{4,8},{5,9},{6,10},{7,11},{8,4},{9... | collective-permute-start | bytes 98312 | tf_op jit(solution)/shard_map/ppermute | solution.py:421
  64.6 6.5 %collective-permute-done.20 = f32[32,256]{1,0:T(8,128)S(1)} collective-permute-done((f32[32,256]{1,0:T(8,128)S(1)}, f32[32,256]{1,0:T(8,128)S(1)}, u32[]{:S(2)}, u32[]{:S(2)}) %collective-permute-start.20) | collective-permute-done | bytes 32800 | tf_op jit(solution)/shard_map/ppermute | solution.py:421
  71.1 2.0 %collective-permute-start.22 = (f32[40,256]{1,0:T(8,128)S(1)}, f32[40,256]{1,0:T(8,128)S(1)}, u32[]{:S(2)}, u32[]{:S(2)}) collective-permute-start(f32[40,256]{1,0:T(8,128)S(1)} %pad_maximum_fusion), channel_id=1, source_target_pairs={{0,2},{1,3},{2,0},{3,1},{4,6},{5,7},{6,4},{7,5},{8,10},{9,11},{10,... | collective-permute-start | bytes 122888 | tf_op jit(solution)/shard_map/ppermute | solution.py:430
  73.1 1.9 %collective-permute-start.23 = (f32[40,256]{1,0:T(8,128)S(1)}, f32[40,256]{1,0:T(8,128)S(1)}, u32[]{:S(2)}, u32[]{:S(2)}) collective-permute-start(f32[40,256]{1,0:T(8,128)S(1)} %pad_maximum_fusion), channel_id=1, source_target_pairs={{0,3},{1,2},{2,1},{3,0},{4,7},{5,6},{6,5},{7,4},{8,11},{9,10},{10,... | collective-permute-start | bytes 122888 | tf_op jit(solution)/shard_map/ppermute | solution.py:430
  75.0 2.0 %collective-permute-start.16 = (bf16[20,8,256]{2,1,0:T(8,128)(2,1)S(1)}, bf16[20,8,256]{2,1,0:T(8,128)(2,1)S(1)}, u32[]{:S(2)}, u32[]{:S(2)}) collective-permute-start(bf16[20,8,256]{2,1,0:T(8,128)(2,1)S(1)} %get-tuple-element.57), channel_id=1, source_target_pairs={{0,1},{1,0},{2,3},{3,2},{4,5},{5,4},{6,7},{7,6},{8,9},{9,8},{10,11... | collective-permute-start | bytes 245768 | tf_op jit(solution)/shard_map/ppermute | solution.py:425
  80.8 3.6 %collective-permute-done.28 = f32[8,256]{1,0:T(8,128)S(1)} collective-permute-done((f32[8,256]{1,0:T(8,128)S(1)}, f32[8,256]{1,0:T(8,128)S(1)}, u32[]{:S(2)}, u32[]{:S(2)}) %collective-permute-start.28) | collective-permute-done | bytes 8224 | tf_op jit(solution)/shard_map/ppermute | solution.py:560
  85.0 1.9 %collective-permute-start.18 = (bf16[20,8,256]{2,1,0:T(8,128)(2,1)S(1)}, bf16[20,8,256]{2,1,0:T(8,128)(2,1)S(1)}, u32[]{:S(2)}, u32[]{:S(2)}) collective-permute-start(bf16[20,8,256]{2,1,0:T(8,128)(2,1)S(1)} %get-tuple-element.59), channel_id=1, source_target_pairs={{0,3},{1,2},{2,1},{3,0},{4,7},{5,6},{6,5},{7,4},{8,11},{9,10},{10,... | collective-permute-start | bytes 245768 | tf_op jit(solution)/shard_map/ppermute | solution.py:425
  86.9 2.4 %collective-permute-done.29 = f32[8,256]{1,0:T(8,128)S(1)} collective-permute-done((f32[8,256]{1,0:T(8,128)S(1)}, f32[8,256]{1,0:T(8,128)S(1)}, u32[]{:S(2)}, u32[]{:S(2)}) %collective-permute-start.29) | collective-permute-done | bytes 8224 | tf_op jit(solution)/shard_map/ppermute | solution.py:561
  90.1 5.0 %collective-permute-done.30 = f32[8,256]{1,0:T(8,128)S(1)} collective-permute-done((f32[8,256]{1,0:T(8,128)S(1)}, f32[8,256]{1,0:T(8,128)S(1)}, u32[]{:S(2)}, u32[]{:S(2)}) %collective-permute-start.30) | collective-permute-done | bytes 8224 | tf_op jit(solution)/shard_map/ppermute | solution.py:562
  95.1 6.3 %collective-permute-start.31 = (f32[8,256]{1,0:T(8,128)S(1)}, f32[8,256]{1,0:T(8,128)S(1)}, u32[]{:S(2)}, u32[]{:S(2)}) collective-permute-start(f32[8,256]{1,0:T(8,128)S(1)} %add.63), channel_id=1, source_target_pairs={{0,64},{4,68},{8,72},{12,76},{16,80},{20,84},{24,88},{28,92},{32,9... | collective-permute-start | bytes 24584 | tf_op jit(solution)/shard_map/ppermute | solution.py:563
  103.3 2.4 %collective-permute-start.26 = (bf16[20,8,256]{2,1,0:T(8,128)(2,1)S(1)}, bf16[20,8,256]{2,1,0:T(8,128)(2,1)S(1)}, u32[]{:S(2)}, u32[]{:S(2)}) collective-permute-start(bf16[20,8,256]{2,1,0:T(8,128)(2,1)S(1)} %get-tuple-element.65), channel_id=1, source_target_pairs={{0,2},{1,3},{2,0},{3,1},{4,6},{5,7},{6,4},{7,5},{8,10},{9,11},{10,... | collective-permute-start | bytes 245768 | tf_op jit(solution)/shard_map/ppermute | solution.py:425
  108.8 2.2 %collective-permute-done.32 = f32[8,256]{1,0:T(8,128)S(1)} collective-permute-done((f32[8,256]{1,0:T(8,128)S(1)}, f32[8,256]{1,0:T(8,128)S(1)}, u32[]{:S(2)}, u32[]{:S(2)}) %collective-permute-start.32) | collective-permute-done | bytes 8224 | tf_op jit(solution)/shard_map/ppermute | solution.py:564
  (82 shorter events, 29.1 us)
Async XLA Ops:
  2.3 5.3 %collective-permute-start.3 = (bf16[20,8,256]{2,1,0:T(8,128)(2,1)S(1)}, bf16[20,8,256]{2,1,0:T(8,128)(2,1)S(1)}, u32[]{:S(2)}, u32[]{:S(2)}) collective-permute-start(bf16[20,8,256]{2,1,0:T(8,128)(2,1)S(1)} %get-tuple-element.41), channel_id=1, source_target_pairs={{0,1},{1,0},{2,3},{3,2},{4,5},{5,4},{6,7},{7,6},{8,9},{9,8},{10,11... | collective-permute-start | bytes 245768 | tf_op jit(solution)/shard_map/ppermute | solution.py:425
  4.3 9.8 %collective-permute-start.4 = (bf16[20,8,256]{2,1,0:T(8,128)(2,1)S(1)}, bf16[20,8,256]{2,1,0:T(8,128)(2,1)S(1)}, u32[]{:S(2)}, u32[]{:S(2)}) collective-permute-start(bf16[20,8,256]{2,1,0:T(8,128)(2,1)S(1)} %get-tuple-element.42), channel_id=1, source_target_pairs={{0,2},{1,3},{2,0},{3,1},{4,6},{5,7},{6,4},{7,5},{8,10},{9,11},{10,... | collective-permute-start | bytes 245768 | tf_op jit(solution)/shard_map/ppermute | solution.py:425
  7.6 6.5 %collective-permute-start.5 = (bf16[20,8,256]{2,1,0:T(8,128)(2,1)S(1)}, bf16[20,8,256]{2,1,0:T(8,128)(2,1)S(1)}, u32[]{:S(2)}, u32[]{:S(2)}) collective-permute-start(bf16[20,8,256]{2,1,0:T(8,128)(2,1)S(1)} %get-tuple-element.43), channel_id=1, source_target_pairs={{0,3},{1,2},{2,1},{3,0},{4,7},{5,6},{6,5},{7,4},{8,11},{9,10},{10,... | collective-permute-start | bytes 245768 | tf_op jit(solution)/shard_map/ppermute | solution.py:425
  14.7 23.7 %collective-permute-start.6 = (bf16[20,4,8,256]{3,2,1,0:T(8,128)(2,1)S(1)}, bf16[20,4,8,256]{3,2,1,0:T(8,128)(2,1)S(1)}, u32[]{:S(2)}, u32[]{:S(2)}) collective-permute-start(bf16[20,4,8,256]{3,2,1,0:T(8,128)(2,1)S(1)} %shard_map.105.refs_5_.refs_2_.refs_4_), channel_id=1, source_target_pairs={{0,4},{4,0},{8,12},{12,8},{16,20},{20,16},{24,28},{28,24},{32,36},... | collective-permute-start | bytes 983048 | tf_op jit(solution)/shard_map/ppermute | solution.py:418
  14.8 26.5 %collective-permute-start.9 = (bf16[20,4,8,256]{3,2,1,0:T(8,128)(2,1)S(1)}, bf16[20,4,8,256]{3,2,1,0:T(8,128)(2,1)S(1)}, u32[]{:S(2)}, u32[]{:S(2)}) collective-permute-start(bf16[20,4,8,256]{3,2,1,0:T(8,128)(2,1)S(1)} %shard_map.105.refs_5_.refs_2_.refs_4_), channel_id=1, source_target_pairs={{0,254},{1,255},{2,252},{3,253},{4,8},{5,9},{6,10},{7,11},{8,4},{9... | collective-permute-start | bytes 983048 | tf_op jit(solution)/shard_map/ppermute | solution.py:421
  23.3 7.0 %collective-permute-start = (bf16[23,8,256]{2,1,0:T(8,128)(2,1)S(1)}, bf16[23,8,256]{2,1,0:T(8,128)(2,1)S(1)}, u32[]{:S(2)}, u32[]{:S(2)}) collective-permute-start(bf16[23,8,256]{2,1,0:T(8,128)(2,1)S(1)} %get-tuple-element.37), channel_id=1, source_target_pairs={{0,1},{1,0},{2,3},{3,2},{4,5},{5,4},{6,7},{7,6},{8,9},{9,8},{10,11... | collective-permute-start | bytes 282632 | tf_op jit(solution)/shard_map/ppermute | solution.py:425
  24.0 6.7 %collective-permute-start.1 = (bf16[23,8,256]{2,1,0:T(8,128)(2,1)S(1)}, bf16[23,8,256]{2,1,0:T(8,128)(2,1)S(1)}, u32[]{:S(2)}, u32[]{:S(2)}) collective-permute-start(bf16[23,8,256]{2,1,0:T(8,128)(2,1)S(1)} %get-tuple-element.38), channel_id=1, source_target_pairs={{0,2},{1,3},{2,0},{3,1},{4,6},{5,7},{6,4},{7,5},{8,10},{9,11},{10,... | collective-permute-start | bytes 282632 | tf_op jit(solution)/shard_map/ppermute | solution.py:425
  28.0 10.4 %collective-permute-start.7 = (bf16[352,256]{1,0:T(8,128)(2,1)S(1)}, bf16[352,256]{1,0:T(8,128)(2,1)S(1)}, u32[]{:S(2)}, u32[]{:S(2)}) collective-permute-start(bf16[352,256]{1,0:T(8,128)(2,1)S(1)} %get-tuple-element.45), channel_id=1, source_target_pairs={{0,4},{4,0},{8,12},{12,8},{16,20},{20,16},{24,28},{28,24},{32,36},... | collective-permute-start | bytes 540680 | tf_op jit(solution)/shard_map/ppermute | solution.py:418
  30.2 11.0 %collective-permute-start.10 = (bf16[352,256]{1,0:T(8,128)(2,1)S(1)}, bf16[352,256]{1,0:T(8,128)(2,1)S(1)}, u32[]{:S(2)}, u32[]{:S(2)}) collective-permute-start(bf16[352,256]{1,0:T(8,128)(2,1)S(1)} %get-tuple-element.50), channel_id=1, source_target_pairs={{0,254},{1,255},{2,252},{3,253},{4,8},{5,9},{6,10},{7,11},{8,4},{9... | collective-permute-start | bytes 540680 | tf_op jit(solution)/shard_map/ppermute | solution.py:421
  30.7 7.8 %collective-permute-start.2 = (bf16[23,8,256]{2,1,0:T(8,128)(2,1)S(1)}, bf16[23,8,256]{2,1,0:T(8,128)(2,1)S(1)}, u32[]{:S(2)}, u32[]{:S(2)}) collective-permute-start(bf16[23,8,256]{2,1,0:T(8,128)(2,1)S(1)} %get-tuple-element.39), channel_id=1, source_target_pairs={{0,3},{1,2},{2,1},{3,0},{4,7},{5,6},{6,5},{7,4},{8,11},{9,10},{10,... | collective-permute-start | bytes 282632 | tf_op jit(solution)/shard_map/ppermute | solution.py:425
  41.9 8.5 %collective-permute-start.11 = (f32[32,256]{1,0:T(8,128)S(1)}, f32[32,256]{1,0:T(8,128)S(1)}, u32[]{:S(2)}, u32[]{:S(2)}) collective-permute-start(f32[32,256]{1,0:T(8,128)S(1)} %pad_maximum_fusion.1), channel_id=1, source_target_pairs={{0,254},{1,255},{2,252},{3,253},{4,8},{5,9},{6,10},{7,11},{8,4},{9... | collective-permute-start | bytes 98312 | tf_op jit(solution)/shard_map/ppermute | solution.py:421
  50.4 4.9 %collective-permute-start.13 = (f32[32,256]{1,0:T(8,128)S(1)}, f32[32,256]{1,0:T(8,128)S(1)}, u32[]{:S(2)}, u32[]{:S(2)}) collective-permute-start(f32[32,256]{1,0:T(8,128)S(1)} %maximum_add_fusion), channel_id=1, source_target_pairs={{0,2},{1,3},{2,0},{3,1},{4,6},{5,7},{6,4},{7,5},{8,10},{9,11},{10,... | collective-permute-start | bytes 98312 | tf_op jit(solution)/shard_map/ppermute | solution.py:430
  50.5 5.8 %collective-permute-start.14 = (f32[32,256]{1,0:T(8,128)S(1)}, f32[32,256]{1,0:T(8,128)S(1)}, u32[]{:S(2)}, u32[]{:S(2)}) collective-permute-start(f32[32,256]{1,0:T(8,128)S(1)} %maximum_add_fusion), channel_id=1, source_target_pairs={{0,3},{1,2},{2,1},{3,0},{4,7},{5,6},{6,5},{7,4},{8,11},{9,10},{10,... | collective-permute-start | bytes 98312 | tf_op jit(solution)/shard_map/ppermute | solution.py:430
  62.4 8.6 %collective-permute-start.20 = (f32[32,256]{1,0:T(8,128)S(1)}, f32[32,256]{1,0:T(8,128)S(1)}, u32[]{:S(2)}, u32[]{:S(2)}) collective-permute-start(f32[32,256]{1,0:T(8,128)S(1)} %pad_maximum_fusion.2), channel_id=1, source_target_pairs={{0,254},{1,255},{2,252},{3,253},{4,8},{5,9},{6,10},{7,11},{8,4},{9... | collective-permute-start | bytes 98312 | tf_op jit(solution)/shard_map/ppermute | solution.py:421
  71.1 6.0 %collective-permute-start.22 = (f32[40,256]{1,0:T(8,128)S(1)}, f32[40,256]{1,0:T(8,128)S(1)}, u32[]{:S(2)}, u32[]{:S(2)}) collective-permute-start(f32[40,256]{1,0:T(8,128)S(1)} %pad_maximum_fusion), channel_id=1, source_target_pairs={{0,2},{1,3},{2,0},{3,1},{4,6},{5,7},{6,4},{7,5},{8,10},{9,11},{10,... | collective-permute-start | bytes 122888 | tf_op jit(solution)/shard_map/ppermute | solution.py:430
  73.1 5.8 %collective-permute-start.23 = (f32[40,256]{1,0:T(8,128)S(1)}, f32[40,256]{1,0:T(8,128)S(1)}, u32[]{:S(2)}, u32[]{:S(2)}) collective-permute-start(f32[40,256]{1,0:T(8,128)S(1)} %pad_maximum_fusion), channel_id=1, source_target_pairs={{0,3},{1,2},{2,1},{3,0},{4,7},{5,6},{6,5},{7,4},{8,11},{9,10},{10,... | collective-permute-start | bytes 122888 | tf_op jit(solution)/shard_map/ppermute | solution.py:430
  75.0 28.2 %collective-permute-start.16 = (bf16[20,8,256]{2,1,0:T(8,128)(2,1)S(1)}, bf16[20,8,256]{2,1,0:T(8,128)(2,1)S(1)}, u32[]{:S(2)}, u32[]{:S(2)}) collective-permute-start(bf16[20,8,256]{2,1,0:T(8,128)(2,1)S(1)} %get-tuple-element.57), channel_id=1, source_target_pairs={{0,1},{1,0},{2,3},{3,2},{4,5},{5,4},{6,7},{7,6},{8,9},{9,8},{10,11... | collective-permute-start | bytes 245768 | tf_op jit(solution)/shard_map/ppermute | solution.py:425
  84.4 22.9 %collective-permute-start.17 = (bf16[20,8,256]{2,1,0:T(8,128)(2,1)S(1)}, bf16[20,8,256]{2,1,0:T(8,128)(2,1)S(1)}, u32[]{:S(2)}, u32[]{:S(2)}) collective-permute-start(bf16[20,8,256]{2,1,0:T(8,128)(2,1)S(1)} %get-tuple-element.58), channel_id=1, source_target_pairs={{0,2},{1,3},{2,0},{3,1},{4,6},{5,7},{6,4},{7,5},{8,10},{9,11},{10,... | collective-permute-start | bytes 245768 | tf_op jit(solution)/shard_map/ppermute | solution.py:425
  85.0 22.4 %collective-permute-start.18 = (bf16[20,8,256]{2,1,0:T(8,128)(2,1)S(1)}, bf16[20,8,256]{2,1,0:T(8,128)(2,1)S(1)}, u32[]{:S(2)}, u32[]{:S(2)}) collective-permute-start(bf16[20,8,256]{2,1,0:T(8,128)(2,1)S(1)} %get-tuple-element.59), channel_id=1, source_target_pairs={{0,3},{1,2},{2,1},{3,0},{4,7},{5,6},{6,5},{7,4},{8,11},{9,10},{10,... | collective-permute-start | bytes 245768 | tf_op jit(solution)/shard_map/ppermute | solution.py:425
  89.3 5.8 %collective-permute-start.30 = (f32[8,256]{1,0:T(8,128)S(1)}, f32[8,256]{1,0:T(8,128)S(1)}, u32[]{:S(2)}, u32[]{:S(2)}) collective-permute-start(f32[8,256]{1,0:T(8,128)S(1)} %add.62), channel_id=1, source_target_pairs={{0,34},{1,35},{2,32},{3,33},{4,38},{5,39},{6,36},{7,37},{8,42},{9,... | collective-permute-start | bytes 24584 | tf_op jit(solution)/shard_map/ppermute | solution.py:562
  95.1 10.6 %collective-permute-start.31 = (f32[8,256]{1,0:T(8,128)S(1)}, f32[8,256]{1,0:T(8,128)S(1)}, u32[]{:S(2)}, u32[]{:S(2)}) collective-permute-start(f32[8,256]{1,0:T(8,128)S(1)} %add.63), channel_id=1, source_target_pairs={{0,64},{4,68},{8,72},{12,76},{16,80},{20,84},{24,88},{28,92},{32,9... | collective-permute-start | bytes 24584 | tf_op jit(solution)/shard_map/ppermute | solution.py:563
  102.9 8.1 %collective-permute-start.25 = (bf16[20,8,256]{2,1,0:T(8,128)(2,1)S(1)}, bf16[20,8,256]{2,1,0:T(8,128)(2,1)S(1)}, u32[]{:S(2)}, u32[]{:S(2)}) collective-permute-start(bf16[20,8,256]{2,1,0:T(8,128)(2,1)S(1)} %get-tuple-element.64), channel_id=1, source_target_pairs={{0,1},{1,0},{2,3},{3,2},{4,5},{5,4},{6,7},{7,6},{8,9},{9,8},{10,11... | collective-permute-start | bytes 245768 | tf_op jit(solution)/shard_map/ppermute | solution.py:425
  103.3 7.7 %collective-permute-start.26 = (bf16[20,8,256]{2,1,0:T(8,128)(2,1)S(1)}, bf16[20,8,256]{2,1,0:T(8,128)(2,1)S(1)}, u32[]{:S(2)}, u32[]{:S(2)}) collective-permute-start(bf16[20,8,256]{2,1,0:T(8,128)(2,1)S(1)} %get-tuple-element.65), channel_id=1, source_target_pairs={{0,2},{1,3},{2,0},{3,1},{4,6},{5,7},{6,4},{7,5},{8,10},{9,11},{10,... | collective-permute-start | bytes 245768 | tf_op jit(solution)/shard_map/ppermute | solution.py:425
  105.7 6.2 %collective-permute-start.27 = (bf16[20,8,256]{2,1,0:T(8,128)(2,1)S(1)}, bf16[20,8,256]{2,1,0:T(8,128)(2,1)S(1)}, u32[]{:S(2)}, u32[]{:S(2)}) collective-permute-start(bf16[20,8,256]{2,1,0:T(8,128)(2,1)S(1)} %get-tuple-element.66), channel_id=1, source_target_pairs={{0,3},{1,2},{2,1},{3,0},{4,7},{5,6},{6,5},{7,4},{8,11},{9,10},{10,... | collective-permute-start | bytes 245768 | tf_op jit(solution)/shard_map/ppermute | solution.py:425
  (11 other events, 56.7 us)

commit v6 on v5

--- a/solution.py
+++ b/solution.py
@@ -11,7 +11,7 @@
 HV = 4
 NS = 2 * HV + 1
 STEP = 0.5
-GRP = 160
+GRP = 128
 F32 = jnp.float32
 BF16 = jnp.bfloat16
 VM = pl.BlockSpec(memory_space=pltpu.VMEM)
@@ -103,12 +103,11 @@
     band = narrow[...]
     band = band + pltpu.roll(band, 32, 1)
     band = band + pltpu.roll(band, 64, 1)
-    band = jnp.concatenate([band, band], axis=1)
-    row = lax.broadcasted_iota(jnp.int32, (256, 256), 0)
-    col = lax.broadcasted_iota(jnp.int32, (256, 256), 1)
+    row = lax.broadcasted_iota(jnp.int32, (GRP, GRP), 0)
+    col = lax.broadcasted_iota(jnp.int32, (GRP, GRP), 1)
     shift = row - col
     same = (row >> 5) == (col >> 5)
-    tot = jnp.zeros((256, 256), F32)
+    tot = jnp.zeros((GRP, GRP), F32)
     for s in range(NS):
         tot = jnp.where(same & (shift == s - HV), band[s : s + 1, :], tot)
     mat[...] = tot
@@ -116,8 +115,9 @@
     fwd = mat[...].T
     for i, m in enumerate((fwd, back)):
         hi = m.astype(BF16)
-        bands[2 * i] = hi[0:GRP, 0:GRP]
-        bands[2 * i + 1] = (m - hi.astype(F32)).astype(BF16)[0:GRP, 0:GRP]
+        bands[i, :, 0:GRP] = hi
+        bands[i, :, GRP : 2 * GRP] = hi
+        bands[i, :, 2 * GRP : 3 * GRP] = (m - hi.astype(F32)).astype(BF16)
     tile = scal[0]
     core_rel = 2 - 2 * (tile & 1)
     acc[...] = jnp.zeros(acc.shape, F32)
@@ -148,22 +148,19 @@
         out[:, scal[1] ^ k] = e[...]
 
 
-def band_apply(mats, x, exact):
-    hi, lo = mats
-
-    def mul(a, b):
-        return jnp.dot(a, b, preferred_element_type=F32)
-
+def band_apply(mat, x, exact):
     if exact:
-        return mul(hi, x) + mul(lo, x)
+        return jnp.dot(
+            mat[:, GRP : 3 * GRP], jnp.concatenate([x, x], axis=0), preferred_element_type=F32
+        )
     xh = x.astype(BF16)
     xl = (x - xh.astype(F32)).astype(BF16)
-    return mul(hi, xh) + (mul(lo, xh) + mul(hi, xl))
-
-
-def smooth_rows(src, exact, mats, avb):
+    return jnp.dot(mat, jnp.concatenate([xh, xl, xh], axis=0), preferred_element_type=F32)
+
+
+def smooth_rows(src, exact, mat, avb):
     for r in range(0, avb.shape[0], GRP):
-        avb[r : r + GRP, :] = band_apply(mats, src(r), exact).astype(BF16)
+        avb[r : r + GRP, :] = band_apply(mat, src(r), exact).astype(BF16)
 
 
 def obs_rows(avb, umat, ens3, dmats, w, dxs, norm):
@@ -207,13 +204,12 @@
     return total
 
 
-def adjoint_finish(mats, umat, out):
-    ms = out.shape[0]
+def adjoint_finish(mat, umat, out):
     lev = 32
-    five = GRP // lev
-    for i in range(0, ms, five):
-        got = band_apply(mats, umat[lev * i : lev * i + GRP, :], False)
-        out[i : i + five] = got.reshape(five, 4, 8, 256)
+    some = GRP // lev
+    for i in range(0, out.shape[0], some):
+        got = band_apply(mat, umat[lev * i : lev * i + GRP, :], False)
+        out[i : i + some] = got.reshape(some, 4, 8, 256)
 
 
 def obs_of(x):
@@ -241,10 +237,10 @@
     wt[...] = wsq[0:32, :]
 
     def rows_of(r):
-        five = GRP // 32
-        return src[r // 32 : r // 32 + five].reshape(GRP, 256).astype(BF16)
-
-    smooth_rows(rows_of, True, (bands[0], bands[1]), avb)
+        some = GRP // 32
+        return src[r // 32 : r // 32 + some].reshape(GRP, 256).astype(BF16)
+
+    smooth_rows(rows_of, True, bands[0], avb)
     hx = obs_rows(avb, umat, (e_own, e_core), (d_own[...], x_core[0:256, :]), w, dxs, norm)
     hx_own[...] = hx[:, 0:256]
     hx_core[...] = hx[:, 256:512]
@@ -252,6 +248,14 @@
 
 def edge_kernel(norm, avb, e_edge, x_edge, w, hx_edge, umat, dxs):
     hx_edge[...] = obs_rows(avb, umat, (e_edge,), (x_edge[0:256, :],), w, dxs, norm)
+
+
+def own_edge_kernel(norm, avb, e_own, e_edge, d_own, x_edge, w, hx_own, hx_edge, umat, dxs):
+    hx = obs_rows(
+        avb, umat, (e_own, e_edge), (d_own[...], x_edge[0:256, :]), w, dxs, norm
+    )
+    hx_own[...] = hx[:, 0:256]
+    hx_edge[...] = hx[:, 256:512]
 
 
 def partial_kernel(norm, affine, h_oe, obs, e_own, e_edge, d_own, x_edge, wt, out, ua):
@@ -266,15 +270,15 @@
 
 
 def second_kernel(
-    norm, scal, part, h_core, cm, e_own, e_core, d_own, x_core, bands, w, wt, s0,
-    a0, a1, a2, a3, avb, hx_core, hx_own, adj, ua, umat, dxs,
+    norm, scal, part, h_core, cm, e_core, x_core, bands, w, wt, s0,
+    a0, a1, a2, a3, avb, hx_core, adj, ua, umat, dxs,
 ):
     share = adj.shape[0]
     ic, yc = obs_of(x_core)
     dcore = x_core[0:256, :]
     q = ic * (h_core[...] - yc)
     umat[...] = part[...] + adjoint_rows(q, wt, (e_core,), (dcore,), ua, norm)
-    adjoint_finish((bands[2], bands[3]), umat, adj)
+    adjoint_finish(bands[1], umat, adj)
     for k, a in enumerate((a0, a1, a2, a3)):
         a[...] = adj[:, scal[1] ^ k].astype(BF16)
 
@@ -289,13 +293,11 @@
     gg, cg = lax.fori_loop(0, share, total, (zero, zero), unroll=2)
 
     def rows_of(r):
-        five = GRP // 32
-        return adj[r // 32 : r // 32 + five].reshape(GRP, 256)
-
-    smooth_rows(rows_of, False, (bands[0], bands[1]), avb)
-    hx = obs_rows(avb, umat, (e_own, e_core), (d_own[...], dcore), w, dxs, norm)
-    hx_own[...] = hx[:, 0:256]
-    hx_core[0:16, :] = hx[:, 256:512]
+        some = GRP // 32
+        return adj[r // 32 : r // 32 + some].reshape(GRP, 256)
+
+    smooth_rows(rows_of, False, bands[0], avb)
+    hx_core[0:16, :] = obs_rows(avb, umat, (e_core,), (dcore,), w, dxs, norm)
     hx_core[16:24, :] = jnp.zeros((8, 256), F32)
     hx_core[16:17, :] = jnp.sum(s0[...], axis=0, keepdims=True)
     hx_core[17:18, :] = jnp.sum(gg, axis=0, keepdims=True)
@@ -336,7 +338,7 @@
     umat[...] = part[...] + adjoint_rows(
         ic * h_core[...], wt, (e_core,), (x_core[0:256, :],), ua, norm
     )
-    adjoint_finish((bands[2], bands[3]), umat, adj)
+    adjoint_finish(bands[1], umat, adj)
     for k, a in enumerate((a0, a1, a2, a3)):
         a[...] = adj[:, scal[1] ^ k].astype(BF16)
 
@@ -421,9 +423,7 @@
         return lax.ppermute(x, both, edge)
 
     def shuffle(parts):
-        return [parts[0]] + [
-            lax.ppermute(parts[k], "lev", lev_xor(k)) for k in range(1, 4)
-        ]
+        return [parts[0]] + [lax.ppermute(parts[k], "lev", lev_xor(k)) for k in range(1, 4)]
 
     def sum4(x, axis, pairs, steps):
         one, two, three = (
@@ -448,7 +448,7 @@
         densify_kernel,
         [
             sds((256, 256), BF16), sds((352, 256), BF16), sds((352, 256), BF16),
-            sds((4, GRP, GRP), BF16), sds((2, obs_n, pdev), F32),
+            sds((2, GRP, 3 * GRP), BF16), sds((2, obs_n, pdev), F32),
         ],
         (
             scal, far_off(neighbours), far_off(loc_blocks), far_off(inv_error),
@@ -457,7 +457,7 @@
         1,
         [
             pltpu.VMEM((12, 128, 128), F32), pltpu.VMEM(loc_blocks.shape, BF16),
-            pltpu.VMEM((256, 256), F32), pltpu.VMEM((16, 128), F32),
+            pltpu.VMEM((GRP, GRP), F32), pltpu.VMEM((16, 128), F32),
             pltpu.SMEM(neighbours.shape, jnp.int32), pltpu.VMEM((NS, lev), F32),
             pltpu.SemaphoreType.DMA((6,)),
         ],
@@ -505,14 +505,24 @@
 
     def reduce_obs(tag, core_msg, own, smooth):
         got = swap_core(core_msg)
-        (edge_row,) = call(
-            bind(edge_kernel, norm),
-            [row],
-            (smooth, e_edge, x_edge, w),
-            0,
-            [umat, pltpu.VMEM((lev, pdev), F32)],
-            mm,
-        )
+        if own is None:
+            own, edge_row = call(
+                bind(own_edge_kernel, norm),
+                [row, row],
+                (smooth, e_own, e_edge, d_own, x_edge, w),
+                0,
+                [umat, pltpu.VMEM((lev, 2 * pdev), F32)],
+                2 * mm,
+            )
+        else:
+            (edge_row,) = call(
+                bind(edge_kernel, norm),
+                [row],
+                (smooth, e_edge, x_edge, w),
+                0,
+                [umat, pltpu.VMEM((lev, pdev), F32)],
+                mm,
+            )
         mine = jnp.concatenate([own + got[:obs], edge_row], axis=0)
         other = swap_edge(mine)
         tot = mine + jnp.concatenate([other[obs:], other[:obs]], axis=0)
@@ -534,20 +544,16 @@
     h1_oe, h1_core, part = reduce_obs("a", hx_core, hx_own, avb)
     outs = call(
         bind(second_kernel, norm),
-        [chunk] * 4 + [flat, sds((obs + 8, pdev), F32), row],
-        (scal, part, h1_core, cm, e_own, e_core, d_own, x_core, bands, w, wt, s0),
+        [chunk] * 4 + [flat, sds((obs + 8, pdev), F32)],
+        (scal, part, h1_core, cm, e_core, x_core, bands, w, wt, s0),
         1,
-        [full, half, umat, pltpu.VMEM((lev, 2 * pdev), F32)],
-        6 * mm,
+        [full, half, umat, pltpu.VMEM((lev, pdev), F32)],
+        5 * mm,
     )
     aparts = shuffle(outs[:4])
-    (misfit,) = call(
-        misfit_kernel, [sds((40, pdev), F32)], (h1_oe, h1_core, obs_own, x_core), 0
-    )
-    hs, hd_core, part = reduce_obs("b", outs[5], outs[6], outs[4])
-    sums = call(
-        sums_kernel, [sds((8, pdev), F32)], (hs, hd_core, misfit, obs_own, x_core), 0
-    )[0]
+    (misfit,) = call(misfit_kernel, [sds((40, pdev), F32)], (h1_oe, h1_core, obs_own, x_core), 0)
+    hs, hd_core, part = reduce_obs("b", outs[5], None, outs[4])
+    sums = call(sums_kernel, [sds((8, pdev), F32)], (hs, hd_core, misfit, obs_own, x_core), 0)[0]
     bparts = call(
         bind(third_kernel, norm),
         [chunk] * 4,
@@ -557,11 +563,9 @@
         3 * mm,
     )
     bparts = shuffle(bparts)
-    sums = sums + lax.ppermute(sums, "tile", tile_xor(2))
-    sums = sums + lax.ppermute(sums, "tile", tile_xor(6))
+    sums = sum4(sums, "tile", tile_xor, (2, 4, 6))
     sums = sums + lax.ppermute(sums, both, far)
-    sums = sums + lax.ppermute(sums, "tile", tile_xor(16))
-    sums = sums + lax.ppermute(sums, "tile", tile_xor(48))
+    sums = sum4(sums, "tile", tile_xor, (16, 32, 48))
     whole = sds((members, ldev, pdev), F32)
     (grad_first,) = call(grad_first_kernel, [whole], (scal, control, *aparts), 1)
     count = float(members * lev * pdev * tiles)

time: 114 us -> 113 us (level); the launches traced: 114 us -> 111 us
  waiting for transfers between devices: 48.9 us -> 41.9 us
  starting transfers between devices: 46.6 us -> 51.5 us
    ppermute x6 -> x12, starting transfers between devices: 7.5 us -> 18.4 us  [sum4(): one, two, three = (lax.ppermute(x, axis, pairs(k)) for k in steps)]
    ppermute x4 -> x0, waiting for transfers between devices: 8.21 us -> none  [the longest x1 3.64 us: per_device(): sums = sums + lax.ppermute(sums, 'tile', tile_xor(2))]
    ppermute x4 -> x0, starting transfers between devices: 6.4 us -> none  [the longest x1 6.3 us: per_device(): sums = sums + lax.ppermute(sums, 'tile', tile_xor(16))]
    ppermute x12, waiting for transfers between devices: 15.4 us -> 19 us  [shuffle(): lax.ppermute(parts[k], 'lev', lev_xor(k))]
    ppermute x6 -> x12, waiting for transfers between devices: 4.98 us -> 3.33 us  [sum4(): one, two, three = (lax.ppermute(x, axis, pairs(k)) for k in steps)]
  transfers between devices with their start and end apart: 33 -> 35, of which waited for: 19 -> 17; matrix products, arithmetic and copies ran while one was open for 0% -> 0% of each run, Pallas kernels for 9% -> 9%
where the time goes in v6:
time: 113 us; the launch traced here: 111 us
  starting transfers between devices  51.5 us (46%)
  waiting for transfers between devices  41.9 us (37%)
  Pallas kernels  16.7 us (15%)
    ppermute x12, waiting for transfers between devices, shuffle(): lax.ppermute(parts[k], 'lev', lev_xor(k))  19 us
    ppermute x12, starting transfers between devices, shuffle(): lax.ppermute(parts[k], 'lev', lev_xor(k))  18.9 us
    ppermute x12, starting transfers between devices, sum4(): one, two, three = (lax.ppermute(x, axis, pairs(k)) for k in steps)  18.4 us
    pallas_call x15, Pallas kernels, call(): pl.pallas_call(body, out_shape=tuple(outs), in_specs=specs, out_specs=out...  16.7 us
    ppermute x4, waiting for transfers between devices, swap_edge(): return lax.ppermute(x, both, edge)  13.3 us
    ppermute x4, starting transfers between devices, swap_edge(): return lax.ppermute(x, both, edge)  13 us
    ppermute x1, waiting for transfers between devices, per_device(): sums = sums + lax.ppermute(sums, both, far)  4.73 us
    ppermute x12, waiting for transfers between devices, sum4(): one, two, three = (lax.ppermute(x, axis, pairs(k)) for k in steps)  3.33 us
  transfers between devices with their start and end apart: 35, of which 17 were waited for; matrix products, arithmetic and copies ran while one was open for 0% of the time, Pallas kernels for 9%

profile of v6, /device:TPU:2, one launch (start us, length us, event | category | flops | bytes accessed | tf_op | source)
XLA Modules:
  0.0 111.3 jit_solution(5465284805543129252)
XLA Ops:
  2.3 2.0 %collective-permute-start.3 = (bf16[20,8,256]{2,1,0:T(8,128)(2,1)S(1)}, bf16[20,8,256]{2,1,0:T(8,128)(2,1)S(1)}, u32[]{:S(2)}, u32[]{:S(2)}) collective-permute-start(bf16[20,8,256]{2,1,0:T(8,128)(2,1)S(1)} %get-tuple-element.42), channel_id=1, source_target_pairs={{0,1},{1,0},{2,3},{3,2},{4,5},{5,4},{6,7},{7,6},{8,9},{9,8},{10,11... | collective-permute-start | bytes 245768 | tf_op jit(solution)/shard_map/ppermute | solution.py:426
  4.3 3.3 %collective-permute-start.4 = (bf16[20,8,256]{2,1,0:T(8,128)(2,1)S(1)}, bf16[20,8,256]{2,1,0:T(8,128)(2,1)S(1)}, u32[]{:S(2)}, u32[]{:S(2)}) collective-permute-start(bf16[20,8,256]{2,1,0:T(8,128)(2,1)S(1)} %get-tuple-element.43), channel_id=1, source_target_pairs={{0,2},{1,3},{2,0},{3,1},{4,6},{5,7},{6,4},{7,5},{8,10},{9,11},{10,... | collective-permute-start | bytes 245768 | tf_op jit(solution)/shard_map/ppermute | solution.py:426
  7.6 6.5 %collective-permute-done.4.e2 = bf16[20,8,256]{2,1,0:T(8,128)(2,1)S(1)} collective-permute-done((bf16[20,8,256]{2,1,0:T(8,128)(2,1)S(1)}, bf16[20,8,256]{2,1,0:T(8,128)(2,1)S(1)}, u32[]{:S(2)}, u32[]{:S(2)}) %collective-permute-start.4) | collective-permute-done | bytes 81952 | tf_op jit(solution)/shard_map/ppermute | solution.py:426
  14.8 7.8 %collective-permute-start.9 = (bf16[20,4,8,256]{3,2,1,0:T(8,128)(2,1)S(1)}, bf16[20,4,8,256]{3,2,1,0:T(8,128)(2,1)S(1)}, u32[]{:S(2)}, u32[]{:S(2)}) collective-permute-start(bf16[20,4,8,256]{3,2,1,0:T(8,128)(2,1)S(1)} %shard_map.105.refs_5_.refs_2_.refs_1_), channel_id=1, source_target_pairs={{0,254},{1,255},{2,252},{3,253},{4,8},{5,9},{6,10},{7,11},{8,4},{9... | collective-permute-start | bytes 983048 | tf_op jit(solution)/shard_map/ppermute | solution.py:423
  24.0 1.9 %collective-permute-start.1 = (bf16[23,8,256]{2,1,0:T(8,128)(2,1)S(1)}, bf16[23,8,256]{2,1,0:T(8,128)(2,1)S(1)}, u32[]{:S(2)}, u32[]{:S(2)}) collective-permute-start(bf16[23,8,256]{2,1,0:T(8,128)(2,1)S(1)} %get-tuple-element.39), channel_id=1, source_target_pairs={{0,2},{1,3},{2,0},{3,1},{4,6},{5,7},{6,4},{7,5},{8,10},{9,11},{10,... | collective-permute-start | bytes 282632 | tf_op jit(solution)/shard_map/ppermute | solution.py:426
  25.8 2.1 %shard_map.106 = (bf16[256,256]{1,0:T(8,128)(2,1)S(1)}, bf16[352,256]{1,0:T(8,128)(2,1)S(1)}, bf16[352,256]{1,0:T(8,128)(2,1)S(1)}, bf16[2,128,384]{2,1,0:T(8,128)(2,1)S(1)}, f32[2,16,256]{2,1,0:T(8,128)S(1)}) custom-call(s32[4]{0:T(128)S(1)} %pad_add_fusion.scal.refs_0_, s32[2,9]{1,0:T(2,128)} %nb_hbm.1, bf16[2,9,128,128]{3,2,1,0:T(8,128)(2,1)} %loc_hbm.1, ...), custom_call_target="tpu_custom_call" | custom-call | bytes 1344728 | tf_op jit(solution)/shard_map/pallas_call | solution.py:28
  28.0 2.2 %collective-permute-done.refs_2_ = bf16[23,8,256]{2,1,0:T(8,128)(2,1)S(1)} collective-permute-done((bf16[23,8,256]{2,1,0:T(8,128)(2,1)S(1)}, bf16[23,8,256]{2,1,0:T(8,128)(2,1)S(1)}, u32[]{:S(2)}, u32[]{:S(2)}) %collective-permute-start) | collective-permute-done | bytes 94240 | tf_op jit(solution)/shard_map/ppermute | solution.py:426
  30.7 1.9 %collective-permute-start.2 = (bf16[23,8,256]{2,1,0:T(8,128)(2,1)S(1)}, bf16[23,8,256]{2,1,0:T(8,128)(2,1)S(1)}, u32[]{:S(2)}, u32[]{:S(2)}) collective-permute-start(bf16[23,8,256]{2,1,0:T(8,128)(2,1)S(1)} %get-tuple-element.40), channel_id=1, source_target_pairs={{0,3},{1,2},{2,1},{3,0},{4,7},{5,6},{6,5},{7,4},{8,11},{9,10},{10,... | collective-permute-start | bytes 282632 | tf_op jit(solution)/shard_map/ppermute | solution.py:426
  32.6 5.9 %collective-permute-done.2.refs_4_ = bf16[23,8,256]{2,1,0:T(8,128)(2,1)S(1)} collective-permute-done((bf16[23,8,256]{2,1,0:T(8,128)(2,1)S(1)}, bf16[23,8,256]{2,1,0:T(8,128)(2,1)S(1)}, u32[]{:S(2)}, u32[]{:S(2)}) %collective-permute-start.2) | collective-permute-done | bytes 94240 | tf_op jit(solution)/shard_map/ppermute | solution.py:426
  41.9 2.8 %collective-permute-start.11 = (f32[32,256]{1,0:T(8,128)S(1)}, f32[32,256]{1,0:T(8,128)S(1)}, u32[]{:S(2)}, u32[]{:S(2)}) collective-permute-start(f32[32,256]{1,0:T(8,128)S(1)} %pad_maximum_fusion.1), channel_id=1, source_target_pairs={{0,254},{1,255},{2,252},{3,253},{4,8},{5,9},{6,10},{7,11},{8,4},{9... | collective-permute-start | bytes 98312 | tf_op jit(solution)/shard_map/ppermute | solution.py:423
  44.6 5.8 %collective-permute-done.11 = f32[32,256]{1,0:T(8,128)S(1)} collective-permute-done((f32[32,256]{1,0:T(8,128)S(1)}, f32[32,256]{1,0:T(8,128)S(1)}, u32[]{:S(2)}, u32[]{:S(2)}) %collective-permute-start.11) | collective-permute-done | bytes 32800 | tf_op jit(solution)/shard_map/ppermute | solution.py:423
  50.5 2.0 %collective-permute-start.14 = (f32[32,256]{1,0:T(8,128)S(1)}, f32[32,256]{1,0:T(8,128)S(1)}, u32[]{:S(2)}, u32[]{:S(2)}) collective-permute-start(f32[32,256]{1,0:T(8,128)S(1)} %maximum_add_fusion), channel_id=1, source_target_pairs={{0,3},{1,2},{2,1},{3,0},{4,7},{5,6},{6,5},{7,4},{8,11},{9,10},{10,... | collective-permute-start | bytes 98312 | tf_op jit(solution)/shard_map/ppermute | solution.py:430
  58.1 2.4 %shard_map.110 = (bf16[20,8,256]{2,1,0:T(8,128)(2,1)S(1)}, bf16[20,8,256]{2,1,0:T(8,128)(2,1)S(1)}, bf16[20,8,256]{2,1,0:T(8,128)(2,1)S(1)}, bf16[20,8,256]{2,1,...) custom-call(s32[4]{0:T(128)S(1)} %pad_add_fusion.scal.refs_0_, ...), custom_call_target="tpu_custom_call" | custom-call | flops 419430400 | bytes 2416656 | tf_op jit(solution)/shard_map/pallas_call | solution.py:28
  61.8 2.1 %collective-permute-start.20 = (f32[32,256]{1,0:T(8,128)S(1)}, f32[32,256]{1,0:T(8,128)S(1)}, u32[]{:S(2)}, u32[]{:S(2)}) collective-permute-start(f32[32,256]{1,0:T(8,128)S(1)} %pad_maximum_fusion.2), channel_id=1, source_target_pairs={{0,254},{1,255},{2,252},{3,253},{4,8},{5,9},{6,10},{7,11},{8,4},{9... | collective-permute-start | bytes 98312 | tf_op jit(solution)/shard_map/ppermute | solution.py:423
  63.9 6.5 %collective-permute-done.20 = f32[32,256]{1,0:T(8,128)S(1)} collective-permute-done((f32[32,256]{1,0:T(8,128)S(1)}, f32[32,256]{1,0:T(8,128)S(1)}, u32[]{:S(2)}, u32[]{:S(2)}) %collective-permute-start.20) | collective-permute-done | bytes 32800 | tf_op jit(solution)/shard_map/ppermute | solution.py:423
  70.4 2.0 %collective-permute-start.22 = (f32[40,256]{1,0:T(8,128)S(1)}, f32[40,256]{1,0:T(8,128)S(1)}, u32[]{:S(2)}, u32[]{:S(2)}) collective-permute-start(f32[40,256]{1,0:T(8,128)S(1)} %pad_maximum_fusion), channel_id=1, source_target_pairs={{0,2},{1,3},{2,0},{3,1},{4,6},{5,7},{6,4},{7,5},{8,10},{9,11},{10,... | collective-permute-start | bytes 122888 | tf_op jit(solution)/shard_map/ppermute | solution.py:430
  74.1 2.0 %collective-permute-start.16 = (bf16[20,8,256]{2,1,0:T(8,128)(2,1)S(1)}, bf16[20,8,256]{2,1,0:T(8,128)(2,1)S(1)}, u32[]{:S(2)}, u32[]{:S(2)}) collective-permute-start(bf16[20,8,256]{2,1,0:T(8,128)(2,1)S(1)} %get-tuple-element.58), channel_id=1, source_target_pairs={{0,1},{1,0},{2,3},{3,2},{4,5},{5,4},{6,7},{7,6},{8,9},{9,8},{10,11... | collective-permute-start | bytes 245768 | tf_op jit(solution)/shard_map/ppermute | solution.py:426
  77.2 1.9 %collective-permute-start.18 = (bf16[20,8,256]{2,1,0:T(8,128)(2,1)S(1)}, bf16[20,8,256]{2,1,0:T(8,128)(2,1)S(1)}, u32[]{:S(2)}, u32[]{:S(2)}) collective-permute-start(bf16[20,8,256]{2,1,0:T(8,128)(2,1)S(1)} %get-tuple-element.60), channel_id=1, source_target_pairs={{0,3},{1,2},{2,1},{3,0},{4,7},{5,6},{6,5},{7,4},{8,11},{9,10},{10,... | collective-permute-start | bytes 245768 | tf_op jit(solution)/shard_map/ppermute | solution.py:426
  80.6 3.4 %collective-permute-start.28 = (f32[8,256]{1,0:T(8,128)S(1)}, f32[8,256]{1,0:T(8,128)S(1)}, u32[]{:S(2)}, u32[]{:S(2)}) collective-permute-start(f32[8,256]{1,0:T(8,128)S(1)} %shard_map.116), channel_id=1, source_target_pairs={{0,8},{4,12},{8,0},{12,4},{16,24},{20,28},{24,16},{28,20},{32,40},... | collective-permute-start | bytes 24584 | tf_op jit(solution)/shard_map/ppermute | solution.py:430
  86.8 4.7 %collective-permute-done.31 = f32[8,256]{1,0:T(8,128)S(1)} collective-permute-done((f32[8,256]{1,0:T(8,128)S(1)}, f32[8,256]{1,0:T(8,128)S(1)}, u32[]{:S(2)}, u32[]{:S(2)}) %collective-permute-start.31) | collective-permute-done | bytes 8224 | tf_op jit(solution)/shard_map/ppermute | solution.py:567
  91.5 2.5 %collective-permute-start.33 = (f32[8,256]{1,0:T(8,128)S(1)}, f32[8,256]{1,0:T(8,128)S(1)}, u32[]{:S(2)}, u32[]{:S(2)}) collective-permute-start(f32[8,256]{1,0:T(8,128)S(1)} %add.70), channel_id=1, source_target_pairs={{0,128},{4,132},{8,136},{12,140},{16,144},{20,148},{24,152},{28,15... | collective-permute-start | bytes 24584 | tf_op jit(solution)/shard_map/ppermute | solution.py:430
  94.0 5.2 %collective-permute-start.34 = (f32[8,256]{1,0:T(8,128)S(1)}, f32[8,256]{1,0:T(8,128)S(1)}, u32[]{:S(2)}, u32[]{:S(2)}) collective-permute-start(f32[8,256]{1,0:T(8,128)S(1)} %add.70), channel_id=1, source_target_pairs={{0,192},{4,196},{8,200},{12,204},{16,208},{20,212},{24,216},{28,22... | collective-permute-start | bytes 24584 | tf_op jit(solution)/shard_map/ppermute | solution.py:430
  103.2 1.9 %collective-permute-start.27 = (bf16[20,8,256]{2,1,0:T(8,128)(2,1)S(1)}, bf16[20,8,256]{2,1,0:T(8,128)(2,1)S(1)}, u32[]{:S(2)}, u32[]{:S(2)}) collective-permute-start(bf16[20,8,256]{2,1,0:T(8,128)(2,1)S(1)} %get-tuple-element.68), channel_id=1, source_target_pairs={{0,3},{1,2},{2,1},{3,0},{4,7},{5,6},{6,5},{7,4},{8,11},{9,10},{10,... | collective-permute-start | bytes 245768 | tf_op jit(solution)/shard_map/ppermute | solution.py:426
  106.0 2.0 %collective-permute-done.26.refs_8_ = bf16[20,8,256]{2,1,0:T(8,128)(2,1)S(1)} collective-permute-done((bf16[20,8,256]{2,1,0:T(8,128)(2,1)S(1)}, bf16[20,8,256]{2,1,0:T(8,128)(2,1)S(1)}, u32[]{:S(2)}, u32[]{:S(2)}) %collective-permute-start.26) | collective-permute-done | bytes 81952 | tf_op jit(solution)/shard_map/ppermute | solution.py:426
  (84 shorter events, 29.8 us)
Async XLA Ops:
  4.3 9.8 %collective-permute-start.4 = (bf16[20,8,256]{2,1,0:T(8,128)(2,1)S(1)}, bf16[20,8,256]{2,1,0:T(8,128)(2,1)S(1)}, u32[]{:S(2)}, u32[]{:S(2)}) collective-permute-start(bf16[20,8,256]{2,1,0:T(8,128)(2,1)S(1)} %get-tuple-element.43), channel_id=1, source_target_pairs={{0,2},{1,3},{2,0},{3,1},{4,6},{5,7},{6,4},{7,5},{8,10},{9,11},{10,... | collective-permute-start | bytes 245768 | tf_op jit(solution)/shard_map/ppermute | solution.py:426
  7.6 6.5 %collective-permute-start.5 = (bf16[20,8,256]{2,1,0:T(8,128)(2,1)S(1)}, bf16[20,8,256]{2,1,0:T(8,128)(2,1)S(1)}, u32[]{:S(2)}, u32[]{:S(2)}) collective-permute-start(bf16[20,8,256]{2,1,0:T(8,128)(2,1)S(1)} %get-tuple-element.44), channel_id=1, source_target_pairs={{0,3},{1,2},{2,1},{3,0},{4,7},{5,6},{6,5},{7,4},{8,11},{9,10},{10,... | collective-permute-start | bytes 245768 | tf_op jit(solution)/shard_map/ppermute | solution.py:426
  14.7 23.7 %collective-permute-start.6 = (bf16[20,4,8,256]{3,2,1,0:T(8,128)(2,1)S(1)}, bf16[20,4,8,256]{3,2,1,0:T(8,128)(2,1)S(1)}, u32[]{:S(2)}, u32[]{:S(2)}) collective-permute-start(bf16[20,4,8,256]{3,2,1,0:T(8,128)(2,1)S(1)} %shard_map.105.refs_5_.refs_2_.refs_1_), channel_id=1, source_target_pairs={{0,4},{4,0},{8,12},{12,8},{16,20},{20,16},{24,28},{28,24},{32,36},... | collective-permute-start | bytes 983048 | tf_op jit(solution)/shard_map/ppermute | solution.py:420
  14.8 26.5 %collective-permute-start.9 = (bf16[20,4,8,256]{3,2,1,0:T(8,128)(2,1)S(1)}, bf16[20,4,8,256]{3,2,1,0:T(8,128)(2,1)S(1)}, u32[]{:S(2)}, u32[]{:S(2)}) collective-permute-start(bf16[20,4,8,256]{3,2,1,0:T(8,128)(2,1)S(1)} %shard_map.105.refs_5_.refs_2_.refs_1_), channel_id=1, source_target_pairs={{0,254},{1,255},{2,252},{3,253},{4,8},{5,9},{6,10},{7,11},{8,4},{9... | collective-permute-start | bytes 983048 | tf_op jit(solution)/shard_map/ppermute | solution.py:423
  23.3 7.0 %collective-permute-start = (bf16[23,8,256]{2,1,0:T(8,128)(2,1)S(1)}, bf16[23,8,256]{2,1,0:T(8,128)(2,1)S(1)}, u32[]{:S(2)}, u32[]{:S(2)}) collective-permute-start(bf16[23,8,256]{2,1,0:T(8,128)(2,1)S(1)} %get-tuple-element.38), channel_id=1, source_target_pairs={{0,1},{1,0},{2,3},{3,2},{4,5},{5,4},{6,7},{7,6},{8,9},{9,8},{10,11... | collective-permute-start | bytes 282632 | tf_op jit(solution)/shard_map/ppermute | solution.py:426
  24.0 6.7 %collective-permute-start.1 = (bf16[23,8,256]{2,1,0:T(8,128)(2,1)S(1)}, bf16[23,8,256]{2,1,0:T(8,128)(2,1)S(1)}, u32[]{:S(2)}, u32[]{:S(2)}) collective-permute-start(bf16[23,8,256]{2,1,0:T(8,128)(2,1)S(1)} %get-tuple-element.39), channel_id=1, source_target_pairs={{0,2},{1,3},{2,0},{3,1},{4,6},{5,7},{6,4},{7,5},{8,10},{9,11},{10,... | collective-permute-start | bytes 282632 | tf_op jit(solution)/shard_map/ppermute | solution.py:426
  27.9 10.5 %collective-permute-start.7 = (bf16[352,256]{1,0:T(8,128)(2,1)S(1)}, bf16[352,256]{1,0:T(8,128)(2,1)S(1)}, u32[]{:S(2)}, u32[]{:S(2)}) collective-permute-start(bf16[352,256]{1,0:T(8,128)(2,1)S(1)} %get-tuple-element.46), channel_id=1, source_target_pairs={{0,4},{4,0},{8,12},{12,8},{16,20},{20,16},{24,28},{28,24},{32,36},... | collective-permute-start | bytes 540680 | tf_op jit(solution)/shard_map/ppermute | solution.py:420
  30.2 11.0 %collective-permute-start.10 = (bf16[352,256]{1,0:T(8,128)(2,1)S(1)}, bf16[352,256]{1,0:T(8,128)(2,1)S(1)}, u32[]{:S(2)}, u32[]{:S(2)}) collective-permute-start(bf16[352,256]{1,0:T(8,128)(2,1)S(1)} %get-tuple-element.51), channel_id=1, source_target_pairs={{0,254},{1,255},{2,252},{3,253},{4,8},{5,9},{6,10},{7,11},{8,4},{9... | collective-permute-start | bytes 540680 | tf_op jit(solution)/shard_map/ppermute | solution.py:423
  30.7 7.8 %collective-permute-start.2 = (bf16[23,8,256]{2,1,0:T(8,128)(2,1)S(1)}, bf16[23,8,256]{2,1,0:T(8,128)(2,1)S(1)}, u32[]{:S(2)}, u32[]{:S(2)}) collective-permute-start(bf16[23,8,256]{2,1,0:T(8,128)(2,1)S(1)} %get-tuple-element.40), channel_id=1, source_target_pairs={{0,3},{1,2},{2,1},{3,0},{4,7},{5,6},{6,5},{7,4},{8,11},{9,10},{10,... | collective-permute-start | bytes 282632 | tf_op jit(solution)/shard_map/ppermute | solution.py:426
  41.9 8.5 %collective-permute-start.11 = (f32[32,256]{1,0:T(8,128)S(1)}, f32[32,256]{1,0:T(8,128)S(1)}, u32[]{:S(2)}, u32[]{:S(2)}) collective-permute-start(f32[32,256]{1,0:T(8,128)S(1)} %pad_maximum_fusion.1), channel_id=1, source_target_pairs={{0,254},{1,255},{2,252},{3,253},{4,8},{5,9},{6,10},{7,11},{8,4},{9... | collective-permute-start | bytes 98312 | tf_op jit(solution)/shard_map/ppermute | solution.py:423
  50.5 6.0 %collective-permute-start.14 = (f32[32,256]{1,0:T(8,128)S(1)}, f32[32,256]{1,0:T(8,128)S(1)}, u32[]{:S(2)}, u32[]{:S(2)}) collective-permute-start(f32[32,256]{1,0:T(8,128)S(1)} %maximum_add_fusion), channel_id=1, source_target_pairs={{0,3},{1,2},{2,1},{3,0},{4,7},{5,6},{6,5},{7,4},{8,11},{9,10},{10,... | collective-permute-start | bytes 98312 | tf_op jit(solution)/shard_map/ppermute | solution.py:430
  61.8 8.6 %collective-permute-start.20 = (f32[32,256]{1,0:T(8,128)S(1)}, f32[32,256]{1,0:T(8,128)S(1)}, u32[]{:S(2)}, u32[]{:S(2)}) collective-permute-start(f32[32,256]{1,0:T(8,128)S(1)} %pad_maximum_fusion.2), channel_id=1, source_target_pairs={{0,254},{1,255},{2,252},{3,253},{4,8},{5,9},{6,10},{7,11},{8,4},{9... | collective-permute-start | bytes 98312 | tf_op jit(solution)/shard_map/ppermute | solution.py:423
  70.4 6.7 %collective-permute-start.22 = (f32[40,256]{1,0:T(8,128)S(1)}, f32[40,256]{1,0:T(8,128)S(1)}, u32[]{:S(2)}, u32[]{:S(2)}) collective-permute-start(f32[40,256]{1,0:T(8,128)S(1)} %pad_maximum_fusion), channel_id=1, source_target_pairs={{0,2},{1,3},{2,0},{3,1},{4,6},{5,7},{6,4},{7,5},{8,10},{9,11},{10,... | collective-permute-start | bytes 122888 | tf_op jit(solution)/shard_map/ppermute | solution.py:430
  72.4 6.6 %collective-permute-start.23 = (f32[40,256]{1,0:T(8,128)S(1)}, f32[40,256]{1,0:T(8,128)S(1)}, u32[]{:S(2)}, u32[]{:S(2)}) collective-permute-start(f32[40,256]{1,0:T(8,128)S(1)} %pad_maximum_fusion), channel_id=1, source_target_pairs={{0,3},{1,2},{2,1},{3,0},{4,7},{5,6},{6,5},{7,4},{8,11},{9,10},{10,... | collective-permute-start | bytes 122888 | tf_op jit(solution)/shard_map/ppermute | solution.py:430
  74.1 6.5 %collective-permute-start.16 = (bf16[20,8,256]{2,1,0:T(8,128)(2,1)S(1)}, bf16[20,8,256]{2,1,0:T(8,128)(2,1)S(1)}, u32[]{:S(2)}, u32[]{:S(2)}) collective-permute-start(bf16[20,8,256]{2,1,0:T(8,128)(2,1)S(1)} %get-tuple-element.58), channel_id=1, source_target_pairs={{0,1},{1,0},{2,3},{3,2},{4,5},{5,4},{6,7},{7,6},{8,9},{9,8},{10,11... | collective-permute-start | bytes 245768 | tf_op jit(solution)/shard_map/ppermute | solution.py:426
  76.1 7.9 %collective-permute-start.17 = (bf16[20,8,256]{2,1,0:T(8,128)(2,1)S(1)}, bf16[20,8,256]{2,1,0:T(8,128)(2,1)S(1)}, u32[]{:S(2)}, u32[]{:S(2)}) collective-permute-start(bf16[20,8,256]{2,1,0:T(8,128)(2,1)S(1)} %get-tuple-element.59), channel_id=1, source_target_pairs={{0,2},{1,3},{2,0},{3,1},{4,6},{5,7},{6,4},{7,5},{8,10},{9,11},{10,... | collective-permute-start | bytes 245768 | tf_op jit(solution)/shard_map/ppermute | solution.py:426
  77.2 6.8 %collective-permute-start.18 = (bf16[20,8,256]{2,1,0:T(8,128)(2,1)S(1)}, bf16[20,8,256]{2,1,0:T(8,128)(2,1)S(1)}, u32[]{:S(2)}, u32[]{:S(2)}) collective-permute-start(bf16[20,8,256]{2,1,0:T(8,128)(2,1)S(1)} %get-tuple-element.60), channel_id=1, source_target_pairs={{0,3},{1,2},{2,1},{3,0},{4,7},{5,6},{6,5},{7,4},{8,11},{9,10},{10,... | collective-permute-start | bytes 245768 | tf_op jit(solution)/shard_map/ppermute | solution.py:426
  85.6 5.8 %collective-permute-start.31 = (f32[8,256]{1,0:T(8,128)S(1)}, f32[8,256]{1,0:T(8,128)S(1)}, u32[]{:S(2)}, u32[]{:S(2)}) collective-permute-start(f32[8,256]{1,0:T(8,128)S(1)} %add_add_fusion.3), channel_id=1, source_target_pairs={{0,34},{1,35},{2,32},{3,33},{4,38},{5,39},{6,36},{7,37},{8,42},{9,... | collective-permute-start | bytes 24584 | tf_op jit(solution)/shard_map/ppermute | solution.py:567
  91.5 11.7 %collective-permute-start.33 = (f32[8,256]{1,0:T(8,128)S(1)}, f32[8,256]{1,0:T(8,128)S(1)}, u32[]{:S(2)}, u32[]{:S(2)}) collective-permute-start(f32[8,256]{1,0:T(8,128)S(1)} %add.70), channel_id=1, source_target_pairs={{0,128},{4,132},{8,136},{12,140},{16,144},{20,148},{24,152},{28,15... | collective-permute-start | bytes 24584 | tf_op jit(solution)/shard_map/ppermute | solution.py:430
  94.0 11.1 %collective-permute-start.34 = (f32[8,256]{1,0:T(8,128)S(1)}, f32[8,256]{1,0:T(8,128)S(1)}, u32[]{:S(2)}, u32[]{:S(2)}) collective-permute-start(f32[8,256]{1,0:T(8,128)S(1)} %add.70), channel_id=1, source_target_pairs={{0,192},{4,196},{8,200},{12,204},{16,208},{20,212},{24,216},{28,22... | collective-permute-start | bytes 24584 | tf_op jit(solution)/shard_map/ppermute | solution.py:430
  99.2 5.9 %collective-permute-start.32 = (f32[8,256]{1,0:T(8,128)S(1)}, f32[8,256]{1,0:T(8,128)S(1)}, u32[]{:S(2)}, u32[]{:S(2)}) collective-permute-start(f32[8,256]{1,0:T(8,128)S(1)} %add.70), channel_id=1, source_target_pairs={{0,64},{4,68},{8,72},{12,76},{16,80},{20,84},{24,88},{28,92},{32,9... | collective-permute-start | bytes 24584 | tf_op jit(solution)/shard_map/ppermute | solution.py:430
  100.6 5.4 %collective-permute-start.25 = (bf16[20,8,256]{2,1,0:T(8,128)(2,1)S(1)}, bf16[20,8,256]{2,1,0:T(8,128)(2,1)S(1)}, u32[]{:S(2)}, u32[]{:S(2)}) collective-permute-start(bf16[20,8,256]{2,1,0:T(8,128)(2,1)S(1)} %get-tuple-element.66), channel_id=1, source_target_pairs={{0,1},{1,0},{2,3},{3,2},{4,5},{5,4},{6,7},{7,6},{8,9},{9,8},{10,11... | collective-permute-start | bytes 245768 | tf_op jit(solution)/shard_map/ppermute | solution.py:426
  101.8 6.2 %collective-permute-start.26 = (bf16[20,8,256]{2,1,0:T(8,128)(2,1)S(1)}, bf16[20,8,256]{2,1,0:T(8,128)(2,1)S(1)}, u32[]{:S(2)}, u32[]{:S(2)}) collective-permute-start(bf16[20,8,256]{2,1,0:T(8,128)(2,1)S(1)} %get-tuple-element.67), channel_id=1, source_target_pairs={{0,2},{1,3},{2,0},{3,1},{4,6},{5,7},{6,4},{7,5},{8,10},{9,11},{10,... | collective-permute-start | bytes 245768 | tf_op jit(solution)/shard_map/ppermute | solution.py:426
  103.2 6.3 %collective-permute-start.27 = (bf16[20,8,256]{2,1,0:T(8,128)(2,1)S(1)}, bf16[20,8,256]{2,1,0:T(8,128)(2,1)S(1)}, u32[]{:S(2)}, u32[]{:S(2)}) collective-permute-start(bf16[20,8,256]{2,1,0:T(8,128)(2,1)S(1)} %get-tuple-element.68), channel_id=1, source_target_pairs={{0,3},{1,2},{2,1},{3,0},{4,7},{5,6},{6,5},{7,4},{8,11},{9,10},{10,... | collective-permute-start | bytes 245768 | tf_op jit(solution)/shard_map/ppermute | solution.py:426
  (13 other events, 70.8 us)

commit v7 on v6

--- a/solution.py
+++ b/solution.py
@@ -52,14 +52,16 @@
     return (hi.astype(F32) + mid.astype(F32)) + lo.astype(F32)
 
 
-def pack_ens_kernel(scal, ens, *refs):
-    outs, sems = refs[:4], refs[4]
+def pack_ens_kernel(scal, ens, loc, inv, inn, vbt, nb, *refs):
+    outs, (loc_out, obs_out, vbt_out, nb_out, sems) = refs[:4], refs[4:]
     share = outs[0].shape[0]
+    moves = [(ens.at[pl.ds(share * (scal[2] ^ k), share)], outs[k]) for k in range(4)]
+    moves += [
+        (loc, loc_out), (inv, obs_out.at[0]), (inn, obs_out.at[1]), (vbt, vbt_out),
+        (nb, nb_out),
+    ]
     copies = [
-        pltpu.make_async_copy(
-            ens.at[pl.ds(share * (scal[2] ^ k), share)], outs[k], sems.at[k]
-        )
-        for k in range(4)
+        pltpu.make_async_copy(src, dst, sems.at[i]) for i, (src, dst) in enumerate(moves)
     ]
     for c in copies:
         c.start()
@@ -84,21 +86,11 @@
 
 
 def densify_kernel(
-    scal, nb_hbm, loc_hbm, inv_hbm, inn_hbm, vbt_hbm, d_own, x_core, x_edge, bands, obs, acc, loc, mat,
-    narrow, nb, vbt, sems,
+    scal, nb_near, loc, obs, vbt, d_own, x_core, x_edge, bands, acc, mat, narrow, nb, sem
 ):
-    copies = [
-        pltpu.make_async_copy(loc_hbm.at[0], loc.at[0], sems.at[0]),
-        pltpu.make_async_copy(loc_hbm.at[1], loc.at[1], sems.at[1]),
-        pltpu.make_async_copy(inv_hbm, obs.at[0], sems.at[2]),
-        pltpu.make_async_copy(inn_hbm, obs.at[1], sems.at[3]),
-        pltpu.make_async_copy(nb_hbm, nb, sems.at[4]),
-        pltpu.make_async_copy(vbt_hbm, vbt, sems.at[5]),
-    ]
-    for c in copies:
-        c.start()
+    fetch = pltpu.make_async_copy(nb_near, nb, sem)
+    fetch.start()
     narrow[...] = jnp.zeros(narrow.shape, F32)
-    copies[5].wait()
     narrow[0:NS, 0:32] = vbt[...]
     band = narrow[...]
     band = band + pltpu.roll(band, 32, 1)
@@ -121,9 +113,8 @@
     tile = scal[0]
     core_rel = 2 - 2 * (tile & 1)
     acc[...] = jnp.zeros(acc.shape, F32)
-    copies[4].wait()
+    fetch.wait()
     for b in range(2):
-        copies[b].wait()
         for j in range(loc.shape[1]):
             n = nb[b, j]
             rel = ((n >> 1) - tile + 65) & 63
@@ -136,8 +127,6 @@
                 out[128 * b : 128 * b + 128, 128 * h : 128 * h + 128] = acc[
                     b * 6 + role * 2 + h
                 ].astype(BF16)
-    copies[2].wait()
-    copies[3].wait()
     for out in (x_core, x_edge):
         for i, v in enumerate(split3(obs[0]) + split3(obs[1])):
             out[256 + 16 * i : 272 + 16 * i, :] = v
@@ -437,31 +426,36 @@
     def far_off(x):
         return pltpu.with_memory_space_constraint(x, pltpu.HBM)
 
-    eparts = call(
-        pack_ens_kernel, [chunk] * 4, (scal, far_off(ensemble)), 1,
-        [pltpu.SemaphoreType.DMA((4,))],
-        specs=[SM, hbm],
+    obs_n = channel_weights.shape[0]
+    *eparts, loc_near, obs_own, vbt, nb_near = call(
+        pack_ens_kernel,
+        [chunk] * 4
+        + [
+            sds(loc_blocks.shape, BF16), sds((2, obs_n, pdev), F32),
+            sds(vert_band.shape[::-1], F32), sds(neighbours.shape, jnp.int32),
+        ],
+        (
+            scal, far_off(ensemble), far_off(loc_blocks), far_off(inv_error),
+            far_off(innovation), far_off(vert_band.T), far_off(neighbours),
+        ),
+        1,
+        [pltpu.SemaphoreType.DMA((9,))],
+        specs=[SM, hbm, hbm, hbm, hbm, hbm, hbm],
     )
     eparts = shuffle(eparts)
-    obs_n = channel_weights.shape[0]
-    d_own, x_core, x_edge, bands, obs_own = call(
+    d_own, x_core, x_edge, bands = call(
         densify_kernel,
         [
             sds((256, 256), BF16), sds((352, 256), BF16), sds((352, 256), BF16),
-            sds((2, GRP, 3 * GRP), BF16), sds((2, obs_n, pdev), F32),
+            sds((2, GRP, 3 * GRP), BF16),
         ],
-        (
-            scal, far_off(neighbours), far_off(loc_blocks), far_off(inv_error),
-            far_off(innovation), far_off(vert_band.T),
-        ),
+        (scal, nb_near, loc_near, obs_own, vbt),
         1,
         [
-            pltpu.VMEM((12, 128, 128), F32), pltpu.VMEM(loc_blocks.shape, BF16),
-            pltpu.VMEM((GRP, GRP), F32), pltpu.VMEM((16, 128), F32),
-            pltpu.SMEM(neighbours.shape, jnp.int32), pltpu.VMEM((NS, lev), F32),
-            pltpu.SemaphoreType.DMA((6,)),
+            pltpu.VMEM((12, 128, 128), F32), pltpu.VMEM((GRP, GRP), F32),
+            pltpu.VMEM((16, 128), F32), pltpu.SMEM(neighbours.shape, jnp.int32),
+            pltpu.SemaphoreType.DMA,
         ],
-        specs=[SM, hbm, hbm, hbm, hbm, hbm],
     )
     wt_own = jnp.pad(channel_weights.T, ((0, 0), (0, pdev - channel_weights.shape[0])))
     packed = call(
@@ -563,8 +557,8 @@
         3 * mm,
     )
     bparts = shuffle(bparts)
+    sums = sums + lax.ppermute(sums, both, far)
     sums = sum4(sums, "tile", tile_xor, (2, 4, 6))
-    sums = sums + lax.ppermute(sums, both, far)
     sums = sum4(sums, "tile", tile_xor, (16, 32, 48))
     whole = sds((members, ldev, pdev), F32)
     (grad_first,) = call(grad_first_kernel, [whole], (scal, control, *aparts), 1)

time: 113 us -> 114 us (level)
    ppermute x12, waiting for transfers between devices: 19 us -> 22.8 us  [shuffle(): lax.ppermute(parts[k], 'lev', lev_xor(k))]
    ppermute x1, waiting for transfers between devices: 4.73 us -> 1.23 us  [per_device(): sums = sums + lax.ppermute(sums, both, far)]
  transfers between devices with their start and end apart: 35 -> 35, of which waited for: 17 -> 19; matrix products, arithmetic and copies ran while one was open for 0% -> 0% of each run, Pallas kernels for 9% -> 9%
where the time goes in v7:
time: 114 us; the launch traced here: 112 us
  starting transfers between devices  51.2 us (45%)
  waiting for transfers between devices  42.9 us (38%)
  Pallas kernels  16.3 us (14%)
    ppermute x12, waiting for transfers between devices, shuffle(): lax.ppermute(parts[k], 'lev', lev_xor(k))  22.8 us
    ppermute x12, starting transfers between devices, shuffle(): lax.ppermute(parts[k], 'lev', lev_xor(k))  18.9 us
    ppermute x12, starting transfers between devices, sum4(): one, two, three = (lax.ppermute(x, axis, pairs(k)) for k in steps)  18.4 us
    pallas_call x15, Pallas kernels, call(): pl.pallas_call(body, out_shape=tuple(outs), in_specs=specs, out_specs=out...  16.3 us
    ppermute x4, waiting for transfers between devices, swap_edge(): return lax.ppermute(x, both, edge)  13.3 us
    ppermute x4, starting transfers between devices, swap_edge(): return lax.ppermute(x, both, edge)  13 us
    ppermute x12, waiting for transfers between devices, sum4(): one, two, three = (lax.ppermute(x, axis, pairs(k)) for k in steps)  4.03 us
  transfers between devices with their start and end apart: 35, of which 19 were waited for; matrix products, arithmetic and copies ran while one was open for 0% of the time, Pallas kernels for 9%

profile of v7, /device:TPU:2, one launch (start us, length us, event | category | flops | bytes accessed | tf_op | source)
XLA Modules:
  0.0 111.6 jit_solution(6599109518182316472)
XLA Ops:
  0.7 1.9 %shard_map.104 = (bf16[20,8,256]{2,1,0:T(8,128)(2,1)S(1)}, bf16[20,8,256]{2,1,0:T(8,128)(2,1)S(1)}, bf16[20,8,256]{2,1,0:T(8,128)(2,1)S(1)}, bf16[20,8,256]{2,1,...) custom-call(s32[4]{0:T(128)S(1)} %pad_add_fusion.scal.refs_0_, ...), custom_call_target="tpu_custom_call" | custom-call | bytes 1903008 | tf_op jit(solution)/shard_map/pallas_call | solution.py:28
  2.6 2.0 %collective-permute-start.3 = (bf16[20,8,256]{2,1,0:T(8,128)(2,1)S(1)}, bf16[20,8,256]{2,1,0:T(8,128)(2,1)S(1)}, u32[]{:S(2)}, u32[]{:S(2)}) collective-permute-start(bf16[20,8,256]{2,1,0:T(8,128)(2,1)S(1)} %get-tuple-element.45), channel_id=1, source_target_pairs={{0,1},{1,0},{2,3},{3,2},{4,5},{5,4},{6,7},{7,6},{8,9},{9,8},{10,11... | collective-permute-start | bytes 245768 | tf_op jit(solution)/shard_map/ppermute | solution.py:415
  4.6 3.3 %collective-permute-start.4 = (bf16[20,8,256]{2,1,0:T(8,128)(2,1)S(1)}, bf16[20,8,256]{2,1,0:T(8,128)(2,1)S(1)}, u32[]{:S(2)}, u32[]{:S(2)}) collective-permute-start(bf16[20,8,256]{2,1,0:T(8,128)(2,1)S(1)} %get-tuple-element.46), channel_id=1, source_target_pairs={{0,2},{1,3},{2,0},{3,1},{4,6},{5,7},{6,4},{7,5},{8,10},{9,11},{10,... | collective-permute-start | bytes 245768 | tf_op jit(solution)/shard_map/ppermute | solution.py:415
  7.9 6.5 %collective-permute-done.4.e2 = bf16[20,8,256]{2,1,0:T(8,128)(2,1)S(1)} collective-permute-done((bf16[20,8,256]{2,1,0:T(8,128)(2,1)S(1)}, bf16[20,8,256]{2,1,0:T(8,128)(2,1)S(1)}, u32[]{:S(2)}, u32[]{:S(2)}) %collective-permute-start.4) | collective-permute-done | bytes 81952 | tf_op jit(solution)/shard_map/ppermute | solution.py:415
  15.0 7.8 %collective-permute-start.9 = (bf16[20,4,8,256]{3,2,1,0:T(8,128)(2,1)S(1)}, bf16[20,4,8,256]{3,2,1,0:T(8,128)(2,1)S(1)}, u32[]{:S(2)}, u32[]{:S(2)}) collective-permute-start(bf16[20,4,8,256]{3,2,1,0:T(8,128)(2,1)S(1)} %shard_map.105.refs_5_.refs_2_.refs_1_), channel_id=1, source_target_pairs={{0,254},{1,255},{2,252},{3,253},{4,8},{5,9},{6,10},{7,11},{8,4},{9... | collective-permute-start | bytes 983048 | tf_op jit(solution)/shard_map/ppermute | solution.py:412
  24.2 1.9 %collective-permute-start.1 = (bf16[23,8,256]{2,1,0:T(8,128)(2,1)S(1)}, bf16[23,8,256]{2,1,0:T(8,128)(2,1)S(1)}, u32[]{:S(2)}, u32[]{:S(2)}) collective-permute-start(bf16[23,8,256]{2,1,0:T(8,128)(2,1)S(1)} %get-tuple-element.42), channel_id=1, source_target_pairs={{0,2},{1,3},{2,0},{3,1},{4,6},{5,7},{6,4},{7,5},{8,10},{9,11},{10,... | collective-permute-start | bytes 282632 | tf_op jit(solution)/shard_map/ppermute | solution.py:415
  27.6 2.9 %collective-permute-done.refs_2_ = bf16[23,8,256]{2,1,0:T(8,128)(2,1)S(1)} collective-permute-done((bf16[23,8,256]{2,1,0:T(8,128)(2,1)S(1)}, bf16[23,8,256]{2,1,0:T(8,128)(2,1)S(1)}, u32[]{:S(2)}, u32[]{:S(2)}) %collective-permute-start) | collective-permute-done | bytes 94240 | tf_op jit(solution)/shard_map/ppermute | solution.py:415
  30.9 1.9 %collective-permute-start.2 = (bf16[23,8,256]{2,1,0:T(8,128)(2,1)S(1)}, bf16[23,8,256]{2,1,0:T(8,128)(2,1)S(1)}, u32[]{:S(2)}, u32[]{:S(2)}) collective-permute-start(bf16[23,8,256]{2,1,0:T(8,128)(2,1)S(1)} %get-tuple-element.43), channel_id=1, source_target_pairs={{0,3},{1,2},{2,1},{3,0},{4,7},{5,6},{6,5},{7,4},{8,11},{9,10},{10,... | collective-permute-start | bytes 282632 | tf_op jit(solution)/shard_map/ppermute | solution.py:415
  32.8 5.9 %collective-permute-done.2.refs_4_ = bf16[23,8,256]{2,1,0:T(8,128)(2,1)S(1)} collective-permute-done((bf16[23,8,256]{2,1,0:T(8,128)(2,1)S(1)}, bf16[23,8,256]{2,1,0:T(8,128)(2,1)S(1)}, u32[]{:S(2)}, u32[]{:S(2)}) %collective-permute-start.2) | collective-permute-done | bytes 94240 | tf_op jit(solution)/shard_map/ppermute | solution.py:415
  42.1 2.8 %collective-permute-start.11 = (f32[32,256]{1,0:T(8,128)S(1)}, f32[32,256]{1,0:T(8,128)S(1)}, u32[]{:S(2)}, u32[]{:S(2)}) collective-permute-start(f32[32,256]{1,0:T(8,128)S(1)} %pad_maximum_fusion.1), channel_id=1, source_target_pairs={{0,254},{1,255},{2,252},{3,253},{4,8},{5,9},{6,10},{7,11},{8,4},{9... | collective-permute-start | bytes 98312 | tf_op jit(solution)/shard_map/ppermute | solution.py:412
  44.9 5.8 %collective-permute-done.11 = f32[32,256]{1,0:T(8,128)S(1)} collective-permute-done((f32[32,256]{1,0:T(8,128)S(1)}, f32[32,256]{1,0:T(8,128)S(1)}, u32[]{:S(2)}, u32[]{:S(2)}) %collective-permute-start.11) | collective-permute-done | bytes 32800 | tf_op jit(solution)/shard_map/ppermute | solution.py:412
  50.8 2.0 %collective-permute-start.14 = (f32[32,256]{1,0:T(8,128)S(1)}, f32[32,256]{1,0:T(8,128)S(1)}, u32[]{:S(2)}, u32[]{:S(2)}) collective-permute-start(f32[32,256]{1,0:T(8,128)S(1)} %maximum_add_fusion), channel_id=1, source_target_pairs={{0,3},{1,2},{2,1},{3,0},{4,7},{5,6},{6,5},{7,4},{8,11},{9,10},{10,... | collective-permute-start | bytes 98312 | tf_op jit(solution)/shard_map/ppermute | solution.py:419
  58.3 2.4 %shard_map.110 = (bf16[20,8,256]{2,1,0:T(8,128)(2,1)S(1)}, bf16[20,8,256]{2,1,0:T(8,128)(2,1)S(1)}, bf16[20,8,256]{2,1,0:T(8,128)(2,1)S(1)}, bf16[20,8,256]{2,1,...) custom-call(s32[4]{0:T(128)S(1)} %pad_add_fusion.scal.refs_0_, ...), custom_call_target="tpu_custom_call" | custom-call | flops 419430400 | bytes 2416656 | tf_op jit(solution)/shard_map/pallas_call | solution.py:28
  62.1 2.1 %collective-permute-start.20 = (f32[32,256]{1,0:T(8,128)S(1)}, f32[32,256]{1,0:T(8,128)S(1)}, u32[]{:S(2)}, u32[]{:S(2)}) collective-permute-start(f32[32,256]{1,0:T(8,128)S(1)} %pad_maximum_fusion.2), channel_id=1, source_target_pairs={{0,254},{1,255},{2,252},{3,253},{4,8},{5,9},{6,10},{7,11},{8,4},{9... | collective-permute-start | bytes 98312 | tf_op jit(solution)/shard_map/ppermute | solution.py:412
  64.2 6.5 %collective-permute-done.20 = f32[32,256]{1,0:T(8,128)S(1)} collective-permute-done((f32[32,256]{1,0:T(8,128)S(1)}, f32[32,256]{1,0:T(8,128)S(1)}, u32[]{:S(2)}, u32[]{:S(2)}) %collective-permute-start.20) | collective-permute-done | bytes 32800 | tf_op jit(solution)/shard_map/ppermute | solution.py:412
  70.7 2.0 %collective-permute-start.22 = (f32[40,256]{1,0:T(8,128)S(1)}, f32[40,256]{1,0:T(8,128)S(1)}, u32[]{:S(2)}, u32[]{:S(2)}) collective-permute-start(f32[40,256]{1,0:T(8,128)S(1)} %pad_maximum_fusion), channel_id=1, source_target_pairs={{0,2},{1,3},{2,0},{3,1},{4,6},{5,7},{6,4},{7,5},{8,10},{9,11},{10,... | collective-permute-start | bytes 122888 | tf_op jit(solution)/shard_map/ppermute | solution.py:419
  74.3 2.0 %collective-permute-start.16 = (bf16[20,8,256]{2,1,0:T(8,128)(2,1)S(1)}, bf16[20,8,256]{2,1,0:T(8,128)(2,1)S(1)}, u32[]{:S(2)}, u32[]{:S(2)}) collective-permute-start(bf16[20,8,256]{2,1,0:T(8,128)(2,1)S(1)} %get-tuple-element.64), channel_id=1, source_target_pairs={{0,1},{1,0},{2,3},{3,2},{4,5},{5,4},{6,7},{7,6},{8,9},{9,8},{10,11... | collective-permute-start | bytes 245768 | tf_op jit(solution)/shard_map/ppermute | solution.py:415
  77.4 1.9 %collective-permute-start.18 = (bf16[20,8,256]{2,1,0:T(8,128)(2,1)S(1)}, bf16[20,8,256]{2,1,0:T(8,128)(2,1)S(1)}, u32[]{:S(2)}, u32[]{:S(2)}) collective-permute-start(bf16[20,8,256]{2,1,0:T(8,128)(2,1)S(1)} %get-tuple-element.66), channel_id=1, source_target_pairs={{0,3},{1,2},{2,1},{3,0},{4,7},{5,6},{6,5},{7,4},{8,11},{9,10},{10,... | collective-permute-start | bytes 245768 | tf_op jit(solution)/shard_map/ppermute | solution.py:415
  80.8 1.8 %collective-permute-done.17.a2.refs_4_ = bf16[20,8,256]{2,1,0:T(8,128)(2,1)S(1)} collective-permute-done((bf16[20,8,256]{2,1,0:T(8,128)(2,1)S(1)}, bf16[20,8,256]{2,1,0:T(8,128)(2,1)S(1)}, u32[]{:S(2)}, u32[]{:S(2)}) %collective-permute-start.17) | collective-permute-done | bytes 81952 | tf_op jit(solution)/shard_map/ppermute | solution.py:415
  86.5 3.5 %collective-permute-start.29 = (f32[8,256]{1,0:T(8,128)S(1)}, f32[8,256]{1,0:T(8,128)S(1)}, u32[]{:S(2)}, u32[]{:S(2)}) collective-permute-start(f32[8,256]{1,0:T(8,128)S(1)} %add.67), channel_id=1, source_target_pairs={{0,8},{4,12},{8,0},{12,4},{16,24},{20,28},{24,16},{28,20},{32,40},... | collective-permute-start | bytes 24584 | tf_op jit(solution)/shard_map/ppermute | solution.py:419
  91.7 2.5 %collective-permute-start.33 = (f32[8,256]{1,0:T(8,128)S(1)}, f32[8,256]{1,0:T(8,128)S(1)}, u32[]{:S(2)}, u32[]{:S(2)}) collective-permute-start(f32[8,256]{1,0:T(8,128)S(1)} %add_add_fusion.3), channel_id=1, source_target_pairs={{0,128},{4,132},{8,136},{12,140},{16,144},{20,148},{24,152},{28,15... | collective-permute-start | bytes 24584 | tf_op jit(solution)/shard_map/ppermute | solution.py:419
  94.2 5.2 %collective-permute-start.34 = (f32[8,256]{1,0:T(8,128)S(1)}, f32[8,256]{1,0:T(8,128)S(1)}, u32[]{:S(2)}, u32[]{:S(2)}) collective-permute-start(f32[8,256]{1,0:T(8,128)S(1)} %add_add_fusion.3), channel_id=1, source_target_pairs={{0,192},{4,196},{8,200},{12,204},{16,208},{20,212},{24,216},{28,22... | collective-permute-start | bytes 24584 | tf_op jit(solution)/shard_map/ppermute | solution.py:419
  103.5 1.9 %collective-permute-start.27 = (bf16[20,8,256]{2,1,0:T(8,128)(2,1)S(1)}, bf16[20,8,256]{2,1,0:T(8,128)(2,1)S(1)}, u32[]{:S(2)}, u32[]{:S(2)}) collective-permute-start(bf16[20,8,256]{2,1,0:T(8,128)(2,1)S(1)} %get-tuple-element.74), channel_id=1, source_target_pairs={{0,3},{1,2},{2,1},{3,0},{4,7},{5,6},{6,5},{7,4},{8,11},{9,10},{10,... | collective-permute-start | bytes 245768 | tf_op jit(solution)/shard_map/ppermute | solution.py:415
  106.3 2.0 %collective-permute-done.26.refs_8_ = bf16[20,8,256]{2,1,0:T(8,128)(2,1)S(1)} collective-permute-done((bf16[20,8,256]{2,1,0:T(8,128)(2,1)S(1)}, bf16[20,8,256]{2,1,0:T(8,128)(2,1)S(1)}, u32[]{:S(2)}, u32[]{:S(2)}) %collective-permute-start.26) | collective-permute-done | bytes 81952 | tf_op jit(solution)/shard_map/ppermute | solution.py:415
  (84 shorter events, 32.3 us)
Async XLA Ops:
  4.6 9.8 %collective-permute-start.4 = (bf16[20,8,256]{2,1,0:T(8,128)(2,1)S(1)}, bf16[20,8,256]{2,1,0:T(8,128)(2,1)S(1)}, u32[]{:S(2)}, u32[]{:S(2)}) collective-permute-start(bf16[20,8,256]{2,1,0:T(8,128)(2,1)S(1)} %get-tuple-element.46), channel_id=1, source_target_pairs={{0,2},{1,3},{2,0},{3,1},{4,6},{5,7},{6,4},{7,5},{8,10},{9,11},{10,... | collective-permute-start | bytes 245768 | tf_op jit(solution)/shard_map/ppermute | solution.py:415
  7.9 6.5 %collective-permute-start.5 = (bf16[20,8,256]{2,1,0:T(8,128)(2,1)S(1)}, bf16[20,8,256]{2,1,0:T(8,128)(2,1)S(1)}, u32[]{:S(2)}, u32[]{:S(2)}) collective-permute-start(bf16[20,8,256]{2,1,0:T(8,128)(2,1)S(1)} %get-tuple-element.47), channel_id=1, source_target_pairs={{0,3},{1,2},{2,1},{3,0},{4,7},{5,6},{6,5},{7,4},{8,11},{9,10},{10,... | collective-permute-start | bytes 245768 | tf_op jit(solution)/shard_map/ppermute | solution.py:415
  14.9 23.8 %collective-permute-start.6 = (bf16[20,4,8,256]{3,2,1,0:T(8,128)(2,1)S(1)}, bf16[20,4,8,256]{3,2,1,0:T(8,128)(2,1)S(1)}, u32[]{:S(2)}, u32[]{:S(2)}) collective-permute-start(bf16[20,4,8,256]{3,2,1,0:T(8,128)(2,1)S(1)} %shard_map.105.refs_5_.refs_2_.refs_1_), channel_id=1, source_target_pairs={{0,4},{4,0},{8,12},{12,8},{16,20},{20,16},{24,28},{28,24},{32,36},... | collective-permute-start | bytes 983048 | tf_op jit(solution)/shard_map/ppermute | solution.py:409
  15.0 26.5 %collective-permute-start.9 = (bf16[20,4,8,256]{3,2,1,0:T(8,128)(2,1)S(1)}, bf16[20,4,8,256]{3,2,1,0:T(8,128)(2,1)S(1)}, u32[]{:S(2)}, u32[]{:S(2)}) collective-permute-start(bf16[20,4,8,256]{3,2,1,0:T(8,128)(2,1)S(1)} %shard_map.105.refs_5_.refs_2_.refs_1_), channel_id=1, source_target_pairs={{0,254},{1,255},{2,252},{3,253},{4,8},{5,9},{6,10},{7,11},{8,4},{9... | collective-permute-start | bytes 983048 | tf_op jit(solution)/shard_map/ppermute | solution.py:412
  23.5 7.0 %collective-permute-start = (bf16[23,8,256]{2,1,0:T(8,128)(2,1)S(1)}, bf16[23,8,256]{2,1,0:T(8,128)(2,1)S(1)}, u32[]{:S(2)}, u32[]{:S(2)}) collective-permute-start(bf16[23,8,256]{2,1,0:T(8,128)(2,1)S(1)} %get-tuple-element.41), channel_id=1, source_target_pairs={{0,1},{1,0},{2,3},{3,2},{4,5},{5,4},{6,7},{7,6},{8,9},{9,8},{10,11... | collective-permute-start | bytes 282632 | tf_op jit(solution)/shard_map/ppermute | solution.py:415
  24.2 6.7 %collective-permute-start.1 = (bf16[23,8,256]{2,1,0:T(8,128)(2,1)S(1)}, bf16[23,8,256]{2,1,0:T(8,128)(2,1)S(1)}, u32[]{:S(2)}, u32[]{:S(2)}) collective-permute-start(bf16[23,8,256]{2,1,0:T(8,128)(2,1)S(1)} %get-tuple-element.42), channel_id=1, source_target_pairs={{0,2},{1,3},{2,0},{3,1},{4,6},{5,7},{6,4},{7,5},{8,10},{9,11},{10,... | collective-permute-start | bytes 282632 | tf_op jit(solution)/shard_map/ppermute | solution.py:415
  27.5 11.2 %collective-permute-start.7 = (bf16[352,256]{1,0:T(8,128)(2,1)S(1)}, bf16[352,256]{1,0:T(8,128)(2,1)S(1)}, u32[]{:S(2)}, u32[]{:S(2)}) collective-permute-start(bf16[352,256]{1,0:T(8,128)(2,1)S(1)} %get-tuple-element.53), channel_id=1, source_target_pairs={{0,4},{4,0},{8,12},{12,8},{16,20},{20,16},{24,28},{28,24},{32,36},... | collective-permute-start | bytes 540680 | tf_op jit(solution)/shard_map/ppermute | solution.py:409
  30.5 11.0 %collective-permute-start.10 = (bf16[352,256]{1,0:T(8,128)(2,1)S(1)}, bf16[352,256]{1,0:T(8,128)(2,1)S(1)}, u32[]{:S(2)}, u32[]{:S(2)}) collective-permute-start(bf16[352,256]{1,0:T(8,128)(2,1)S(1)} %get-tuple-element.58), channel_id=1, source_target_pairs={{0,254},{1,255},{2,252},{3,253},{4,8},{5,9},{6,10},{7,11},{8,4},{9... | collective-permute-start | bytes 540680 | tf_op jit(solution)/shard_map/ppermute | solution.py:412
  30.9 7.8 %collective-permute-start.2 = (bf16[23,8,256]{2,1,0:T(8,128)(2,1)S(1)}, bf16[23,8,256]{2,1,0:T(8,128)(2,1)S(1)}, u32[]{:S(2)}, u32[]{:S(2)}) collective-permute-start(bf16[23,8,256]{2,1,0:T(8,128)(2,1)S(1)} %get-tuple-element.43), channel_id=1, source_target_pairs={{0,3},{1,2},{2,1},{3,0},{4,7},{5,6},{6,5},{7,4},{8,11},{9,10},{10,... | collective-permute-start | bytes 282632 | tf_op jit(solution)/shard_map/ppermute | solution.py:415
  42.1 8.5 %collective-permute-start.11 = (f32[32,256]{1,0:T(8,128)S(1)}, f32[32,256]{1,0:T(8,128)S(1)}, u32[]{:S(2)}, u32[]{:S(2)}) collective-permute-start(f32[32,256]{1,0:T(8,128)S(1)} %pad_maximum_fusion.1), channel_id=1, source_target_pairs={{0,254},{1,255},{2,252},{3,253},{4,8},{5,9},{6,10},{7,11},{8,4},{9... | collective-permute-start | bytes 98312 | tf_op jit(solution)/shard_map/ppermute | solution.py:412
  50.8 6.0 %collective-permute-start.14 = (f32[32,256]{1,0:T(8,128)S(1)}, f32[32,256]{1,0:T(8,128)S(1)}, u32[]{:S(2)}, u32[]{:S(2)}) collective-permute-start(f32[32,256]{1,0:T(8,128)S(1)} %maximum_add_fusion), channel_id=1, source_target_pairs={{0,3},{1,2},{2,1},{3,0},{4,7},{5,6},{6,5},{7,4},{8,11},{9,10},{10,... | collective-permute-start | bytes 98312 | tf_op jit(solution)/shard_map/ppermute | solution.py:419
  62.1 8.6 %collective-permute-start.20 = (f32[32,256]{1,0:T(8,128)S(1)}, f32[32,256]{1,0:T(8,128)S(1)}, u32[]{:S(2)}, u32[]{:S(2)}) collective-permute-start(f32[32,256]{1,0:T(8,128)S(1)} %pad_maximum_fusion.2), channel_id=1, source_target_pairs={{0,254},{1,255},{2,252},{3,253},{4,8},{5,9},{6,10},{7,11},{8,4},{9... | collective-permute-start | bytes 98312 | tf_op jit(solution)/shard_map/ppermute | solution.py:412
  70.7 6.7 %collective-permute-start.22 = (f32[40,256]{1,0:T(8,128)S(1)}, f32[40,256]{1,0:T(8,128)S(1)}, u32[]{:S(2)}, u32[]{:S(2)}) collective-permute-start(f32[40,256]{1,0:T(8,128)S(1)} %pad_maximum_fusion), channel_id=1, source_target_pairs={{0,2},{1,3},{2,0},{3,1},{4,6},{5,7},{6,4},{7,5},{8,10},{9,11},{10,... | collective-permute-start | bytes 122888 | tf_op jit(solution)/shard_map/ppermute | solution.py:419
  72.7 6.6 %collective-permute-start.23 = (f32[40,256]{1,0:T(8,128)S(1)}, f32[40,256]{1,0:T(8,128)S(1)}, u32[]{:S(2)}, u32[]{:S(2)}) collective-permute-start(f32[40,256]{1,0:T(8,128)S(1)} %pad_maximum_fusion), channel_id=1, source_target_pairs={{0,3},{1,2},{2,1},{3,0},{4,7},{5,6},{6,5},{7,4},{8,11},{9,10},{10,... | collective-permute-start | bytes 122888 | tf_op jit(solution)/shard_map/ppermute | solution.py:419
  74.3 6.4 %collective-permute-start.16 = (bf16[20,8,256]{2,1,0:T(8,128)(2,1)S(1)}, bf16[20,8,256]{2,1,0:T(8,128)(2,1)S(1)}, u32[]{:S(2)}, u32[]{:S(2)}) collective-permute-start(bf16[20,8,256]{2,1,0:T(8,128)(2,1)S(1)} %get-tuple-element.64), channel_id=1, source_target_pairs={{0,1},{1,0},{2,3},{3,2},{4,5},{5,4},{6,7},{7,6},{8,9},{9,8},{10,11... | collective-permute-start | bytes 245768 | tf_op jit(solution)/shard_map/ppermute | solution.py:415
  76.4 6.2 %collective-permute-start.17 = (bf16[20,8,256]{2,1,0:T(8,128)(2,1)S(1)}, bf16[20,8,256]{2,1,0:T(8,128)(2,1)S(1)}, u32[]{:S(2)}, u32[]{:S(2)}) collective-permute-start(bf16[20,8,256]{2,1,0:T(8,128)(2,1)S(1)} %get-tuple-element.65), channel_id=1, source_target_pairs={{0,2},{1,3},{2,0},{3,1},{4,6},{5,7},{6,4},{7,5},{8,10},{9,11},{10,... | collective-permute-start | bytes 245768 | tf_op jit(solution)/shard_map/ppermute | solution.py:415
  77.4 6.4 %collective-permute-start.18 = (bf16[20,8,256]{2,1,0:T(8,128)(2,1)S(1)}, bf16[20,8,256]{2,1,0:T(8,128)(2,1)S(1)}, u32[]{:S(2)}, u32[]{:S(2)}) collective-permute-start(bf16[20,8,256]{2,1,0:T(8,128)(2,1)S(1)} %get-tuple-element.66), channel_id=1, source_target_pairs={{0,3},{1,2},{2,1},{3,0},{4,7},{5,6},{6,5},{7,4},{8,11},{9,10},{10,... | collective-permute-start | bytes 245768 | tf_op jit(solution)/shard_map/ppermute | solution.py:415
  80.6 5.8 %collective-permute-start.28 = (f32[8,256]{1,0:T(8,128)S(1)}, f32[8,256]{1,0:T(8,128)S(1)}, u32[]{:S(2)}, u32[]{:S(2)}) collective-permute-start(f32[8,256]{1,0:T(8,128)S(1)} %shard_map.116), channel_id=1, source_target_pairs={{0,34},{1,35},{2,32},{3,33},{4,38},{5,39},{6,36},{7,37},{8,42},{9,... | collective-permute-start | bytes 24584 | tf_op jit(solution)/shard_map/ppermute | solution.py:560
  91.7 11.8 %collective-permute-start.33 = (f32[8,256]{1,0:T(8,128)S(1)}, f32[8,256]{1,0:T(8,128)S(1)}, u32[]{:S(2)}, u32[]{:S(2)}) collective-permute-start(f32[8,256]{1,0:T(8,128)S(1)} %add_add_fusion.3), channel_id=1, source_target_pairs={{0,128},{4,132},{8,136},{12,140},{16,144},{20,148},{24,152},{28,15... | collective-permute-start | bytes 24584 | tf_op jit(solution)/shard_map/ppermute | solution.py:419
  94.2 11.2 %collective-permute-start.34 = (f32[8,256]{1,0:T(8,128)S(1)}, f32[8,256]{1,0:T(8,128)S(1)}, u32[]{:S(2)}, u32[]{:S(2)}) collective-permute-start(f32[8,256]{1,0:T(8,128)S(1)} %add_add_fusion.3), channel_id=1, source_target_pairs={{0,192},{4,196},{8,200},{12,204},{16,208},{20,212},{24,216},{28,22... | collective-permute-start | bytes 24584 | tf_op jit(solution)/shard_map/ppermute | solution.py:419
  99.4 5.9 %collective-permute-start.32 = (f32[8,256]{1,0:T(8,128)S(1)}, f32[8,256]{1,0:T(8,128)S(1)}, u32[]{:S(2)}, u32[]{:S(2)}) collective-permute-start(f32[8,256]{1,0:T(8,128)S(1)} %add_add_fusion.3), channel_id=1, source_target_pairs={{0,64},{4,68},{8,72},{12,76},{16,80},{20,84},{24,88},{28,92},{32,9... | collective-permute-start | bytes 24584 | tf_op jit(solution)/shard_map/ppermute | solution.py:419
  100.9 5.4 %collective-permute-start.25 = (bf16[20,8,256]{2,1,0:T(8,128)(2,1)S(1)}, bf16[20,8,256]{2,1,0:T(8,128)(2,1)S(1)}, u32[]{:S(2)}, u32[]{:S(2)}) collective-permute-start(bf16[20,8,256]{2,1,0:T(8,128)(2,1)S(1)} %get-tuple-element.72), channel_id=1, source_target_pairs={{0,1},{1,0},{2,3},{3,2},{4,5},{5,4},{6,7},{7,6},{8,9},{9,8},{10,11... | collective-permute-start | bytes 245768 | tf_op jit(solution)/shard_map/ppermute | solution.py:415
  102.1 6.2 %collective-permute-start.26 = (bf16[20,8,256]{2,1,0:T(8,128)(2,1)S(1)}, bf16[20,8,256]{2,1,0:T(8,128)(2,1)S(1)}, u32[]{:S(2)}, u32[]{:S(2)}) collective-permute-start(bf16[20,8,256]{2,1,0:T(8,128)(2,1)S(1)} %get-tuple-element.73), channel_id=1, source_target_pairs={{0,2},{1,3},{2,0},{3,1},{4,6},{5,7},{6,4},{7,5},{8,10},{9,11},{10,... | collective-permute-start | bytes 245768 | tf_op jit(solution)/shard_map/ppermute | solution.py:415
  103.5 6.3 %collective-permute-start.27 = (bf16[20,8,256]{2,1,0:T(8,128)(2,1)S(1)}, bf16[20,8,256]{2,1,0:T(8,128)(2,1)S(1)}, u32[]{:S(2)}, u32[]{:S(2)}) collective-permute-start(bf16[20,8,256]{2,1,0:T(8,128)(2,1)S(1)} %get-tuple-element.74), channel_id=1, source_target_pairs={{0,3},{1,2},{2,1},{3,0},{4,7},{5,6},{6,5},{7,4},{8,11},{9,10},{10,... | collective-permute-start | bytes 245768 | tf_op jit(solution)/shard_map/ppermute | solution.py:415
  (13 other events, 71.0 us)

commit v8 on v7

--- a/solution.py
+++ b/solution.py
@@ -147,6 +147,18 @@
     return jnp.dot(mat, jnp.concatenate([xh, xl, xh], axis=0), preferred_element_type=F32)
 
 
+def channel_dot(w, x):
+    hi = x.astype(BF16)
+    lo = (x - hi.astype(F32)).astype(BF16)
+    return jnp.dot(w, jnp.concatenate([hi, lo, hi], axis=0), preferred_element_type=F32)
+
+
+def side_by_side(w, width):
+    hi = w.astype(BF16).astype(F32)
+    lo = w - hi
+    return (hi + pltpu.roll(hi, width, 1) + pltpu.roll(lo, 2 * width, 1)).astype(BF16)
+
+
 def smooth_rows(src, exact, mat, avb):
     for r in range(0, avb.shape[0], GRP):
         avb[r : r + GRP, :] = band_apply(mat, src(r), exact).astype(BF16)
@@ -166,18 +178,13 @@
 
         dx = lax.fori_loop(0, ms, member, jnp.zeros((lev, 256), F32), unroll=4)
         dxs[:, 256 * i : 256 * i + 256] = dx * norm
-    return jnp.dot(
-        w[:, 0:lev], dxs[...], precision=lax.Precision.HIGHEST, preferred_element_type=F32
-    )
+    return channel_dot(w[:, 0 : 3 * lev], dxs[...])
 
 
 def adjoint_rows(q, wt, ens3, dmats, ua, norm):
     lev = 32
     ms = ua.shape[0] // lev
-    dxa = (
-        jnp.dot(wt[:, 0:16], q, precision=lax.Precision.HIGHEST, preferred_element_type=F32)
-        * norm
-    )
+    dxa = channel_dot(wt[:, 0:48], q) * norm
     total = None
     for i, (ens, d) in enumerate(zip(ens3, dmats)):
         mine = dxa[:, 256 * i : 256 * i + 256]
@@ -222,8 +229,8 @@
         wsq[pl.ds(pl.multiple_of(8 * group, 8), 8), :] = join3(
             c[share], c[share + 1], c[share + 2]
         )[:, 0:128]
-    w[...] = wsq[...].T[0:16, :]
-    wt[...] = wsq[0:32, :]
+    w[...] = side_by_side(wsq[...].T[0:16, :], 32)
+    wt[...] = side_by_side(wsq[0:32, :], 16)
 
     def rows_of(r):
         some = GRP // 32
@@ -490,7 +497,7 @@
 
     cm, avb, hx_core, hx_own, w, wt = call(
         bind(first_kernel, norm),
-        [field, flat, row, row, sds((obs, 128), F32), sds((lev, 128), F32)],
+        [field, flat, row, row, sds((obs, 128), BF16), sds((lev, 128), BF16)],
         (scal, *cparts, e_own, e_core, d_own, x_core, bands),
         1,
         [full, pltpu.VMEM((128, 128), F32), umat, pltpu.VMEM((lev, 2 * pdev), F32)],
@@ -557,8 +564,8 @@
         3 * mm,
     )
     bparts = shuffle(bparts)
+    sums = sum4(sums, "tile", tile_xor, (2, 4, 6))
     sums = sums + lax.ppermute(sums, both, far)
-    sums = sum4(sums, "tile", tile_xor, (2, 4, 6))
     sums = sum4(sums, "tile", tile_xor, (16, 32, 48))
     whole = sds((members, ldev, pdev), F32)
     (grad_first,) = call(grad_first_kernel, [whole], (scal, control, *aparts), 1)

time: 114 us -> 113 us (level)
    ppermute x1, waiting for transfers between devices: 1.23 us -> 4.8 us  [per_device(): sums = sums + lax.ppermute(sums, both, far)]
    ppermute x12, waiting for transfers between devices: 22.8 us -> 19.7 us  [shuffle(): lax.ppermute(parts[k], 'lev', lev_xor(k))]
  transfers between devices with their start and end apart: 35 -> 35, of which waited for: 19 -> 17; matrix products, arithmetic and copies ran while one was open for 0% -> 0% of each run, Pallas kernels for 9% -> 9%
where the time goes in v8:
time: 113 us; the launch traced here: 111 us
  starting transfers between devices  51.3 us (45%)
  waiting for transfers between devices  42.9 us (38%)
  Pallas kernels  16 us (14%)
    ppermute x12, waiting for transfers between devices, shuffle(): lax.ppermute(parts[k], 'lev', lev_xor(k))  19.7 us
    ppermute x12, starting transfers between devices, shuffle(): lax.ppermute(parts[k], 'lev', lev_xor(k))  18.9 us
    ppermute x12, starting transfers between devices, sum4(): one, two, three = (lax.ppermute(x, axis, pairs(k)) for k in steps)  18.3 us
    pallas_call x15, Pallas kernels, call(): pl.pallas_call(body, out_shape=tuple(outs), in_specs=specs, out_specs=out...  16 us
    ppermute x4, waiting for transfers between devices, swap_edge(): return lax.ppermute(x, both, edge)  13.5 us
    ppermute x4, starting transfers between devices, swap_edge(): return lax.ppermute(x, both, edge)  13 us
    ppermute x1, waiting for transfers between devices, per_device(): sums = sums + lax.ppermute(sums, both, far)  4.8 us
    ppermute x12, waiting for transfers between devices, sum4(): one, two, three = (lax.ppermute(x, axis, pairs(k)) for k in steps)  3.31 us
  transfers between devices with their start and end apart: 35, of which 17 were waited for; matrix products, arithmetic and copies ran while one was open for 0% of the time, Pallas kernels for 9%

profile of v8, /device:TPU:2, one launch (start us, length us, event | category | flops | bytes accessed | tf_op | source)
XLA Modules:
  0.0 111.4 jit_solution(12457650737298883331)
XLA Ops:
  0.7 1.9 %shard_map.104 = (bf16[20,8,256]{2,1,0:T(8,128)(2,1)S(1)}, bf16[20,8,256]{2,1,0:T(8,128)(2,1)S(1)}, bf16[20,8,256]{2,1,0:T(8,128)(2,1)S(1)}, bf16[20,8,256]{2,1,...) custom-call(s32[4]{0:T(128)S(1)} %pad_add_fusion.scal.refs_0_, ...), custom_call_target="tpu_custom_call" | custom-call | bytes 1903008 | tf_op jit(solution)/shard_map/pallas_call | solution.py:28
  2.6 2.0 %collective-permute-start.3 = (bf16[20,8,256]{2,1,0:T(8,128)(2,1)S(1)}, bf16[20,8,256]{2,1,0:T(8,128)(2,1)S(1)}, u32[]{:S(2)}, u32[]{:S(2)}) collective-permute-start(bf16[20,8,256]{2,1,0:T(8,128)(2,1)S(1)} %get-tuple-element.45), channel_id=1, source_target_pairs={{0,1},{1,0},{2,3},{3,2},{4,5},{5,4},{6,7},{7,6},{8,9},{9,8},{10,11... | collective-permute-start | bytes 245768 | tf_op jit(solution)/shard_map/ppermute | solution.py:422
  4.6 3.3 %collective-permute-start.4 = (bf16[20,8,256]{2,1,0:T(8,128)(2,1)S(1)}, bf16[20,8,256]{2,1,0:T(8,128)(2,1)S(1)}, u32[]{:S(2)}, u32[]{:S(2)}) collective-permute-start(bf16[20,8,256]{2,1,0:T(8,128)(2,1)S(1)} %get-tuple-element.46), channel_id=1, source_target_pairs={{0,2},{1,3},{2,0},{3,1},{4,6},{5,7},{6,4},{7,5},{8,10},{9,11},{10,... | collective-permute-start | bytes 245768 | tf_op jit(solution)/shard_map/ppermute | solution.py:422
  7.9 6.5 %collective-permute-done.4.e2 = bf16[20,8,256]{2,1,0:T(8,128)(2,1)S(1)} collective-permute-done((bf16[20,8,256]{2,1,0:T(8,128)(2,1)S(1)}, bf16[20,8,256]{2,1,0:T(8,128)(2,1)S(1)}, u32[]{:S(2)}, u32[]{:S(2)}) %collective-permute-start.4) | collective-permute-done | bytes 81952 | tf_op jit(solution)/shard_map/ppermute | solution.py:422
  15.0 7.8 %collective-permute-start.9 = (bf16[20,4,8,256]{3,2,1,0:T(8,128)(2,1)S(1)}, bf16[20,4,8,256]{3,2,1,0:T(8,128)(2,1)S(1)}, u32[]{:S(2)}, u32[]{:S(2)}) collective-permute-start(bf16[20,4,8,256]{3,2,1,0:T(8,128)(2,1)S(1)} %shard_map.105.refs_5_.refs_2_.refs_1_), channel_id=1, source_target_pairs={{0,254},{1,255},{2,252},{3,253},{4,8},{5,9},{6,10},{7,11},{8,4},{9... | collective-permute-start | bytes 983048 | tf_op jit(solution)/shard_map/ppermute | solution.py:419
  24.2 1.9 %collective-permute-start.1 = (bf16[23,8,256]{2,1,0:T(8,128)(2,1)S(1)}, bf16[23,8,256]{2,1,0:T(8,128)(2,1)S(1)}, u32[]{:S(2)}, u32[]{:S(2)}) collective-permute-start(bf16[23,8,256]{2,1,0:T(8,128)(2,1)S(1)} %get-tuple-element.42), channel_id=1, source_target_pairs={{0,2},{1,3},{2,0},{3,1},{4,6},{5,7},{6,4},{7,5},{8,10},{9,11},{10,... | collective-permute-start | bytes 282632 | tf_op jit(solution)/shard_map/ppermute | solution.py:422
  27.6 2.9 %collective-permute-done.refs_2_ = bf16[23,8,256]{2,1,0:T(8,128)(2,1)S(1)} collective-permute-done((bf16[23,8,256]{2,1,0:T(8,128)(2,1)S(1)}, bf16[23,8,256]{2,1,0:T(8,128)(2,1)S(1)}, u32[]{:S(2)}, u32[]{:S(2)}) %collective-permute-start) | collective-permute-done | bytes 94240 | tf_op jit(solution)/shard_map/ppermute | solution.py:422
  30.9 1.9 %collective-permute-start.2 = (bf16[23,8,256]{2,1,0:T(8,128)(2,1)S(1)}, bf16[23,8,256]{2,1,0:T(8,128)(2,1)S(1)}, u32[]{:S(2)}, u32[]{:S(2)}) collective-permute-start(bf16[23,8,256]{2,1,0:T(8,128)(2,1)S(1)} %get-tuple-element.43), channel_id=1, source_target_pairs={{0,3},{1,2},{2,1},{3,0},{4,7},{5,6},{6,5},{7,4},{8,11},{9,10},{10,... | collective-permute-start | bytes 282632 | tf_op jit(solution)/shard_map/ppermute | solution.py:422
  32.8 5.9 %collective-permute-done.2.refs_4_ = bf16[23,8,256]{2,1,0:T(8,128)(2,1)S(1)} collective-permute-done((bf16[23,8,256]{2,1,0:T(8,128)(2,1)S(1)}, bf16[23,8,256]{2,1,0:T(8,128)(2,1)S(1)}, u32[]{:S(2)}, u32[]{:S(2)}) %collective-permute-start.2) | collective-permute-done | bytes 94240 | tf_op jit(solution)/shard_map/ppermute | solution.py:422
  42.1 2.7 %collective-permute-start.11 = (f32[32,256]{1,0:T(8,128)S(1)}, f32[32,256]{1,0:T(8,128)S(1)}, u32[]{:S(2)}, u32[]{:S(2)}) collective-permute-start(f32[32,256]{1,0:T(8,128)S(1)} %pad_maximum_fusion.1), channel_id=1, source_target_pairs={{0,254},{1,255},{2,252},{3,253},{4,8},{5,9},{6,10},{7,11},{8,4},{9... | collective-permute-start | bytes 98312 | tf_op jit(solution)/shard_map/ppermute | solution.py:419
  44.8 5.8 %collective-permute-done.11 = f32[32,256]{1,0:T(8,128)S(1)} collective-permute-done((f32[32,256]{1,0:T(8,128)S(1)}, f32[32,256]{1,0:T(8,128)S(1)}, u32[]{:S(2)}, u32[]{:S(2)}) %collective-permute-start.11) | collective-permute-done | bytes 32800 | tf_op jit(solution)/shard_map/ppermute | solution.py:419
  50.7 2.0 %collective-permute-start.14 = (f32[32,256]{1,0:T(8,128)S(1)}, f32[32,256]{1,0:T(8,128)S(1)}, u32[]{:S(2)}, u32[]{:S(2)}) collective-permute-start(f32[32,256]{1,0:T(8,128)S(1)} %maximum_add_fusion), channel_id=1, source_target_pairs={{0,3},{1,2},{2,1},{3,0},{4,7},{5,6},{6,5},{7,4},{8,11},{9,10},{10,... | collective-permute-start | bytes 98312 | tf_op jit(solution)/shard_map/ppermute | solution.py:426
  58.3 2.3 %shard_map.110 = (bf16[20,8,256]{2,1,0:T(8,128)(2,1)S(1)}, bf16[20,8,256]{2,1,0:T(8,128)(2,1)S(1)}, bf16[20,8,256]{2,1,0:T(8,128)(2,1)S(1)}, bf16[20,8,256]{2,1,...) custom-call(s32[4]{0:T(128)S(1)} %pad_add_fusion.scal.refs_0_, ...), custom_call_target="tpu_custom_call" | custom-call | flops 419430400 | bytes 2404368 | tf_op jit(solution)/shard_map/pallas_call | solution.py:28
  62.0 2.0 %collective-permute-start.20 = (f32[32,256]{1,0:T(8,128)S(1)}, f32[32,256]{1,0:T(8,128)S(1)}, u32[]{:S(2)}, u32[]{:S(2)}) collective-permute-start(f32[32,256]{1,0:T(8,128)S(1)} %pad_maximum_fusion.2), channel_id=1, source_target_pairs={{0,254},{1,255},{2,252},{3,253},{4,8},{5,9},{6,10},{7,11},{8,4},{9... | collective-permute-start | bytes 98312 | tf_op jit(solution)/shard_map/ppermute | solution.py:419
  64.0 6.5 %collective-permute-done.20 = f32[32,256]{1,0:T(8,128)S(1)} collective-permute-done((f32[32,256]{1,0:T(8,128)S(1)}, f32[32,256]{1,0:T(8,128)S(1)}, u32[]{:S(2)}, u32[]{:S(2)}) %collective-permute-start.20) | collective-permute-done | bytes 32800 | tf_op jit(solution)/shard_map/ppermute | solution.py:419
  70.6 2.0 %collective-permute-start.22 = (f32[40,256]{1,0:T(8,128)S(1)}, f32[40,256]{1,0:T(8,128)S(1)}, u32[]{:S(2)}, u32[]{:S(2)}) collective-permute-start(f32[40,256]{1,0:T(8,128)S(1)} %pad_maximum_fusion), channel_id=1, source_target_pairs={{0,2},{1,3},{2,0},{3,1},{4,6},{5,7},{6,4},{7,5},{8,10},{9,11},{10,... | collective-permute-start | bytes 122888 | tf_op jit(solution)/shard_map/ppermute | solution.py:426
  74.1 2.0 %collective-permute-start.16 = (bf16[20,8,256]{2,1,0:T(8,128)(2,1)S(1)}, bf16[20,8,256]{2,1,0:T(8,128)(2,1)S(1)}, u32[]{:S(2)}, u32[]{:S(2)}) collective-permute-start(bf16[20,8,256]{2,1,0:T(8,128)(2,1)S(1)} %get-tuple-element.64), channel_id=1, source_target_pairs={{0,1},{1,0},{2,3},{3,2},{4,5},{5,4},{6,7},{7,6},{8,9},{9,8},{10,11... | collective-permute-start | bytes 245768 | tf_op jit(solution)/shard_map/ppermute | solution.py:422
  77.3 1.9 %collective-permute-start.18 = (bf16[20,8,256]{2,1,0:T(8,128)(2,1)S(1)}, bf16[20,8,256]{2,1,0:T(8,128)(2,1)S(1)}, u32[]{:S(2)}, u32[]{:S(2)}) collective-permute-start(bf16[20,8,256]{2,1,0:T(8,128)(2,1)S(1)} %get-tuple-element.66), channel_id=1, source_target_pairs={{0,3},{1,2},{2,1},{3,0},{4,7},{5,6},{6,5},{7,4},{8,11},{9,10},{10,... | collective-permute-start | bytes 245768 | tf_op jit(solution)/shard_map/ppermute | solution.py:422
  80.7 3.4 %collective-permute-start.28 = (f32[8,256]{1,0:T(8,128)S(1)}, f32[8,256]{1,0:T(8,128)S(1)}, u32[]{:S(2)}, u32[]{:S(2)}) collective-permute-start(f32[8,256]{1,0:T(8,128)S(1)} %shard_map.116), channel_id=1, source_target_pairs={{0,8},{4,12},{8,0},{12,4},{16,24},{20,28},{24,16},{28,20},{32,40},... | collective-permute-start | bytes 24584 | tf_op jit(solution)/shard_map/ppermute | solution.py:426
  86.8 4.8 %collective-permute-done.31 = f32[8,256]{1,0:T(8,128)S(1)} collective-permute-done((f32[8,256]{1,0:T(8,128)S(1)}, f32[8,256]{1,0:T(8,128)S(1)}, u32[]{:S(2)}, u32[]{:S(2)}) %collective-permute-start.31) | collective-permute-done | bytes 8224 | tf_op jit(solution)/shard_map/ppermute | solution.py:568
  91.6 2.4 %collective-permute-start.33 = (f32[8,256]{1,0:T(8,128)S(1)}, f32[8,256]{1,0:T(8,128)S(1)}, u32[]{:S(2)}, u32[]{:S(2)}) collective-permute-start(f32[8,256]{1,0:T(8,128)S(1)} %add.70), channel_id=1, source_target_pairs={{0,128},{4,132},{8,136},{12,140},{16,144},{20,148},{24,152},{28,15... | collective-permute-start | bytes 24584 | tf_op jit(solution)/shard_map/ppermute | solution.py:426
  94.0 5.2 %collective-permute-start.34 = (f32[8,256]{1,0:T(8,128)S(1)}, f32[8,256]{1,0:T(8,128)S(1)}, u32[]{:S(2)}, u32[]{:S(2)}) collective-permute-start(f32[8,256]{1,0:T(8,128)S(1)} %add.70), channel_id=1, source_target_pairs={{0,192},{4,196},{8,200},{12,204},{16,208},{20,212},{24,216},{28,22... | collective-permute-start | bytes 24584 | tf_op jit(solution)/shard_map/ppermute | solution.py:426
  103.3 1.9 %collective-permute-start.27 = (bf16[20,8,256]{2,1,0:T(8,128)(2,1)S(1)}, bf16[20,8,256]{2,1,0:T(8,128)(2,1)S(1)}, u32[]{:S(2)}, u32[]{:S(2)}) collective-permute-start(bf16[20,8,256]{2,1,0:T(8,128)(2,1)S(1)} %get-tuple-element.74), channel_id=1, source_target_pairs={{0,3},{1,2},{2,1},{3,0},{4,7},{5,6},{6,5},{7,4},{8,11},{9,10},{10,... | collective-permute-start | bytes 245768 | tf_op jit(solution)/shard_map/ppermute | solution.py:422
  106.1 2.0 %collective-permute-done.26.refs_8_ = bf16[20,8,256]{2,1,0:T(8,128)(2,1)S(1)} collective-permute-done((bf16[20,8,256]{2,1,0:T(8,128)(2,1)S(1)}, bf16[20,8,256]{2,1,0:T(8,128)(2,1)S(1)}, u32[]{:S(2)}, u32[]{:S(2)}) %collective-permute-start.26) | collective-permute-done | bytes 81952 | tf_op jit(solution)/shard_map/ppermute | solution.py:422
  (84 shorter events, 29.4 us)
Async XLA Ops:
  4.6 9.8 %collective-permute-start.4 = (bf16[20,8,256]{2,1,0:T(8,128)(2,1)S(1)}, bf16[20,8,256]{2,1,0:T(8,128)(2,1)S(1)}, u32[]{:S(2)}, u32[]{:S(2)}) collective-permute-start(bf16[20,8,256]{2,1,0:T(8,128)(2,1)S(1)} %get-tuple-element.46), channel_id=1, source_target_pairs={{0,2},{1,3},{2,0},{3,1},{4,6},{5,7},{6,4},{7,5},{8,10},{9,11},{10,... | collective-permute-start | bytes 245768 | tf_op jit(solution)/shard_map/ppermute | solution.py:422
  7.9 6.5 %collective-permute-start.5 = (bf16[20,8,256]{2,1,0:T(8,128)(2,1)S(1)}, bf16[20,8,256]{2,1,0:T(8,128)(2,1)S(1)}, u32[]{:S(2)}, u32[]{:S(2)}) collective-permute-start(bf16[20,8,256]{2,1,0:T(8,128)(2,1)S(1)} %get-tuple-element.47), channel_id=1, source_target_pairs={{0,3},{1,2},{2,1},{3,0},{4,7},{5,6},{6,5},{7,4},{8,11},{9,10},{10,... | collective-permute-start | bytes 245768 | tf_op jit(solution)/shard_map/ppermute | solution.py:422
  14.9 23.7 %collective-permute-start.6 = (bf16[20,4,8,256]{3,2,1,0:T(8,128)(2,1)S(1)}, bf16[20,4,8,256]{3,2,1,0:T(8,128)(2,1)S(1)}, u32[]{:S(2)}, u32[]{:S(2)}) collective-permute-start(bf16[20,4,8,256]{3,2,1,0:T(8,128)(2,1)S(1)} %shard_map.105.refs_5_.refs_2_.refs_1_), channel_id=1, source_target_pairs={{0,4},{4,0},{8,12},{12,8},{16,20},{20,16},{24,28},{28,24},{32,36},... | collective-permute-start | bytes 983048 | tf_op jit(solution)/shard_map/ppermute | solution.py:416
  15.0 26.5 %collective-permute-start.9 = (bf16[20,4,8,256]{3,2,1,0:T(8,128)(2,1)S(1)}, bf16[20,4,8,256]{3,2,1,0:T(8,128)(2,1)S(1)}, u32[]{:S(2)}, u32[]{:S(2)}) collective-permute-start(bf16[20,4,8,256]{3,2,1,0:T(8,128)(2,1)S(1)} %shard_map.105.refs_5_.refs_2_.refs_1_), channel_id=1, source_target_pairs={{0,254},{1,255},{2,252},{3,253},{4,8},{5,9},{6,10},{7,11},{8,4},{9... | collective-permute-start | bytes 983048 | tf_op jit(solution)/shard_map/ppermute | solution.py:419
  23.6 7.0 %collective-permute-start = (bf16[23,8,256]{2,1,0:T(8,128)(2,1)S(1)}, bf16[23,8,256]{2,1,0:T(8,128)(2,1)S(1)}, u32[]{:S(2)}, u32[]{:S(2)}) collective-permute-start(bf16[23,8,256]{2,1,0:T(8,128)(2,1)S(1)} %get-tuple-element.41), channel_id=1, source_target_pairs={{0,1},{1,0},{2,3},{3,2},{4,5},{5,4},{6,7},{7,6},{8,9},{9,8},{10,11... | collective-permute-start | bytes 282632 | tf_op jit(solution)/shard_map/ppermute | solution.py:422
  24.2 6.7 %collective-permute-start.1 = (bf16[23,8,256]{2,1,0:T(8,128)(2,1)S(1)}, bf16[23,8,256]{2,1,0:T(8,128)(2,1)S(1)}, u32[]{:S(2)}, u32[]{:S(2)}) collective-permute-start(bf16[23,8,256]{2,1,0:T(8,128)(2,1)S(1)} %get-tuple-element.42), channel_id=1, source_target_pairs={{0,2},{1,3},{2,0},{3,1},{4,6},{5,7},{6,4},{7,5},{8,10},{9,11},{10,... | collective-permute-start | bytes 282632 | tf_op jit(solution)/shard_map/ppermute | solution.py:422
  27.5 11.2 %collective-permute-start.7 = (bf16[352,256]{1,0:T(8,128)(2,1)S(1)}, bf16[352,256]{1,0:T(8,128)(2,1)S(1)}, u32[]{:S(2)}, u32[]{:S(2)}) collective-permute-start(bf16[352,256]{1,0:T(8,128)(2,1)S(1)} %get-tuple-element.53), channel_id=1, source_target_pairs={{0,4},{4,0},{8,12},{12,8},{16,20},{20,16},{24,28},{28,24},{32,36},... | collective-permute-start | bytes 540680 | tf_op jit(solution)/shard_map/ppermute | solution.py:416
  30.5 11.0 %collective-permute-start.10 = (bf16[352,256]{1,0:T(8,128)(2,1)S(1)}, bf16[352,256]{1,0:T(8,128)(2,1)S(1)}, u32[]{:S(2)}, u32[]{:S(2)}) collective-permute-start(bf16[352,256]{1,0:T(8,128)(2,1)S(1)} %get-tuple-element.58), channel_id=1, source_target_pairs={{0,254},{1,255},{2,252},{3,253},{4,8},{5,9},{6,10},{7,11},{8,4},{9... | collective-permute-start | bytes 540680 | tf_op jit(solution)/shard_map/ppermute | solution.py:419
  30.9 7.8 %collective-permute-start.2 = (bf16[23,8,256]{2,1,0:T(8,128)(2,1)S(1)}, bf16[23,8,256]{2,1,0:T(8,128)(2,1)S(1)}, u32[]{:S(2)}, u32[]{:S(2)}) collective-permute-start(bf16[23,8,256]{2,1,0:T(8,128)(2,1)S(1)} %get-tuple-element.43), channel_id=1, source_target_pairs={{0,3},{1,2},{2,1},{3,0},{4,7},{5,6},{6,5},{7,4},{8,11},{9,10},{10,... | collective-permute-start | bytes 282632 | tf_op jit(solution)/shard_map/ppermute | solution.py:422
  42.1 8.5 %collective-permute-start.11 = (f32[32,256]{1,0:T(8,128)S(1)}, f32[32,256]{1,0:T(8,128)S(1)}, u32[]{:S(2)}, u32[]{:S(2)}) collective-permute-start(f32[32,256]{1,0:T(8,128)S(1)} %pad_maximum_fusion.1), channel_id=1, source_target_pairs={{0,254},{1,255},{2,252},{3,253},{4,8},{5,9},{6,10},{7,11},{8,4},{9... | collective-permute-start | bytes 98312 | tf_op jit(solution)/shard_map/ppermute | solution.py:419
  50.7 6.0 %collective-permute-start.14 = (f32[32,256]{1,0:T(8,128)S(1)}, f32[32,256]{1,0:T(8,128)S(1)}, u32[]{:S(2)}, u32[]{:S(2)}) collective-permute-start(f32[32,256]{1,0:T(8,128)S(1)} %maximum_add_fusion), channel_id=1, source_target_pairs={{0,3},{1,2},{2,1},{3,0},{4,7},{5,6},{6,5},{7,4},{8,11},{9,10},{10,... | collective-permute-start | bytes 98312 | tf_op jit(solution)/shard_map/ppermute | solution.py:426
  62.0 8.6 %collective-permute-start.20 = (f32[32,256]{1,0:T(8,128)S(1)}, f32[32,256]{1,0:T(8,128)S(1)}, u32[]{:S(2)}, u32[]{:S(2)}) collective-permute-start(f32[32,256]{1,0:T(8,128)S(1)} %pad_maximum_fusion.2), channel_id=1, source_target_pairs={{0,254},{1,255},{2,252},{3,253},{4,8},{5,9},{6,10},{7,11},{8,4},{9... | collective-permute-start | bytes 98312 | tf_op jit(solution)/shard_map/ppermute | solution.py:419
  70.6 6.7 %collective-permute-start.22 = (f32[40,256]{1,0:T(8,128)S(1)}, f32[40,256]{1,0:T(8,128)S(1)}, u32[]{:S(2)}, u32[]{:S(2)}) collective-permute-start(f32[40,256]{1,0:T(8,128)S(1)} %pad_maximum_fusion), channel_id=1, source_target_pairs={{0,2},{1,3},{2,0},{3,1},{4,6},{5,7},{6,4},{7,5},{8,10},{9,11},{10,... | collective-permute-start | bytes 122888 | tf_op jit(solution)/shard_map/ppermute | solution.py:426
  72.6 6.6 %collective-permute-start.23 = (f32[40,256]{1,0:T(8,128)S(1)}, f32[40,256]{1,0:T(8,128)S(1)}, u32[]{:S(2)}, u32[]{:S(2)}) collective-permute-start(f32[40,256]{1,0:T(8,128)S(1)} %pad_maximum_fusion), channel_id=1, source_target_pairs={{0,3},{1,2},{2,1},{3,0},{4,7},{5,6},{6,5},{7,4},{8,11},{9,10},{10,... | collective-permute-start | bytes 122888 | tf_op jit(solution)/shard_map/ppermute | solution.py:426
  74.1 6.6 %collective-permute-start.16 = (bf16[20,8,256]{2,1,0:T(8,128)(2,1)S(1)}, bf16[20,8,256]{2,1,0:T(8,128)(2,1)S(1)}, u32[]{:S(2)}, u32[]{:S(2)}) collective-permute-start(bf16[20,8,256]{2,1,0:T(8,128)(2,1)S(1)} %get-tuple-element.64), channel_id=1, source_target_pairs={{0,1},{1,0},{2,3},{3,2},{4,5},{5,4},{6,7},{7,6},{8,9},{9,8},{10,11... | collective-permute-start | bytes 245768 | tf_op jit(solution)/shard_map/ppermute | solution.py:422
  76.2 7.9 %collective-permute-start.17 = (bf16[20,8,256]{2,1,0:T(8,128)(2,1)S(1)}, bf16[20,8,256]{2,1,0:T(8,128)(2,1)S(1)}, u32[]{:S(2)}, u32[]{:S(2)}) collective-permute-start(bf16[20,8,256]{2,1,0:T(8,128)(2,1)S(1)} %get-tuple-element.65), channel_id=1, source_target_pairs={{0,2},{1,3},{2,0},{3,1},{4,6},{5,7},{6,4},{7,5},{8,10},{9,11},{10,... | collective-permute-start | bytes 245768 | tf_op jit(solution)/shard_map/ppermute | solution.py:422
  77.3 6.8 %collective-permute-start.18 = (bf16[20,8,256]{2,1,0:T(8,128)(2,1)S(1)}, bf16[20,8,256]{2,1,0:T(8,128)(2,1)S(1)}, u32[]{:S(2)}, u32[]{:S(2)}) collective-permute-start(bf16[20,8,256]{2,1,0:T(8,128)(2,1)S(1)} %get-tuple-element.66), channel_id=1, source_target_pairs={{0,3},{1,2},{2,1},{3,0},{4,7},{5,6},{6,5},{7,4},{8,11},{9,10},{10,... | collective-permute-start | bytes 245768 | tf_op jit(solution)/shard_map/ppermute | solution.py:422
  85.8 5.8 %collective-permute-start.31 = (f32[8,256]{1,0:T(8,128)S(1)}, f32[8,256]{1,0:T(8,128)S(1)}, u32[]{:S(2)}, u32[]{:S(2)}) collective-permute-start(f32[8,256]{1,0:T(8,128)S(1)} %add_add_fusion.3), channel_id=1, source_target_pairs={{0,34},{1,35},{2,32},{3,33},{4,38},{5,39},{6,36},{7,37},{8,42},{9,... | collective-permute-start | bytes 24584 | tf_op jit(solution)/shard_map/ppermute | solution.py:568
  91.6 11.6 %collective-permute-start.33 = (f32[8,256]{1,0:T(8,128)S(1)}, f32[8,256]{1,0:T(8,128)S(1)}, u32[]{:S(2)}, u32[]{:S(2)}) collective-permute-start(f32[8,256]{1,0:T(8,128)S(1)} %add.70), channel_id=1, source_target_pairs={{0,128},{4,132},{8,136},{12,140},{16,144},{20,148},{24,152},{28,15... | collective-permute-start | bytes 24584 | tf_op jit(solution)/shard_map/ppermute | solution.py:426
  94.0 11.1 %collective-permute-start.34 = (f32[8,256]{1,0:T(8,128)S(1)}, f32[8,256]{1,0:T(8,128)S(1)}, u32[]{:S(2)}, u32[]{:S(2)}) collective-permute-start(f32[8,256]{1,0:T(8,128)S(1)} %add.70), channel_id=1, source_target_pairs={{0,192},{4,196},{8,200},{12,204},{16,208},{20,212},{24,216},{28,22... | collective-permute-start | bytes 24584 | tf_op jit(solution)/shard_map/ppermute | solution.py:426
  99.3 5.9 %collective-permute-start.32 = (f32[8,256]{1,0:T(8,128)S(1)}, f32[8,256]{1,0:T(8,128)S(1)}, u32[]{:S(2)}, u32[]{:S(2)}) collective-permute-start(f32[8,256]{1,0:T(8,128)S(1)} %add.70), channel_id=1, source_target_pairs={{0,64},{4,68},{8,72},{12,76},{16,80},{20,84},{24,88},{28,92},{32,9... | collective-permute-start | bytes 24584 | tf_op jit(solution)/shard_map/ppermute | solution.py:426
  100.7 5.4 %collective-permute-start.25 = (bf16[20,8,256]{2,1,0:T(8,128)(2,1)S(1)}, bf16[20,8,256]{2,1,0:T(8,128)(2,1)S(1)}, u32[]{:S(2)}, u32[]{:S(2)}) collective-permute-start(bf16[20,8,256]{2,1,0:T(8,128)(2,1)S(1)} %get-tuple-element.72), channel_id=1, source_target_pairs={{0,1},{1,0},{2,3},{3,2},{4,5},{5,4},{6,7},{7,6},{8,9},{9,8},{10,11... | collective-permute-start | bytes 245768 | tf_op jit(solution)/shard_map/ppermute | solution.py:422
  101.9 6.2 %collective-permute-start.26 = (bf16[20,8,256]{2,1,0:T(8,128)(2,1)S(1)}, bf16[20,8,256]{2,1,0:T(8,128)(2,1)S(1)}, u32[]{:S(2)}, u32[]{:S(2)}) collective-permute-start(bf16[20,8,256]{2,1,0:T(8,128)(2,1)S(1)} %get-tuple-element.73), channel_id=1, source_target_pairs={{0,2},{1,3},{2,0},{3,1},{4,6},{5,7},{6,4},{7,5},{8,10},{9,11},{10,... | collective-permute-start | bytes 245768 | tf_op jit(solution)/shard_map/ppermute | solution.py:422
  103.3 6.3 %collective-permute-start.27 = (bf16[20,8,256]{2,1,0:T(8,128)(2,1)S(1)}, bf16[20,8,256]{2,1,0:T(8,128)(2,1)S(1)}, u32[]{:S(2)}, u32[]{:S(2)}) collective-permute-start(bf16[20,8,256]{2,1,0:T(8,128)(2,1)S(1)} %get-tuple-element.74), channel_id=1, source_target_pairs={{0,3},{1,2},{2,1},{3,0},{4,7},{5,6},{6,5},{7,4},{8,11},{9,10},{10,... | collective-permute-start | bytes 245768 | tf_op jit(solution)/shard_map/ppermute | solution.py:422
  (13 other events, 71.0 us)
